TPU v7x, 256 devices: a whole 4x4x8 slice. The times are simulated.
256 devices in a mesh: ctx: 256 (over y, x, z, core).
Axes of the slice: x: 4, y: 4, z: 8, core: 2. Of those that a mesh axis runs over, the one named last changes fastest.
Arguments:
- query_rows: bfloat16 [32768, 1024], P('ctx'), may hold values from -12 to 12
- key_rows: bfloat16 [32768, 1024], P('ctx'), may hold values from -6 to 6
- value_rows: bfloat16 [32768, 1024], P('ctx'), may hold values from -6 to 6
- out_grad: bfloat16 [32768, 1024], P('ctx'), may hold values from -192 to 192
- inputs: bfloat16 [32768, 2048], P('ctx'), may hold values from -24 to 24
Outputs:
- query_grad: bfloat16 [32768, 1024], P('ctx')
- key_grad: bfloat16 [32768, 1024], P('ctx')
- value_grad: bfloat16 [32768, 1024], P('ctx')
- weight_grad: float32 [2048, 1024], P('ctx')
All inputs are finite; a program needn't handle non-finite values.
Results may differ from a plain program's by a relative error of at most 0.015.
Values may be sent and summed in bfloat16 or wider, within the bound.
No kernel may reach another device: no remote copies, remote signals or barrier semaphores. Data moves between devices by JAX's collectives and lax.ppermute only.
A program may use at most 128 MiB of HBM per device.

v0:
```python
import math

import jax
import jax.numpy as jnp
from jax import lax
from jax.experimental import pallas as pl
from jax.experimental.pallas import tpu as pltpu
from jax.sharding import Mesh, PartitionSpec as P


HEAD = 128
NEG = -1e30
ROOM = pltpu.CompilerParams(vmem_limit_bytes=20 << 20)


AXES = ("y", "x", "z", "c")
LAST = (((1,), (1,)), ((), ()))
FIRST = (((0,), (0,)), ((), ()))


def physical_mesh(mesh):
    count = mesh.devices.size
    sizes = (4, 4, 8, 2) if count == 256 else (2, count // 8, 2, 2)
    return Mesh(mesh.devices.reshape(sizes), AXES)


def to_core(array, count):
    return lax.ppermute(array, AXES, [(device, device ^ 1) for device in range(count)])


def swap(array, count, odd):
    chips = count // 2
    pairs = []
    for device in range(count):
        chip, core = device // 2, device % 2
        other = ((chip - odd) ^ 1) + odd
        pairs.append((device, other % chips * 2 + core))
    return lax.ppermute(array, AXES, pairs)


def along_x(array, sizes, step):
    ny, nx, nz, nc = sizes
    pairs = []
    for y in range(ny):
        for x in range(nx):
            for rest in range(nz * nc):
                pairs.append(
                    ((y * nx + x) * nz * nc + rest, (y * nx + (x + step) % nx) * nz * nc + rest)
                )
    return lax.ppermute(array, AXES, pairs)


def vmem(count):
    return [pl.BlockSpec(memory_space=pltpu.VMEM)] * count


def smem():
    return pl.BlockSpec(memory_space=pltpu.SMEM)


def pack_kernel(core, query, key, value, grad, mine, other, done):
    half = query.shape[1] // 2
    here = pl.multiple_of(core[0] * half, half)
    there = pl.multiple_of((1 - core[0]) * half, half)
    copies = []
    for at, source in enumerate((key, query, grad, value)):
        for side, (target, start) in enumerate(((other, there), (mine, here))):
            copies.append(
                pltpu.make_async_copy(
                    source.at[:, pl.ds(start, half)], target.at[at], done.at[2 * at + side]
                )
            )
    for copy in copies:
        copy.start()
    for copy in copies:
        copy.wait()


def pack(core, query, key, value, grad):
    rows, features = query.shape
    four = jax.ShapeDtypeStruct((4, rows, features // 2), query.dtype)
    return pl.pallas_call(
        pack_kernel,
        out_shape=(four, four),
        in_specs=[smem()] + [pl.BlockSpec(memory_space=pltpu.HBM)] * 4,
        out_specs=tuple(vmem(2)),
        scratch_shapes=[pltpu.SemaphoreType.DMA((8,))],
        compiler_params=ROOM,
        name="pack",
    )(core, query, key, value, grad)


def join_kernel(mine, part, key, query, grad, value):
    rows = mine.shape[1]
    for at, target in enumerate((key, query, grad, value)):
        target[:rows] = mine[at]
        target[rows:] = part[at]


def join(mine, part):
    _, rows, half = mine.shape
    two = jax.ShapeDtypeStruct((2 * rows, half), mine.dtype)
    return pl.pallas_call(
        join_kernel,
        out_shape=(two,) * 4,
        in_specs=vmem(2),
        out_specs=tuple(vmem(4)),
        compiler_params=ROOM,
        name="join",
    )(mine, part)


def window_bias(place, tokens):
    even_core, even_chip = place[0] == 0, place[1] == 0
    left = lax.broadcasted_iota(jnp.int32, (1, 2 * tokens), 1) < tokens
    right = jnp.logical_not(left)

    def bias(core_even, chip_even, columns):
        hit = jnp.logical_and(even_core == core_even, even_chip == chip_even)
        return jnp.where(jnp.logical_and(hit, columns), NEG, 0.0)

    return {
        0: bias(True, False, right) + bias(False, True, right),
        1: bias(True, True, left) + bias(False, False, left),
        4: bias(True, True, right) + bias(False, False, right),
        5: bias(True, False, left) + bias(False, True, left),
    }


def scores_of(bias, keys, queries, scale):
    flat = lax.dot_general(keys, queries, LAST, preferred_element_type=jnp.float32) * scale
    size = flat.shape[0] // 6
    parts = []
    for block in range(6):
        part = flat[block * size : (block + 1) * size]
        parts.append(part + bias[block] if block in bias else part)
    return jnp.concatenate(parts, 0)


def value_kernel(scale, place, query, grad, first_k, key, second_k, first, own, second, lse):
    two, width = query.shape
    bias = window_bias(place, two // 2)
    for head in range(width // HEAD):
        at = slice(head * HEAD, (head + 1) * HEAD)
        keys = jnp.concatenate([first_k[:, at], key[:, at], second_k[:, at]], 0)
        scores = scores_of(bias, keys, query[:, at], scale)
        top = jnp.max(scores, axis=0, keepdims=True)
        raised = jnp.exp(scores - top)
        total = jnp.sum(raised, axis=0, keepdims=True)
        probs = (raised * (1.0 / total)).astype(jnp.bfloat16)
        terms = jnp.dot(probs, grad[:, at], preferred_element_type=jnp.float32)
        first[:, at] = terms[:two].astype(jnp.bfloat16)
        own[:, at] = terms[two : 2 * two]
        second[:, at] = terms[2 * two :].astype(jnp.bfloat16)
        lse[head] = jnp.broadcast_to(top + jnp.log(total), lse.shape[1:])


def score_kernel(
    scale, place, query, grad, first_k, key, second_k, first_v, value, second_v, lse,
    query_grad, query_back, first, own, second,
):
    two, width = query.shape
    bias = window_bias(place, two // 2)
    for head in range(width // HEAD):
        at = slice(head * HEAD, (head + 1) * HEAD)
        keys = jnp.concatenate([first_k[:, at], key[:, at], second_k[:, at]], 0)
        values = jnp.concatenate([first_v[:, at], value[:, at], second_v[:, at]], 0)
        scores = scores_of(bias, keys, query[:, at], scale)
        probs = jnp.exp(scores - lse[head, 0:1])
        grad_probs = lax.dot_general(values, grad[:, at], LAST, preferred_element_type=jnp.float32)
        rounded = probs.astype(jnp.bfloat16).astype(jnp.float32)
        delta = jnp.sum(rounded * grad_probs, axis=0, keepdims=True)
        low = (probs * (grad_probs - delta)).astype(jnp.bfloat16)
        turned = lax.dot_general(keys, low, FIRST, preferred_element_type=jnp.float32) * scale
        found = turned.T.astype(jnp.bfloat16)
        query_grad[:, at] = found[: two // 2]
        query_back[:, at] = found[two // 2 :]
        terms = jnp.dot(low, query[:, at], preferred_element_type=jnp.float32) * scale
        first[:, at] = terms[:two].astype(jnp.bfloat16)
        own[:, at] = terms[two : 2 * two]
        second[:, at] = terms[2 * two :].astype(jnp.bfloat16)


def value_pass(core, query, grad, keys, scale):
    two, width = query.shape
    heads = width // HEAD
    low = jax.ShapeDtypeStruct((two, width), jnp.bfloat16)
    high = jax.ShapeDtypeStruct((two, width), jnp.float32)
    work = heads * two * 3 * two
    return pl.pallas_call(
        lambda *refs: value_kernel(scale, *refs),
        out_shape=(low, high, low, jax.ShapeDtypeStruct((heads, 8, two), jnp.float32)),
        in_specs=[smem()] + vmem(5),
        out_specs=tuple(vmem(4)),
        cost_estimate=pl.CostEstimate(
            flops=4 * work * HEAD, transcendentals=work, bytes_accessed=4 << 20
        ),
        compiler_params=ROOM,
        name="value_pass",
    )(core, query, grad, *keys)


def score_pass(core, query, grad, keys, values, lse, scale):
    two, width = query.shape
    heads = width // HEAD
    low = jax.ShapeDtypeStruct((two, width), jnp.bfloat16)
    high = jax.ShapeDtypeStruct((two, width), jnp.float32)
    part = jax.ShapeDtypeStruct((two // 2, width), jnp.bfloat16)
    work = heads * two * 3 * two
    return pl.pallas_call(
        lambda *refs: score_kernel(scale, *refs),
        out_shape=(part, part, low, high, low),
        in_specs=[smem()] + vmem(9),
        out_specs=tuple(vmem(5)),
        cost_estimate=pl.CostEstimate(
            flops=8 * work * HEAD, transcendentals=work, bytes_accessed=6 << 20
        ),
        compiler_params=ROOM,
        name="score_pass",
    )(core, query, grad, *keys, *values, lse)


def block_kernel(count, groups, place, own, part, *blocks):
    rows, width = own.shape
    size = width // (groups * count)
    for step, block in enumerate(blocks):
        target = lax.rem(place[2] + step, count)
        for group in range(groups):
            start = pl.multiple_of((group * count + target) * size, size)
            at = slice(group * size, (group + 1) * size)
            block[:rows, at] = own[:, pl.ds(start, size)]
            block[rows:, at] = part[:, pl.ds(start, size)]


def input_blocks(place, own, part, count, groups):
    rows, width = own.shape
    block = jax.ShapeDtypeStruct((2 * rows, width // count), own.dtype)
    return pl.pallas_call(
        lambda *refs: block_kernel(count, groups, *refs),
        out_shape=(block,) * count,
        in_specs=[smem()] + vmem(2),
        out_specs=tuple(vmem(count)),
        compiler_params=ROOM,
        name="input_blocks",
    )(place, own, part)


def weight_kernel(count, *refs):
    inputs, gathered, out = refs[:count], refs[count : 2 * count], refs[2 * count]
    tile = 256
    for low in range(0, out.shape[0], tile):
        total = jnp.zeros((tile, out.shape[1]), jnp.float32)
        for step in range(count):
            total += lax.dot_general(
                inputs[step][:, low : low + tile],
                gathered[step][...],
                FIRST,
                preferred_element_type=jnp.float32,
            )
        out[low : low + tile] = total.astype(jnp.bfloat16)


def weight_pass(inputs, gathered):
    count = len(inputs)
    rows, width = inputs[0].shape
    columns = gathered[0].shape[1]
    return pl.pallas_call(
        lambda *refs: weight_kernel(count, *refs),
        out_shape=jax.ShapeDtypeStruct((width, columns), jnp.bfloat16),
        in_specs=vmem(2 * count),
        out_specs=pl.BlockSpec(memory_space=pltpu.VMEM),
        cost_estimate=pl.CostEstimate(
            flops=2 * count * rows * width * columns, transcendentals=0, bytes_accessed=4 << 20
        ),
        compiler_params=ROOM,
        name="weight_pass",
    )(*inputs, *gathered)


def steps(query_rows, key_rows, value_rows, out_grad, inputs):
    rows, features = query_rows.shape
    sizes = tuple(lax.axis_size(name) for name in AXES)
    ny, nx, nz, nc = sizes
    devices = ny * nx * nz * nc
    scale = 1.0 / math.sqrt(HEAD)
    core = lax.axis_index("c").astype(jnp.int32)
    parity = lax.rem(lax.axis_index("z").astype(jnp.int32), 2)
    place = jnp.stack([core, parity, lax.axis_index("x").astype(jnp.int32)])
    even = core == 0
    place, even, query_rows = lax.optimization_barrier((place, even, query_rows))

    def both_halves(mine, other):
        return jnp.where(
            even, jnp.concatenate([mine, other], 1), jnp.concatenate([other, mine], 1)
        )

    def swaps(one, two):
        got_one = swap(one, devices, 0)
        got_two = swap(two, devices, 1)
        return got_one, got_two

    mine, other = pack(place, query_rows, key_rows, value_rows, out_grad)
    part = to_core(other, devices)
    key, query, grad, value = join(mine, part)
    first_k, second_k = swaps(key, key)
    first_v, second_v = swaps(value, value)
    keys, values = (first_k, key, second_k), (first_v, value, second_v)

    inputs, _ = lax.optimization_barrier((inputs, mine))
    inputs_part = to_core(inputs, devices)
    blocks = input_blocks(place, inputs, inputs_part, nx, ny)
    taken = [blocks[0]]
    for step in range(1, nx):
        taken.append(along_x(blocks[step], sizes, step))

    first, own, second, lse = value_pass(place, query, grad, keys, scale)
    from_first, from_second = swaps(first, second)
    dq, dq_other, key_first, key_own, key_second = score_pass(
        place, query, grad, keys, values, lse, scale
    )
    from_first, from_second, dq, key_first, key_second = lax.optimization_barrier(
        (from_first, from_second, dq, key_first, key_second)
    )
    value_half = (own + from_first.astype(jnp.float32) + from_second.astype(jnp.float32)).astype(
        jnp.bfloat16
    )
    gathered = [value_half]
    for step in range(1, nx):
        gathered.append(along_x(value_half, sizes, step))
    key_from_first, key_from_second = swaps(key_first, key_second)
    value_back = to_core(value_half[rows:], devices)
    query_back = to_core(dq_other, devices)

    partial = weight_pass(taken, gathered)
    half = features // 2
    own_count = inputs.shape[1] // devices
    pieces = partial.reshape(ny * nz * nc, own_count, half)
    arrived = lax.all_to_all(pieces, ("y", "z", "c"), 0, 0, tiled=True)
    summed = jnp.sum(
        arrived.reshape(ny * nz, nc, own_count, half).astype(jnp.float32), axis=0
    )
    weight_grad = summed.transpose(1, 0, 2).reshape(own_count, features) * (
        1.0 / math.sqrt(rows * devices)
    )

    key_half = (
        key_own + key_from_first.astype(jnp.float32) + key_from_second.astype(jnp.float32)
    ).astype(jnp.bfloat16)
    key_back = to_core(key_half[rows:], devices)
    query_grad = both_halves(dq, query_back)
    value_grad = both_halves(value_half[:rows], value_back)
    key_grad = both_halves(key_half[:rows], key_back)
    return (query_grad, key_grad, value_grad, weight_grad)


def solution(mesh):
    fine = physical_mesh(mesh)
    spec = P(AXES, None)
    return jax.shard_map(
        steps,
        mesh=fine,
        in_specs=(spec,) * 5,
        out_specs=(spec,) * 4,
        check_vma=False,
    )
```

profile of v0, /device:TPU:1, one launch (start us, length us, event | category | flops | bytes accessed | tf_op | source)
XLA Modules:
  0.0 93.4 jit_solution(2128492850660365180)
XLA Ops:
  0.6 0.1 pad_add_fusion.core.refs_0_
  0.7 0.0 copy-start.1
  0.7 0.9 %copy-done.1 = bf16[128,1024]{1,0:T(8,128)(2,1)S(1)} copy-done((bf16[128,1024]{1,0:T(8,128)(2,1)S(1)}, bf16[128,1024]{1,0:T(8,128)(2,1)}, u32[]{:S(2)}) %copy-start.1) | copy-done | bytes 262168
  1.7 0.0 copy-start.2
  1.7 0.9 %copy-done.2 = bf16[128,1024]{1,0:T(8,128)(2,1)S(1)} copy-done((bf16[128,1024]{1,0:T(8,128)(2,1)S(1)}, bf16[128,1024]{1,0:T(8,128)(2,1)}, u32[]{:S(2)}) %copy-start.2) | copy-done | bytes 262168
  2.6 0.0 copy-start.3
  2.6 0.9 %copy-done.3 = bf16[128,1024]{1,0:T(8,128)(2,1)S(1)} copy-done((bf16[128,1024]{1,0:T(8,128)(2,1)S(1)}, bf16[128,1024]{1,0:T(8,128)(2,1)}, u32[]{:S(2)}) %copy-start.3) | copy-done | bytes 262168
  3.6 0.0 copy-start.4
  3.6 0.9 %copy-done.4 = bf16[128,1024]{1,0:T(8,128)(2,1)S(1)} copy-done((bf16[128,1024]{1,0:T(8,128)(2,1)S(1)}, bf16[128,1024]{1,0:T(8,128)(2,1)}, u32[]{:S(2)}) %copy-start.4) | copy-done | bytes 262168
  4.5 0.0 copy-start
  4.5 0.8 pack.1
  5.3 3.3 %collective-permute-start = (bf16[4,128,512]{2,1,0:T(8,128)(2,1)S(1)}, bf16[4,128,512]{2,1,0:T(8,128)(2,1)S(1)}, u32[]{:S(2)}, u32[]{:S(2)}) collective-permute-start(bf16[4,128,512]{2,1,0:T(8,128)(2,1)S(1)} %get-tuple-element.36), channel_id=1, source_target_pairs={{0,1},{1,0},{2,3},{3,2},{4,5},{5,4},{6,7},{7,6},{8,9},{9,8},{10,11... | collective-permute-start | bytes 1572872 | tf_op jit(solution)/shard_map/ppermute | solution.py:28
  8.6 0.0 copy-done
  8.6 0.2 collective-permute-start.12
  8.8 1.4 %collective-permute-done.part = bf16[4,128,512]{2,1,0:T(8,128)(2,1)S(1)} collective-permute-done((bf16[4,128,512]{2,1,0:T(8,128)(2,1)S(1)}, bf16[4,128,512]{2,1,0:T(8,128)(2,1)S(1)}, u32[]{:S(2)}, u32[]{:S(2)}) %collective-permute-start) | collective-permute-done | bytes 524320 | tf_op jit(solution)/shard_map/ppermute | solution.py:28
  10.1 0.1 join.1
  10.2 0.1 collective-permute-start.1
  10.3 9.2 %collective-permute-start.2 = (bf16[256,512]{1,0:T(8,128)(2,1)S(1)}, bf16[256,512]{1,0:T(8,128)(2,1)S(1)}, u32[]{:S(2)}, u32[]{:S(2)}) collective-permute-start(bf16[256,512]{1,0:T(8,128)(2,1)S(1)} %get-tuple-element.39.refs_4_), channel_id=1, source_target_pairs={{0,254},{1,255},{2,4},{3,5},{4,2},{5,3},{6,8},{7,9},{8,6},{9,7},{1... | collective-permute-start | bytes 786440 | tf_op jit(solution)/shard_map/ppermute | solution.py:38
  19.5 0.0 collective-permute-start.5
  19.5 1.5 %collective-permute-start.6 = (bf16[256,512]{1,0:T(8,128)(2,1)S(1)}, bf16[256,512]{1,0:T(8,128)(2,1)S(1)}, u32[]{:S(2)}, u32[]{:S(2)}) collective-permute-start(bf16[256,512]{1,0:T(8,128)(2,1)S(1)} %get-tuple-element.42.refs_7_), channel_id=1, source_target_pairs={{0,254},{1,255},{2,4},{3,5},{4,2},{5,3},{6,8},{7,9},{8,6},{9,7},{1... | collective-permute-start | bytes 786440 | tf_op jit(solution)/shard_map/ppermute | solution.py:38
  21.0 0.0 collective-permute-done.1.refs_3_
  21.0 4.6 %collective-permute-done.2.refs_5_ = bf16[256,512]{1,0:T(8,128)(2,1)S(1)} collective-permute-done((bf16[256,512]{1,0:T(8,128)(2,1)S(1)}, bf16[256,512]{1,0:T(8,128)(2,1)S(1)}, u32[]{:S(2)}, u32[]{:S(2)}) %collective-permute-start.2) | collective-permute-done | bytes 262176 | tf_op jit(solution)/shard_map/ppermute | solution.py:38
  25.6 2.3 %value_pass.1 = (bf16[256,512]{1,0:T(8,128)(2,1)S(1)}, f32[256,512]{1,0:T(8,128)S(1)}, bf16[256,512]{1,0:T(8,128)(2,1)S(1)}, f32[4,8,256]{2,1,0:T(8,128)S(1)}) custom-call(s32[3]{0:T(128)S(1)} %pad_add_fusion.core.refs_0_, bf16[256,512]{1,0:T(8,128)(2,1)S(1)} %get-tuple-element.37.refs_1_, bf16[256,512]{1,0:T(8,128)(2,1)S(1)} %get-tuple-element.38.refs_2_, ...), custom_call_target="tpu_custom_call" | custom-call | flops 402653184 | bytes 4194304 | tf_op jit(solution)/shard_map/value_pass/pallas_call | solution.py:190
  27.9 0.1 collective-permute-start.3
  28.0 6.7 %collective-permute-start.4 = (bf16[256,512]{1,0:T(8,128)(2,1)S(1)}, bf16[256,512]{1,0:T(8,128)(2,1)S(1)}, u32[]{:S(2)}, u32[]{:S(2)}) collective-permute-start(bf16[256,512]{1,0:T(8,128)(2,1)S(1)} %get-tuple-element.41), channel_id=1, source_target_pairs={{0,254},{1,255},{2,4},{3,5},{4,2},{5,3},{6,8},{7,9},{8,6},{9,7},{1... | collective-permute-start | bytes 786440 | tf_op jit(solution)/shard_map/ppermute | solution.py:38
  34.7 0.0 collective-permute-done.12.refs_2_
  34.7 0.8 input_blocks.1
  35.5 0.1 collective-permute-start.13
  35.6 0.0 collective-permute-done.5.refs_6_
  35.6 0.1 collective-permute-start.14
  35.7 0.0 collective-permute-done.6.refs_8_
  35.7 2.6 %collective-permute-start.15 = (bf16[256,512]{1,0:T(8,128)(2,1)S(1)}, bf16[256,512]{1,0:T(8,128)(2,1)S(1)}, u32[]{:S(2)}, u32[]{:S(2)}) collective-permute-start(bf16[256,512]{1,0:T(8,128)(2,1)S(1)} %get-tuple-element.59), channel_id=1, source_target_pairs={{0,48},{1,49},{2,50},{3,51},{4,52},{5,53},{6,54},{7,55},{8,56},{9,... | collective-permute-start | bytes 786440 | tf_op jit(solution)/shard_map/ppermute | solution.py:50
  38.3 3.6 %score_pass.1 = (bf16[128,512]{1,0:T(8,128)(2,1)S(1)}, bf16[128,512]{1,0:T(8,128)(2,1)S(1)}, bf16[256,512]{1,0:T(8,128)(2,1)S(1)}, f32[256,512]{1,0:T(8,128)S(1)}, bf16[256,512]{1,0:T(8,128)(2,1)S(1)}) custom-call(s32[3]{0:T(128)S(1)} %pad_add_fusion.core.refs_0_, bf16[256,512]{1,0:T(8,128)(2,1)S(1)} %get-tuple-element.37.refs_1_, ...), custom_call_target="tpu_custom_call" | custom-call | flops 805306368 | bytes 6291456 | tf_op jit(solution)/shard_map/score_pass/pallas_call | solution.py:210
  41.9 0.0 collective-permute-done.3
  42.0 0.0 collective-permute-done.4
  42.0 0.1 add_convert_fusion.refs_4_
  42.1 0.8 collective-permute-start.16
  42.8 1.9 %collective-permute-start.17 = (bf16[256,512]{1,0:T(8,128)(2,1)S(1)}, bf16[256,512]{1,0:T(8,128)(2,1)S(1)}, u32[]{:S(2)}, u32[]{:S(2)}) collective-permute-start(bf16[256,512]{1,0:T(8,128)(2,1)S(1)} %add_convert_fusion.refs_4_), channel_id=1, source_target_pairs={{0,32},{1,33},{2,34},{3,35},{4,36},{5,37},{6,38},{7,39},{8,40},{9,... | collective-permute-start | bytes 786440 | tf_op jit(solution)/shard_map/ppermute | solution.py:50
  44.7 2.8 %collective-permute-done.13.refs_1_ = bf16[256,512]{1,0:T(8,128)(2,1)S(1)} collective-permute-done((bf16[256,512]{1,0:T(8,128)(2,1)S(1)}, bf16[256,512]{1,0:T(8,128)(2,1)S(1)}, u32[]{:S(2)}, u32[]{:S(2)}) %collective-permute-start.13) | collective-permute-done | bytes 262176 | tf_op jit(solution)/shard_map/ppermute | solution.py:50
  47.5 0.0 collective-permute-start.18
  47.5 0.0 collective-permute-done.14.refs_2_
  47.5 8.4 %collective-permute-start.7 = (bf16[128,512]{1,0:T(8,128)(2,1)S(1)}, bf16[128,512]{1,0:T(8,128)(2,1)S(1)}, u32[]{:S(2)}, u32[]{:S(2)}) collective-permute-start(bf16[128,512]{1,0:T(8,128)(2,1)S(1)} %get-tuple-element.48), channel_id=1, source_target_pairs={{0,1},{1,0},{2,3},{3,2},{4,5},{5,4},{6,7},{7,6},{8,9},{9,8},{10,11... | collective-permute-start | bytes 393224 | tf_op jit(solution)/shard_map/ppermute | solution.py:28
  55.9 0.0 collective-permute-done.15.refs_3_
  55.9 0.0 collective-permute-start.8
  55.9 3.5 %collective-permute-done.16.refs_5_ = bf16[256,512]{1,0:T(8,128)(2,1)S(1)} collective-permute-done((bf16[256,512]{1,0:T(8,128)(2,1)S(1)}, bf16[256,512]{1,0:T(8,128)(2,1)S(1)}, u32[]{:S(2)}, u32[]{:S(2)}) %collective-permute-start.16) | collective-permute-done | bytes 262176 | tf_op jit(solution)/shard_map/ppermute | solution.py:50
  59.4 0.0 collective-permute-start.9
  59.4 0.0 collective-permute-done.17.refs_6_
  59.4 0.0 collective-permute-done.18.refs_7_
  59.4 1.6 %weight_pass.1 = bf16[512,512]{1,0:T(8,128)(2,1)} custom-call(bf16[256,512]{1,0:T(8,128)(2,1)S(1)} %get-tuple-element.56.refs_0_, bf16[256,512]{1,0:T(8,128)(2,1)S(1)} %collective-permute-done.13.refs_1_, bf16[256,512]{1,0:T(8,128)(2,1)S(1)} %collective-permute-done.14.refs_2_, bf16[256,512]{1,0:T(8,128)(2,1)S(1)} %collective-permute-done.15.refs_3_, ...), custom_call_target="tpu_custom_call" | custom-call | flops 536870912 | bytes 4194304 | tf_op jit(solution)/shard_map/weight_pass/pallas_call | solution.py:267
  61.0 14.4 %all-to-all-start = ((bf16[64,8,512]{2,1,0:T(8,128)(2,1)}), bf16[64,8,512]{2,1,0:T(8,128)(2,1)S(1)}, u32[]{:S(2)}, u32[]{:S(2)}) async-start(bf16[64,8,512]{2,1,0:T(8,128)(2,1)} %bitcast.3), calls=%async_computation | async-start | bytes 1048576 | tf_op jit(solution)/shard_map/all_to_all | solution.py:338
  75.5 0.5 collective-permute-start.11
  76.0 0.0 collective-permute-done.8
  76.0 0.0 collective-permute-done.9
  76.0 0.1 add_convert_fusion.1
  76.1 0.1 collective-permute-start.10
  76.3 0.0 collective-permute-done.7
  76.3 0.8 maximum_select_fusion
  77.1 0.0 collective-permute-done.11
  77.1 0.8 maximum_select_fusion.2
  77.9 0.0 collective-permute-done.10
  77.9 0.8 maximum_select_fusion.1
  78.7 14.1 %all-to-all-done = bf16[64,8,512]{2,1,0:T(8,128)(2,1)S(1)} async-done(((bf16[64,8,512]{2,1,0:T(8,128)(2,1)}), bf16[64,8,512]{2,1,0:T(8,128)(2,1)S(1)}, u32[]{:S(2)}, u32[]{:S(2)}) %all-to-all-start) | async-done | bytes 524320 | tf_op jit(solution)/shard_map/all_to_all | solution.py:338
  92.7 0.1 convert_reduce_fusion
  92.8 0.6 broadcast_multiply_fusion
  (2 shorter events, 0.0 us)
Async XLA Ops:
  0.7 1.0 %copy-start.1 = (bf16[128,1024]{1,0:T(8,128)(2,1)S(1)}, bf16[128,1024]{1,0:T(8,128)(2,1)}, u32[]{:S(2)}) copy-start(bf16[128,1024]{1,0:T(8,128)(2,1)} %query) | copy-start | bytes 786436
  1.7 0.9 %copy-start.2 = (bf16[128,1024]{1,0:T(8,128)(2,1)S(1)}, bf16[128,1024]{1,0:T(8,128)(2,1)}, u32[]{:S(2)}) copy-start(bf16[128,1024]{1,0:T(8,128)(2,1)} %key.1) | copy-start | bytes 786436
  2.6 0.9 %copy-start.3 = (bf16[128,1024]{1,0:T(8,128)(2,1)S(1)}, bf16[128,1024]{1,0:T(8,128)(2,1)}, u32[]{:S(2)}) copy-start(bf16[128,1024]{1,0:T(8,128)(2,1)} %value.1) | copy-start | bytes 786436
  3.6 0.9 %copy-start.4 = (bf16[128,1024]{1,0:T(8,128)(2,1)S(1)}, bf16[128,1024]{1,0:T(8,128)(2,1)}, u32[]{:S(2)}) copy-start(bf16[128,1024]{1,0:T(8,128)(2,1)} %grad.1) | copy-start | bytes 786436
  4.5 4.1 %copy-start = (bf16[128,2048]{1,0:T(8,128)(2,1)S(1)}, bf16[128,2048]{1,0:T(8,128)(2,1)}, u32[]{:S(2)}) copy-start(bf16[128,2048]{1,0:T(8,128)(2,1)} %refs_1_) | copy-start | bytes 1572868
  5.3 4.8 %collective-permute-start = (bf16[4,128,512]{2,1,0:T(8,128)(2,1)S(1)}, bf16[4,128,512]{2,1,0:T(8,128)(2,1)S(1)}, u32[]{:S(2)}, u32[]{:S(2)}) collective-permute-start(bf16[4,128,512]{2,1,0:T(8,128)(2,1)S(1)} %get-tuple-element.36), channel_id=1, source_target_pairs={{0,1},{1,0},{2,3},{3,2},{4,5},{5,4},{6,7},{7,6},{8,9},{9,8},{10,11... | collective-permute-start | bytes 1572872 | tf_op jit(solution)/shard_map/ppermute | solution.py:28
  8.6 26.1 %collective-permute-start.12 = (bf16[128,2048]{1,0:T(8,128)(2,1)S(1)}, bf16[128,2048]{1,0:T(8,128)(2,1)S(1)}, u32[]{:S(2)}, u32[]{:S(2)}) collective-permute-start(bf16[128,2048]{1,0:T(8,128)(2,1)S(1)} %copy-done), channel_id=1, source_target_pairs={{0,1},{1,0},{2,3},{3,2},{4,5},{5,4},{6,7},{7,6},{8,9},{9,8},{10,11... | collective-permute-start | bytes 1572872 | tf_op jit(solution)/shard_map/ppermute | solution.py:28
  10.2 10.8 %collective-permute-start.1 = (bf16[256,512]{1,0:T(8,128)(2,1)S(1)}, bf16[256,512]{1,0:T(8,128)(2,1)S(1)}, u32[]{:S(2)}, u32[]{:S(2)}) collective-permute-start(bf16[256,512]{1,0:T(8,128)(2,1)S(1)} %get-tuple-element.39.refs_4_), channel_id=1, source_target_pairs={{0,2},{1,3},{2,0},{3,1},{4,6},{5,7},{6,4},{7,5},{8,10},{9,11},{10,... | collective-permute-start | bytes 786440 | tf_op jit(solution)/shard_map/ppermute | solution.py:38
  10.3 15.3 %collective-permute-start.2 = (bf16[256,512]{1,0:T(8,128)(2,1)S(1)}, bf16[256,512]{1,0:T(8,128)(2,1)S(1)}, u32[]{:S(2)}, u32[]{:S(2)}) collective-permute-start(bf16[256,512]{1,0:T(8,128)(2,1)S(1)} %get-tuple-element.39.refs_4_), channel_id=1, source_target_pairs={{0,254},{1,255},{2,4},{3,5},{4,2},{5,3},{6,8},{7,9},{8,6},{9,7},{1... | collective-permute-start | bytes 786440 | tf_op jit(solution)/shard_map/ppermute | solution.py:38
  19.5 16.0 %collective-permute-start.5 = (bf16[256,512]{1,0:T(8,128)(2,1)S(1)}, bf16[256,512]{1,0:T(8,128)(2,1)S(1)}, u32[]{:S(2)}, u32[]{:S(2)}) collective-permute-start(bf16[256,512]{1,0:T(8,128)(2,1)S(1)} %get-tuple-element.42.refs_7_), channel_id=1, source_target_pairs={{0,2},{1,3},{2,0},{3,1},{4,6},{5,7},{6,4},{7,5},{8,10},{9,11},{10,... | collective-permute-start | bytes 786440 | tf_op jit(solution)/shard_map/ppermute | solution.py:38
  19.5 16.1 %collective-permute-start.6 = (bf16[256,512]{1,0:T(8,128)(2,1)S(1)}, bf16[256,512]{1,0:T(8,128)(2,1)S(1)}, u32[]{:S(2)}, u32[]{:S(2)}) collective-permute-start(bf16[256,512]{1,0:T(8,128)(2,1)S(1)} %get-tuple-element.42.refs_7_), channel_id=1, source_target_pairs={{0,254},{1,255},{2,4},{3,5},{4,2},{5,3},{6,8},{7,9},{8,6},{9,7},{1... | collective-permute-start | bytes 786440 | tf_op jit(solution)/shard_map/ppermute | solution.py:38
  27.9 14.1 %collective-permute-start.3 = (bf16[256,512]{1,0:T(8,128)(2,1)S(1)}, bf16[256,512]{1,0:T(8,128)(2,1)S(1)}, u32[]{:S(2)}, u32[]{:S(2)}) collective-permute-start(bf16[256,512]{1,0:T(8,128)(2,1)S(1)} %get-tuple-element.40), channel_id=1, source_target_pairs={{0,2},{1,3},{2,0},{3,1},{4,6},{5,7},{6,4},{7,5},{8,10},{9,11},{10,... | collective-permute-start | bytes 786440 | tf_op jit(solution)/shard_map/ppermute | solution.py:38
  28.0 14.0 %collective-permute-start.4 = (bf16[256,512]{1,0:T(8,128)(2,1)S(1)}, bf16[256,512]{1,0:T(8,128)(2,1)S(1)}, u32[]{:S(2)}, u32[]{:S(2)}) collective-permute-start(bf16[256,512]{1,0:T(8,128)(2,1)S(1)} %get-tuple-element.41), channel_id=1, source_target_pairs={{0,254},{1,255},{2,4},{3,5},{4,2},{5,3},{6,8},{7,9},{8,6},{9,7},{1... | collective-permute-start | bytes 786440 | tf_op jit(solution)/shard_map/ppermute | solution.py:38
  35.5 12.0 %collective-permute-start.13 = (bf16[256,512]{1,0:T(8,128)(2,1)S(1)}, bf16[256,512]{1,0:T(8,128)(2,1)S(1)}, u32[]{:S(2)}, u32[]{:S(2)}) collective-permute-start(bf16[256,512]{1,0:T(8,128)(2,1)S(1)} %get-tuple-element.57), channel_id=1, source_target_pairs={{0,16},{1,17},{2,18},{3,19},{4,20},{5,21},{6,22},{7,23},{8,24},{9,... | collective-permute-start | bytes 786440 | tf_op jit(solution)/shard_map/ppermute | solution.py:50
  35.6 11.9 %collective-permute-start.14 = (bf16[256,512]{1,0:T(8,128)(2,1)S(1)}, bf16[256,512]{1,0:T(8,128)(2,1)S(1)}, u32[]{:S(2)}, u32[]{:S(2)}) collective-permute-start(bf16[256,512]{1,0:T(8,128)(2,1)S(1)} %get-tuple-element.58), channel_id=1, source_target_pairs={{0,32},{1,33},{2,34},{3,35},{4,36},{5,37},{6,38},{7,39},{8,40},{9,... | collective-permute-start | bytes 786440 | tf_op jit(solution)/shard_map/ppermute | solution.py:50
  35.7 20.2 %collective-permute-start.15 = (bf16[256,512]{1,0:T(8,128)(2,1)S(1)}, bf16[256,512]{1,0:T(8,128)(2,1)S(1)}, u32[]{:S(2)}, u32[]{:S(2)}) collective-permute-start(bf16[256,512]{1,0:T(8,128)(2,1)S(1)} %get-tuple-element.59), channel_id=1, source_target_pairs={{0,48},{1,49},{2,50},{3,51},{4,52},{5,53},{6,54},{7,55},{8,56},{9,... | collective-permute-start | bytes 786440 | tf_op jit(solution)/shard_map/ppermute | solution.py:50
  42.1 17.3 %collective-permute-start.16 = (bf16[256,512]{1,0:T(8,128)(2,1)S(1)}, bf16[256,512]{1,0:T(8,128)(2,1)S(1)}, u32[]{:S(2)}, u32[]{:S(2)}) collective-permute-start(bf16[256,512]{1,0:T(8,128)(2,1)S(1)} %add_convert_fusion.refs_4_), channel_id=1, source_target_pairs={{0,16},{1,17},{2,18},{3,19},{4,20},{5,21},{6,22},{7,23},{8,24},{9,... | collective-permute-start | bytes 786440 | tf_op jit(solution)/shard_map/ppermute | solution.py:50
  42.8 16.6 %collective-permute-start.17 = (bf16[256,512]{1,0:T(8,128)(2,1)S(1)}, bf16[256,512]{1,0:T(8,128)(2,1)S(1)}, u32[]{:S(2)}, u32[]{:S(2)}) collective-permute-start(bf16[256,512]{1,0:T(8,128)(2,1)S(1)} %add_convert_fusion.refs_4_), channel_id=1, source_target_pairs={{0,32},{1,33},{2,34},{3,35},{4,36},{5,37},{6,38},{7,39},{8,40},{9,... | collective-permute-start | bytes 786440 | tf_op jit(solution)/shard_map/ppermute | solution.py:50
  47.5 11.9 %collective-permute-start.18 = (bf16[256,512]{1,0:T(8,128)(2,1)S(1)}, bf16[256,512]{1,0:T(8,128)(2,1)S(1)}, u32[]{:S(2)}, u32[]{:S(2)}) collective-permute-start(bf16[256,512]{1,0:T(8,128)(2,1)S(1)} %add_convert_fusion.refs_4_), channel_id=1, source_target_pairs={{0,48},{1,49},{2,50},{3,51},{4,52},{5,53},{6,54},{7,55},{8,56},{9,... | collective-permute-start | bytes 786440 | tf_op jit(solution)/shard_map/ppermute | solution.py:50
  47.5 28.8 %collective-permute-start.7 = (bf16[128,512]{1,0:T(8,128)(2,1)S(1)}, bf16[128,512]{1,0:T(8,128)(2,1)S(1)}, u32[]{:S(2)}, u32[]{:S(2)}) collective-permute-start(bf16[128,512]{1,0:T(8,128)(2,1)S(1)} %get-tuple-element.48), channel_id=1, source_target_pairs={{0,1},{1,0},{2,3},{3,2},{4,5},{5,4},{6,7},{7,6},{8,9},{9,8},{10,11... | collective-permute-start | bytes 393224 | tf_op jit(solution)/shard_map/ppermute | solution.py:28
  55.9 20.1 %collective-permute-start.8 = (bf16[256,512]{1,0:T(8,128)(2,1)S(1)}, bf16[256,512]{1,0:T(8,128)(2,1)S(1)}, u32[]{:S(2)}, u32[]{:S(2)}) collective-permute-start(bf16[256,512]{1,0:T(8,128)(2,1)S(1)} %get-tuple-element.50), channel_id=1, source_target_pairs={{0,2},{1,3},{2,0},{3,1},{4,6},{5,7},{6,4},{7,5},{8,10},{9,11},{10,... | collective-permute-start | bytes 786440 | tf_op jit(solution)/shard_map/ppermute | solution.py:38
  59.4 16.6 %collective-permute-start.9 = (bf16[256,512]{1,0:T(8,128)(2,1)S(1)}, bf16[256,512]{1,0:T(8,128)(2,1)S(1)}, u32[]{:S(2)}, u32[]{:S(2)}) collective-permute-start(bf16[256,512]{1,0:T(8,128)(2,1)S(1)} %get-tuple-element.51), channel_id=1, source_target_pairs={{0,254},{1,255},{2,4},{3,5},{4,2},{5,3},{6,8},{7,9},{8,6},{9,7},{1... | collective-permute-start | bytes 786440 | tf_op jit(solution)/shard_map/ppermute | solution.py:38
  61.0 31.7 %all-to-all-start = ((bf16[64,8,512]{2,1,0:T(8,128)(2,1)}), bf16[64,8,512]{2,1,0:T(8,128)(2,1)S(1)}, u32[]{:S(2)}, u32[]{:S(2)}) async-start(bf16[64,8,512]{2,1,0:T(8,128)(2,1)} %bitcast.3), calls=%async_computation | async-start | bytes 1048576 | tf_op jit(solution)/shard_map/all_to_all | solution.py:338
  75.5 1.6 %collective-permute-start.11 = (bf16[128,512]{1,0:T(8,128)(2,1)S(1)}, bf16[128,512]{1,0:T(8,128)(2,1)S(1)}, u32[]{:S(2)}, u32[]{:S(2)}) collective-permute-start(bf16[128,512]{1,0:T(8,128)(2,1)S(1)} %get-tuple-element.61), channel_id=1, source_target_pairs={{0,1},{1,0},{2,3},{3,2},{4,5},{5,4},{6,7},{7,6},{8,9},{9,8},{10,11... | collective-permute-start | bytes 393224 | tf_op jit(solution)/shard_map/ppermute | solution.py:28
  76.1 1.7 %collective-permute-start.10 = (bf16[128,512]{1,0:T(8,128)(2,1)S(1)}, bf16[128,512]{1,0:T(8,128)(2,1)S(1)}, u32[]{:S(2)}, u32[]{:S(2)}) collective-permute-start(bf16[128,512]{1,0:T(8,128)(2,1)S(1)} %get-tuple-element.63), channel_id=1, source_target_pairs={{0,1},{1,0},{2,3},{3,2},{4,5},{5,4},{6,7},{7,6},{8,9},{9,8},{10,11... | collective-permute-start | bytes 393224 | tf_op jit(solution)/shard_map/ppermute | solution.py:28
where the time goes:
time: 93.8 us; the launch traced here: 93.4 us
  starting transfers between devices  50 us (53%)
  waiting for transfers between devices  26.3 us (28%)
  Pallas kernels  9.15 us (10%)
  local copies, waits for them, and re-layouts  3.84 us (4%)
  other arithmetic  3.36 us (4%)
    ppermute x8, starting transfers between devices, swap(): return lax.ppermute(array, AXES, pairs)  17.6 us
    all_to_all x1, starting transfers between devices, steps(): arrived = lax.all_to_all(pieces, ('y', 'z', 'c'), 0, 0, tiled=True)  14.4 us
    all_to_all x1, waiting for transfers between devices, steps(): arrived = lax.all_to_all(pieces, ('y', 'z', 'c'), 0, 0, tiled=True)  14.1 us
    ppermute x5, starting transfers between devices, to_core(): lax.ppermute(array, AXES, [(device, device ^ 1) for device in range(count)])  12.5 us
    ppermute x6, waiting for transfers between devices, along_x(): return lax.ppermute(array, AXES, pairs)  6.29 us
    ppermute x6, starting transfers between devices, along_x(): return lax.ppermute(array, AXES, pairs)  5.45 us
    ppermute x8, waiting for transfers between devices, swap(): return lax.ppermute(array, AXES, pairs)  4.59 us
    unnamed x10, local copies, waits for them, and re-layouts  3.8 us
  transfers between devices with their start and end apart: 20, of which 5 were waited for; matrix products, arithmetic and copies ran while one was open for 3% of the time, Pallas kernels for 9%

commit v1 on v0

--- a/solution.py
+++ b/solution.py
@@ -38,15 +38,10 @@
     return lax.ppermute(array, AXES, pairs)
 
 
-def along_x(array, sizes, step):
+def along_y(array, sizes, step):
     ny, nx, nz, nc = sizes
-    pairs = []
-    for y in range(ny):
-        for x in range(nx):
-            for rest in range(nz * nc):
-                pairs.append(
-                    ((y * nx + x) * nz * nc + rest, (y * nx + (x + step) % nx) * nz * nc + rest)
-                )
+    rest = nx * nz * nc
+    pairs = [(device, (device + step * rest) % (ny * rest)) for device in range(ny * rest)]
     return lax.ppermute(array, AXES, pairs)
 
 
@@ -220,61 +215,74 @@
     )(core, query, grad, *keys, *values, lse)
 
 
-def block_kernel(count, groups, place, own, part, *blocks):
-    rows, width = own.shape
-    size = width // (groups * count)
+def block_kernel(count, place, own, *blocks):
+    size = own.shape[1] // count
     for step, block in enumerate(blocks):
         target = lax.rem(place[2] + step, count)
-        for group in range(groups):
-            start = pl.multiple_of((group * count + target) * size, size)
-            at = slice(group * size, (group + 1) * size)
-            block[:rows, at] = own[:, pl.ds(start, size)]
-            block[rows:, at] = part[:, pl.ds(start, size)]
-
-
-def input_blocks(place, own, part, count, groups):
+        block[...] = own[:, pl.ds(pl.multiple_of(target * size, size), size)]
+
+
+def input_blocks(place, own, count):
     rows, width = own.shape
-    block = jax.ShapeDtypeStruct((2 * rows, width // count), own.dtype)
-    return pl.pallas_call(
-        lambda *refs: block_kernel(count, groups, *refs),
+    block = jax.ShapeDtypeStruct((rows, width // count), own.dtype)
+    return pl.pallas_call(
+        lambda *refs: block_kernel(count, *refs),
         out_shape=(block,) * count,
-        in_specs=[smem()] + vmem(2),
+        in_specs=[smem()] + vmem(1),
         out_specs=tuple(vmem(count)),
         compiler_params=ROOM,
         name="input_blocks",
-    )(place, own, part)
-
-
-def weight_kernel(count, *refs):
-    inputs, gathered, out = refs[:count], refs[count : 2 * count], refs[2 * count]
+    )(place, own)
+
+
+def stack_kernel(count, *refs):
+    for step in range(count):
+        refs[count][step] = refs[step][...]
+
+
+def stack(blocks):
+    count = len(blocks)
+    return pl.pallas_call(
+        lambda *refs: stack_kernel(count, *refs),
+        out_shape=jax.ShapeDtypeStruct((count,) + blocks[0].shape, blocks[0].dtype),
+        in_specs=vmem(count),
+        out_specs=pl.BlockSpec(memory_space=pltpu.VMEM),
+        compiler_params=ROOM,
+        name="stack",
+    )(*blocks)
+
+
+def weight_kernel(count, own, part, *refs):
+    gathered, out = refs[:count], refs[count]
+    rows = own.shape[1]
     tile = 256
     for low in range(0, out.shape[0], tile):
         total = jnp.zeros((tile, out.shape[1]), jnp.float32)
         for step in range(count):
-            total += lax.dot_general(
-                inputs[step][:, low : low + tile],
-                gathered[step][...],
-                FIRST,
-                preferred_element_type=jnp.float32,
-            )
+            for held, start in ((own, 0), (part, rows)):
+                total += lax.dot_general(
+                    held[step, :, low : low + tile],
+                    gathered[step][start : start + rows],
+                    FIRST,
+                    preferred_element_type=jnp.float32,
+                )
         out[low : low + tile] = total.astype(jnp.bfloat16)
 
 
-def weight_pass(inputs, gathered):
-    count = len(inputs)
-    rows, width = inputs[0].shape
+def weight_pass(own, part, gathered):
+    count, rows, width = own.shape
     columns = gathered[0].shape[1]
     return pl.pallas_call(
         lambda *refs: weight_kernel(count, *refs),
         out_shape=jax.ShapeDtypeStruct((width, columns), jnp.bfloat16),
-        in_specs=vmem(2 * count),
+        in_specs=vmem(2 + count),
         out_specs=pl.BlockSpec(memory_space=pltpu.VMEM),
         cost_estimate=pl.CostEstimate(
-            flops=2 * count * rows * width * columns, transcendentals=0, bytes_accessed=4 << 20
+            flops=4 * count * rows * width * columns, transcendentals=0, bytes_accessed=4 << 20
         ),
         compiler_params=ROOM,
         name="weight_pass",
-    )(*inputs, *gathered)
+    )(own, part, *gathered)
 
 
 def steps(query_rows, key_rows, value_rows, out_grad, inputs):
@@ -285,7 +293,7 @@
     scale = 1.0 / math.sqrt(HEAD)
     core = lax.axis_index("c").astype(jnp.int32)
     parity = lax.rem(lax.axis_index("z").astype(jnp.int32), 2)
-    place = jnp.stack([core, parity, lax.axis_index("x").astype(jnp.int32)])
+    place = jnp.stack([core, parity, lax.axis_index("y").astype(jnp.int32)])
     even = core == 0
     place, even, query_rows = lax.optimization_barrier((place, even, query_rows))
 
@@ -307,11 +315,12 @@
     keys, values = (first_k, key, second_k), (first_v, value, second_v)
 
     inputs, _ = lax.optimization_barrier((inputs, mine))
-    inputs_part = to_core(inputs, devices)
-    blocks = input_blocks(place, inputs, inputs_part, nx, ny)
+    blocks = input_blocks(place, inputs, ny)
     taken = [blocks[0]]
-    for step in range(1, nx):
-        taken.append(along_x(blocks[step], sizes, step))
+    for step in range(1, ny):
+        taken.append(along_y(blocks[step], sizes, step))
+    taken = stack(taken)
+    taken_part = to_core(taken, devices)
 
     first, own, second, lse = value_pass(place, query, grad, keys, scale)
     from_first, from_second = swaps(first, second)
@@ -325,19 +334,19 @@
         jnp.bfloat16
     )
     gathered = [value_half]
-    for step in range(1, nx):
-        gathered.append(along_x(value_half, sizes, step))
+    for step in range(1, ny):
+        gathered.append(along_y(value_half, sizes, step))
     key_from_first, key_from_second = swaps(key_first, key_second)
     value_back = to_core(value_half[rows:], devices)
     query_back = to_core(dq_other, devices)
 
-    partial = weight_pass(taken, gathered)
+    partial = weight_pass(taken, taken_part, gathered)
     half = features // 2
     own_count = inputs.shape[1] // devices
-    pieces = partial.reshape(ny * nz * nc, own_count, half)
-    arrived = lax.all_to_all(pieces, ("y", "z", "c"), 0, 0, tiled=True)
+    pieces = partial.reshape(nx * nz * nc, own_count, half)
+    arrived = lax.all_to_all(pieces, ("x", "z", "c"), 0, 0, tiled=True)
     summed = jnp.sum(
-        arrived.reshape(ny * nz, nc, own_count, half).astype(jnp.float32), axis=0
+        arrived.reshape(nx * nz, nc, own_count, half).astype(jnp.float32), axis=0
     )
     weight_grad = summed.transpose(1, 0, 2).reshape(own_count, features) * (
         1.0 / math.sqrt(rows * devices)

time: 93.8 us -> 96.5 us (1.029)
  the two profiles are of different devices: /device:TPU:1 before, /device:TPU:15 now
where the time goes in v1:
time: 96.5 us; the launch traced here: 96.1 us
  starting transfers between devices  51 us (53%)
  waiting for transfers between devices  27.7 us (29%)
  Pallas kernels  9.45 us (10%)
  local copies, waits for them, and re-layouts  3.84 us (4%)
  other arithmetic  3.36 us (3%)
    all_to_all x1, starting transfers between devices, steps(): arrived = lax.all_to_all(pieces, ('x', 'z', 'c'), 0, 0, tiled=True)  22.6 us
    ppermute x8, starting transfers between devices, swap(): return lax.ppermute(array, AXES, pairs)  15.6 us
    all_to_all x1, waiting for transfers between devices, steps(): arrived = lax.all_to_all(pieces, ('x', 'z', 'c'), 0, 0, tiled=True)  13.9 us
    ppermute x6, waiting for transfers between devices, along_y(): return lax.ppermute(array, AXES, pairs)  12.2 us
    ppermute x6, starting transfers between devices, along_y(): return lax.ppermute(array, AXES, pairs)  7.74 us
    ppermute x5, starting transfers between devices, to_core(): lax.ppermute(array, AXES, [(device, device ^ 1) for device in range(count)])  5.05 us
    unnamed x10, local copies, waits for them, and re-layouts  3.8 us
    pallas_call x1, Pallas kernels, score_pass(): pl.pallas_call(lambda *refs: score_kernel(scale, *refs), out_shape=(part,...  3.61 us
  transfers between devices with their start and end apart: 20, of which 6 were waited for; matrix products, arithmetic and copies ran while one was open for 3% of the time, Pallas kernels for 9%

profile of v1, /device:TPU:15, one launch (start us, length us, event | category | flops | bytes accessed | tf_op | source)
XLA Modules:
  0.0 96.1 jit_solution(3948573555175353574)
XLA Ops:
  0.6 0.1 pad_add_fusion.core.refs_0_
  0.7 0.0 copy-start.1
  0.7 0.9 copy-done.1
  1.7 0.0 copy-start.2
  1.7 0.9 copy-done.2
  2.6 0.0 copy-start.3
  2.6 0.9 copy-done.3
  3.6 0.0 copy-start.4
  3.6 0.9 copy-done.4
  4.5 0.8 pack.1
  5.3 0.8 collective-permute-start
  6.1 1.5 %collective-permute-done.part = bf16[4,128,512]{2,1,0:T(8,128)(2,1)S(1)} collective-permute-done((bf16[4,128,512]{2,1,0:T(8,128)(2,1)S(1)}, bf16[4,128,512]{2,1,0:T(8,128)(2,1)S(1)}, u32[]{:S(2)}, u32[]{:S(2)}) %collective-permute-start) | collective-permute-done | bytes 524320 | tf_op jit(solution)/shard_map/ppermute | solution.py:28
  7.6 0.0 copy-start
  7.6 0.1 join.1
  7.7 1.7 %collective-permute-start.1 = (bf16[256,512]{1,0:T(8,128)(2,1)S(1)}, bf16[256,512]{1,0:T(8,128)(2,1)S(1)}, u32[]{:S(2)}, u32[]{:S(2)}) collective-permute-start(bf16[256,512]{1,0:T(8,128)(2,1)S(1)} %get-tuple-element.39.refs_4_), channel_id=1, source_target_pairs={{0,2},{1,3},{2,0},{3,1},{4,6},{5,7},{6,4},{7,5},{8,10},{9,11},{10,... | collective-permute-start | bytes 786440 | tf_op jit(solution)/shard_map/ppermute | solution.py:38
  9.4 4.9 %collective-permute-start.2 = (bf16[256,512]{1,0:T(8,128)(2,1)S(1)}, bf16[256,512]{1,0:T(8,128)(2,1)S(1)}, u32[]{:S(2)}, u32[]{:S(2)}) collective-permute-start(bf16[256,512]{1,0:T(8,128)(2,1)S(1)} %get-tuple-element.39.refs_4_), channel_id=1, source_target_pairs={{0,254},{1,255},{2,4},{3,5},{4,2},{5,3},{6,8},{7,9},{8,6},{9,7},{1... | collective-permute-start | bytes 786440 | tf_op jit(solution)/shard_map/ppermute | solution.py:38
  14.3 0.0 copy-done
  14.3 0.6 input_blocks.1
  14.9 1.4 %collective-permute-start.12 = (bf16[128,512]{1,0:T(8,128)(2,1)S(1)}, bf16[128,512]{1,0:T(8,128)(2,1)S(1)}, u32[]{:S(2)}, u32[]{:S(2)}) collective-permute-start(bf16[128,512]{1,0:T(8,128)(2,1)S(1)} %get-tuple-element.57), channel_id=1, source_target_pairs={{0,64},{1,65},{2,66},{3,67},{4,68},{5,69},{6,70},{7,71},{8,72},{9,... | collective-permute-start | bytes 393224 | tf_op jit(solution)/shard_map/ppermute | solution.py:45
  16.3 0.8 collective-permute-start.13
  17.1 0.0 collective-permute-start.5
  17.1 0.0 collective-permute-done.1.refs_3_
  17.1 4.0 %collective-permute-start.6 = (bf16[256,512]{1,0:T(8,128)(2,1)S(1)}, bf16[256,512]{1,0:T(8,128)(2,1)S(1)}, u32[]{:S(2)}, u32[]{:S(2)}) collective-permute-start(bf16[256,512]{1,0:T(8,128)(2,1)S(1)} %get-tuple-element.42.refs_7_), channel_id=1, source_target_pairs={{0,254},{1,255},{2,4},{3,5},{4,2},{5,3},{6,8},{7,9},{8,6},{9,7},{1... | collective-permute-start | bytes 786440 | tf_op jit(solution)/shard_map/ppermute | solution.py:38
  21.1 0.0 collective-permute-done.2.refs_5_
  21.1 2.3 %value_pass.1 = (bf16[256,512]{1,0:T(8,128)(2,1)S(1)}, f32[256,512]{1,0:T(8,128)S(1)}, bf16[256,512]{1,0:T(8,128)(2,1)S(1)}, f32[4,8,256]{2,1,0:T(8,128)S(1)}) custom-call(s32[3]{0:T(128)S(1)} %pad_add_fusion.core.refs_0_, bf16[256,512]{1,0:T(8,128)(2,1)S(1)} %get-tuple-element.37.refs_1_, bf16[256,512]{1,0:T(8,128)(2,1)S(1)} %get-tuple-element.38.refs_2_, ...), custom_call_target="tpu_custom_call" | custom-call | flops 402653184 | bytes 4194304 | tf_op jit(solution)/shard_map/value_pass/pallas_call | solution.py:185
  23.4 0.1 collective-permute-start.3
  23.5 0.0 collective-permute-done.12.refs_1_
  23.5 2.6 %collective-permute-start.4 = (bf16[256,512]{1,0:T(8,128)(2,1)S(1)}, bf16[256,512]{1,0:T(8,128)(2,1)S(1)}, u32[]{:S(2)}, u32[]{:S(2)}) collective-permute-start(bf16[256,512]{1,0:T(8,128)(2,1)S(1)} %get-tuple-element.41), channel_id=1, source_target_pairs={{0,254},{1,255},{2,4},{3,5},{4,2},{5,3},{6,8},{7,9},{8,6},{9,7},{1... | collective-permute-start | bytes 786440 | tf_op jit(solution)/shard_map/ppermute | solution.py:38
  26.1 0.0 collective-permute-done.13.refs_2_
  26.1 0.2 collective-permute-start.14
  26.3 3.9 %collective-permute-done.14.refs_3_ = bf16[128,512]{1,0:T(8,128)(2,1)S(1)} collective-permute-done((bf16[128,512]{1,0:T(8,128)(2,1)S(1)}, bf16[128,512]{1,0:T(8,128)(2,1)S(1)}, u32[]{:S(2)}, u32[]{:S(2)}) %collective-permute-start.14) | collective-permute-done | bytes 131104 | tf_op jit(solution)/shard_map/ppermute | solution.py:45
  30.3 2.7 %collective-permute-start.15 = (bf16[4,128,512]{2,1,0:T(8,128)(2,1)S(1)}, bf16[4,128,512]{2,1,0:T(8,128)(2,1)S(1)}, u32[]{:S(2)}, u32[]{:S(2)}) collective-permute-start(bf16[4,128,512]{2,1,0:T(8,128)(2,1)S(1)} %stack.17.refs_0_), channel_id=1, source_target_pairs={{0,1},{1,0},{2,3},{3,2},{4,5},{5,4},{6,7},{7,6},{8,9},{9,8},{10,11... | collective-permute-start | bytes 1572872 | tf_op jit(solution)/shard_map/ppermute | solution.py:28
  33.0 0.0 collective-permute-done.5.refs_6_
  33.0 0.0 collective-permute-done.6.refs_8_
  33.0 3.6 %score_pass.1 = (bf16[128,512]{1,0:T(8,128)(2,1)S(1)}, bf16[128,512]{1,0:T(8,128)(2,1)S(1)}, bf16[256,512]{1,0:T(8,128)(2,1)S(1)}, f32[256,512]{1,0:T(8,128)S(1)}, bf16[256,512]{1,0:T(8,128)(2,1)S(1)}) custom-call(s32[3]{0:T(128)S(1)} %pad_add_fusion.core.refs_0_, bf16[256,512]{1,0:T(8,128)(2,1)S(1)} %get-tuple-element.37.refs_1_, ...), custom_call_target="tpu_custom_call" | custom-call | flops 805306368 | bytes 6291456 | tf_op jit(solution)/shard_map/score_pass/pallas_call | solution.py:205
  36.6 0.0 collective-permute-done.3
  36.7 0.0 collective-permute-done.4
  36.7 0.1 add_convert_fusion.refs_2_
  36.8 1.4 %collective-permute-start.16 = (bf16[256,512]{1,0:T(8,128)(2,1)S(1)}, bf16[256,512]{1,0:T(8,128)(2,1)S(1)}, u32[]{:S(2)}, u32[]{:S(2)}) collective-permute-start(bf16[256,512]{1,0:T(8,128)(2,1)S(1)} %add_convert_fusion.refs_2_), channel_id=1, source_target_pairs={{0,64},{1,65},{2,66},{3,67},{4,68},{5,69},{6,70},{7,71},{8,72},{9,... | collective-permute-start | bytes 786440 | tf_op jit(solution)/shard_map/ppermute | solution.py:45
  38.2 2.2 %collective-permute-start.17 = (bf16[256,512]{1,0:T(8,128)(2,1)S(1)}, bf16[256,512]{1,0:T(8,128)(2,1)S(1)}, u32[]{:S(2)}, u32[]{:S(2)}) collective-permute-start(bf16[256,512]{1,0:T(8,128)(2,1)S(1)} %add_convert_fusion.refs_2_), channel_id=1, source_target_pairs={{0,128},{1,129},{2,130},{3,131},{4,132},{5,133},{6,134},{7,135},{8... | collective-permute-start | bytes 786440 | tf_op jit(solution)/shard_map/ppermute | solution.py:45
  40.4 1.8 %collective-permute-start.18 = (bf16[256,512]{1,0:T(8,128)(2,1)S(1)}, bf16[256,512]{1,0:T(8,128)(2,1)S(1)}, u32[]{:S(2)}, u32[]{:S(2)}) collective-permute-start(bf16[256,512]{1,0:T(8,128)(2,1)S(1)} %add_convert_fusion.refs_2_), channel_id=1, source_target_pairs={{0,192},{1,193},{2,194},{3,195},{4,196},{5,197},{6,198},{7,199},{8... | collective-permute-start | bytes 786440 | tf_op jit(solution)/shard_map/ppermute | solution.py:45
  42.2 0.9 collective-permute-start.7
  43.0 0.0 collective-permute-done.15.refs_1_
  43.0 0.4 collective-permute-start.8
  43.4 1.3 %collective-permute-done.16.refs_3_ = bf16[256,512]{1,0:T(8,128)(2,1)S(1)} collective-permute-done((bf16[256,512]{1,0:T(8,128)(2,1)S(1)}, bf16[256,512]{1,0:T(8,128)(2,1)S(1)}, u32[]{:S(2)}, u32[]{:S(2)}) %collective-permute-start.16) | collective-permute-done | bytes 262176 | tf_op jit(solution)/shard_map/ppermute | solution.py:45
  44.7 1.9 %collective-permute-start.9 = (bf16[256,512]{1,0:T(8,128)(2,1)S(1)}, bf16[256,512]{1,0:T(8,128)(2,1)S(1)}, u32[]{:S(2)}, u32[]{:S(2)}) collective-permute-start(bf16[256,512]{1,0:T(8,128)(2,1)S(1)} %get-tuple-element.51), channel_id=1, source_target_pairs={{0,254},{1,255},{2,4},{3,5},{4,2},{5,3},{6,8},{7,9},{8,6},{9,7},{1... | collective-permute-start | bytes 786440 | tf_op jit(solution)/shard_map/ppermute | solution.py:38
  46.6 0.7 collective-permute-done.17.refs_4_
  47.3 6.3 %collective-permute-done.18.refs_5_ = bf16[256,512]{1,0:T(8,128)(2,1)S(1)} collective-permute-done((bf16[256,512]{1,0:T(8,128)(2,1)S(1)}, bf16[256,512]{1,0:T(8,128)(2,1)S(1)}, u32[]{:S(2)}, u32[]{:S(2)}) %collective-permute-start.18) | collective-permute-done | bytes 262176 | tf_op jit(solution)/shard_map/ppermute | solution.py:45
  53.5 2.1 %weight_pass.1 = bf16[512,512]{1,0:T(8,128)(2,1)} custom-call(bf16[4,128,512]{2,1,0:T(8,128)(2,1)S(1)} %stack.17.refs_0_, bf16[4,128,512]{2,1,0:T(8,128)(2,1)S(1)} %collective-permute-done.15.refs_1_, bf16[256,512]{1,0:T(8,128)(2,1)S(1)} %add_convert_fusion.refs_2_, bf16[256,512]{1,0:T(8,128)(2,1)S(1)} %collective-permute-done.16.refs_3_, ...), custom_call_target="tpu_custom_call" | custom-call | flops 536870912 | bytes 4194304 | tf_op jit(solution)/shard_map/weight_pass/pallas_call | solution.py:275
  55.6 22.6 %all-to-all-start = ((bf16[64,8,512]{2,1,0:T(8,128)(2,1)}), bf16[64,8,512]{2,1,0:T(8,128)(2,1)S(1)}, u32[]{:S(2)}, u32[]{:S(2)}) async-start(bf16[64,8,512]{2,1,0:T(8,128)(2,1)} %bitcast.3), calls=%async_computation | async-start | bytes 1048576 | tf_op jit(solution)/shard_map/all_to_all | solution.py:347
  78.3 0.5 collective-permute-start.11
  78.8 0.0 collective-permute-done.8
  78.8 0.0 collective-permute-done.9
  78.8 0.1 add_convert_fusion.1
  78.9 0.2 collective-permute-start.10
  79.1 0.0 collective-permute-done.7
  79.1 0.8 maximum_select_fusion
  79.9 0.0 collective-permute-done.11
  79.9 0.8 maximum_select_fusion.2
  80.7 0.0 collective-permute-done.10
  80.7 0.8 maximum_select_fusion.1
  81.5 13.9 %all-to-all-done = bf16[64,8,512]{2,1,0:T(8,128)(2,1)S(1)} async-done(((bf16[64,8,512]{2,1,0:T(8,128)(2,1)}), bf16[64,8,512]{2,1,0:T(8,128)(2,1)S(1)}, u32[]{:S(2)}, u32[]{:S(2)}) %all-to-all-start) | async-done | bytes 524320 | tf_op jit(solution)/shard_map/all_to_all | solution.py:347
  95.4 0.1 convert_reduce_fusion
  95.5 0.6 broadcast_multiply_fusion
  (3 shorter events, 0.1 us)
Async XLA Ops:
  0.7 1.0 copy-start.1
  1.7 0.9 copy-start.2
  2.6 0.9 copy-start.3
  3.6 0.9 copy-start.4
  5.3 2.3 %collective-permute-start = (bf16[4,128,512]{2,1,0:T(8,128)(2,1)S(1)}, bf16[4,128,512]{2,1,0:T(8,128)(2,1)S(1)}, u32[]{:S(2)}, u32[]{:S(2)}) collective-permute-start(bf16[4,128,512]{2,1,0:T(8,128)(2,1)S(1)} %get-tuple-element.36), channel_id=1, source_target_pairs={{0,1},{1,0},{2,3},{3,2},{4,5},{5,4},{6,7},{7,6},{8,9},{9,8},{10,11... | collective-permute-start | bytes 1572872 | tf_op jit(solution)/shard_map/ppermute | solution.py:28
  7.6 6.7 %copy-start = (bf16[128,2048]{1,0:T(8,128)(2,1)S(1)}, bf16[128,2048]{1,0:T(8,128)(2,1)}, u32[]{:S(2)}) copy-start(bf16[128,2048]{1,0:T(8,128)(2,1)} %refs_1_) | copy-start | bytes 1572868
  7.7 9.4 %collective-permute-start.1 = (bf16[256,512]{1,0:T(8,128)(2,1)S(1)}, bf16[256,512]{1,0:T(8,128)(2,1)S(1)}, u32[]{:S(2)}, u32[]{:S(2)}) collective-permute-start(bf16[256,512]{1,0:T(8,128)(2,1)S(1)} %get-tuple-element.39.refs_4_), channel_id=1, source_target_pairs={{0,2},{1,3},{2,0},{3,1},{4,6},{5,7},{6,4},{7,5},{8,10},{9,11},{10,... | collective-permute-start | bytes 786440 | tf_op jit(solution)/shard_map/ppermute | solution.py:38
  9.4 11.7 %collective-permute-start.2 = (bf16[256,512]{1,0:T(8,128)(2,1)S(1)}, bf16[256,512]{1,0:T(8,128)(2,1)S(1)}, u32[]{:S(2)}, u32[]{:S(2)}) collective-permute-start(bf16[256,512]{1,0:T(8,128)(2,1)S(1)} %get-tuple-element.39.refs_4_), channel_id=1, source_target_pairs={{0,254},{1,255},{2,4},{3,5},{4,2},{5,3},{6,8},{7,9},{8,6},{9,7},{1... | collective-permute-start | bytes 786440 | tf_op jit(solution)/shard_map/ppermute | solution.py:38
  14.9 8.6 %collective-permute-start.12 = (bf16[128,512]{1,0:T(8,128)(2,1)S(1)}, bf16[128,512]{1,0:T(8,128)(2,1)S(1)}, u32[]{:S(2)}, u32[]{:S(2)}) collective-permute-start(bf16[128,512]{1,0:T(8,128)(2,1)S(1)} %get-tuple-element.57), channel_id=1, source_target_pairs={{0,64},{1,65},{2,66},{3,67},{4,68},{5,69},{6,70},{7,71},{8,72},{9,... | collective-permute-start | bytes 393224 | tf_op jit(solution)/shard_map/ppermute | solution.py:45
  16.3 9.8 %collective-permute-start.13 = (bf16[128,512]{1,0:T(8,128)(2,1)S(1)}, bf16[128,512]{1,0:T(8,128)(2,1)S(1)}, u32[]{:S(2)}, u32[]{:S(2)}) collective-permute-start(bf16[128,512]{1,0:T(8,128)(2,1)S(1)} %get-tuple-element.58), channel_id=1, source_target_pairs={{0,128},{1,129},{2,130},{3,131},{4,132},{5,133},{6,134},{7,135},{8... | collective-permute-start | bytes 393224 | tf_op jit(solution)/shard_map/ppermute | solution.py:45
  17.1 15.9 %collective-permute-start.5 = (bf16[256,512]{1,0:T(8,128)(2,1)S(1)}, bf16[256,512]{1,0:T(8,128)(2,1)S(1)}, u32[]{:S(2)}, u32[]{:S(2)}) collective-permute-start(bf16[256,512]{1,0:T(8,128)(2,1)S(1)} %get-tuple-element.42.refs_7_), channel_id=1, source_target_pairs={{0,2},{1,3},{2,0},{3,1},{4,6},{5,7},{6,4},{7,5},{8,10},{9,11},{10,... | collective-permute-start | bytes 786440 | tf_op jit(solution)/shard_map/ppermute | solution.py:38
  17.1 15.9 %collective-permute-start.6 = (bf16[256,512]{1,0:T(8,128)(2,1)S(1)}, bf16[256,512]{1,0:T(8,128)(2,1)S(1)}, u32[]{:S(2)}, u32[]{:S(2)}) collective-permute-start(bf16[256,512]{1,0:T(8,128)(2,1)S(1)} %get-tuple-element.42.refs_7_), channel_id=1, source_target_pairs={{0,254},{1,255},{2,4},{3,5},{4,2},{5,3},{6,8},{7,9},{8,6},{9,7},{1... | collective-permute-start | bytes 786440 | tf_op jit(solution)/shard_map/ppermute | solution.py:38
  23.4 13.3 %collective-permute-start.3 = (bf16[256,512]{1,0:T(8,128)(2,1)S(1)}, bf16[256,512]{1,0:T(8,128)(2,1)S(1)}, u32[]{:S(2)}, u32[]{:S(2)}) collective-permute-start(bf16[256,512]{1,0:T(8,128)(2,1)S(1)} %get-tuple-element.40), channel_id=1, source_target_pairs={{0,2},{1,3},{2,0},{3,1},{4,6},{5,7},{6,4},{7,5},{8,10},{9,11},{10,... | collective-permute-start | bytes 786440 | tf_op jit(solution)/shard_map/ppermute | solution.py:38
  23.5 13.2 %collective-permute-start.4 = (bf16[256,512]{1,0:T(8,128)(2,1)S(1)}, bf16[256,512]{1,0:T(8,128)(2,1)S(1)}, u32[]{:S(2)}, u32[]{:S(2)}) collective-permute-start(bf16[256,512]{1,0:T(8,128)(2,1)S(1)} %get-tuple-element.41), channel_id=1, source_target_pairs={{0,254},{1,255},{2,4},{3,5},{4,2},{5,3},{6,8},{7,9},{8,6},{9,7},{1... | collective-permute-start | bytes 786440 | tf_op jit(solution)/shard_map/ppermute | solution.py:38
  26.1 4.1 %collective-permute-start.14 = (bf16[128,512]{1,0:T(8,128)(2,1)S(1)}, bf16[128,512]{1,0:T(8,128)(2,1)S(1)}, u32[]{:S(2)}, u32[]{:S(2)}) collective-permute-start(bf16[128,512]{1,0:T(8,128)(2,1)S(1)} %get-tuple-element.59), channel_id=1, source_target_pairs={{0,192},{1,193},{2,194},{3,195},{4,196},{5,197},{6,198},{7,199},{8... | collective-permute-start | bytes 393224 | tf_op jit(solution)/shard_map/ppermute | solution.py:45
  30.3 12.7 %collective-permute-start.15 = (bf16[4,128,512]{2,1,0:T(8,128)(2,1)S(1)}, bf16[4,128,512]{2,1,0:T(8,128)(2,1)S(1)}, u32[]{:S(2)}, u32[]{:S(2)}) collective-permute-start(bf16[4,128,512]{2,1,0:T(8,128)(2,1)S(1)} %stack.17.refs_0_), channel_id=1, source_target_pairs={{0,1},{1,0},{2,3},{3,2},{4,5},{5,4},{6,7},{7,6},{8,9},{9,8},{10,11... | collective-permute-start | bytes 1572872 | tf_op jit(solution)/shard_map/ppermute | solution.py:28
  36.8 7.9 %collective-permute-start.16 = (bf16[256,512]{1,0:T(8,128)(2,1)S(1)}, bf16[256,512]{1,0:T(8,128)(2,1)S(1)}, u32[]{:S(2)}, u32[]{:S(2)}) collective-permute-start(bf16[256,512]{1,0:T(8,128)(2,1)S(1)} %add_convert_fusion.refs_2_), channel_id=1, source_target_pairs={{0,64},{1,65},{2,66},{3,67},{4,68},{5,69},{6,70},{7,71},{8,72},{9,... | collective-permute-start | bytes 786440 | tf_op jit(solution)/shard_map/ppermute | solution.py:45
  38.2 9.1 %collective-permute-start.17 = (bf16[256,512]{1,0:T(8,128)(2,1)S(1)}, bf16[256,512]{1,0:T(8,128)(2,1)S(1)}, u32[]{:S(2)}, u32[]{:S(2)}) collective-permute-start(bf16[256,512]{1,0:T(8,128)(2,1)S(1)} %add_convert_fusion.refs_2_), channel_id=1, source_target_pairs={{0,128},{1,129},{2,130},{3,131},{4,132},{5,133},{6,134},{7,135},{8... | collective-permute-start | bytes 786440 | tf_op jit(solution)/shard_map/ppermute | solution.py:45
  40.4 13.2 %collective-permute-start.18 = (bf16[256,512]{1,0:T(8,128)(2,1)S(1)}, bf16[256,512]{1,0:T(8,128)(2,1)S(1)}, u32[]{:S(2)}, u32[]{:S(2)}) collective-permute-start(bf16[256,512]{1,0:T(8,128)(2,1)S(1)} %add_convert_fusion.refs_2_), channel_id=1, source_target_pairs={{0,192},{1,193},{2,194},{3,195},{4,196},{5,197},{6,198},{7,199},{8... | collective-permute-start | bytes 786440 | tf_op jit(solution)/shard_map/ppermute | solution.py:45
  42.2 36.9 %collective-permute-start.7 = (bf16[128,512]{1,0:T(8,128)(2,1)S(1)}, bf16[128,512]{1,0:T(8,128)(2,1)S(1)}, u32[]{:S(2)}, u32[]{:S(2)}) collective-permute-start(bf16[128,512]{1,0:T(8,128)(2,1)S(1)} %get-tuple-element.48), channel_id=1, source_target_pairs={{0,1},{1,0},{2,3},{3,2},{4,5},{5,4},{6,7},{7,6},{8,9},{9,8},{10,11... | collective-permute-start | bytes 393224 | tf_op jit(solution)/shard_map/ppermute | solution.py:28
  43.0 35.7 %collective-permute-start.8 = (bf16[256,512]{1,0:T(8,128)(2,1)S(1)}, bf16[256,512]{1,0:T(8,128)(2,1)S(1)}, u32[]{:S(2)}, u32[]{:S(2)}) collective-permute-start(bf16[256,512]{1,0:T(8,128)(2,1)S(1)} %get-tuple-element.50), channel_id=1, source_target_pairs={{0,2},{1,3},{2,0},{3,1},{4,6},{5,7},{6,4},{7,5},{8,10},{9,11},{10,... | collective-permute-start | bytes 786440 | tf_op jit(solution)/shard_map/ppermute | solution.py:38
  44.7 34.1 %collective-permute-start.9 = (bf16[256,512]{1,0:T(8,128)(2,1)S(1)}, bf16[256,512]{1,0:T(8,128)(2,1)S(1)}, u32[]{:S(2)}, u32[]{:S(2)}) collective-permute-start(bf16[256,512]{1,0:T(8,128)(2,1)S(1)} %get-tuple-element.51), channel_id=1, source_target_pairs={{0,254},{1,255},{2,4},{3,5},{4,2},{5,3},{6,8},{7,9},{8,6},{9,7},{1... | collective-permute-start | bytes 786440 | tf_op jit(solution)/shard_map/ppermute | solution.py:38
  55.6 39.8 %all-to-all-start = ((bf16[64,8,512]{2,1,0:T(8,128)(2,1)}), bf16[64,8,512]{2,1,0:T(8,128)(2,1)S(1)}, u32[]{:S(2)}, u32[]{:S(2)}) async-start(bf16[64,8,512]{2,1,0:T(8,128)(2,1)} %bitcast.3), calls=%async_computation | async-start | bytes 1048576 | tf_op jit(solution)/shard_map/all_to_all | solution.py:347
  78.3 1.6 %collective-permute-start.11 = (bf16[128,512]{1,0:T(8,128)(2,1)S(1)}, bf16[128,512]{1,0:T(8,128)(2,1)S(1)}, u32[]{:S(2)}, u32[]{:S(2)}) collective-permute-start(bf16[128,512]{1,0:T(8,128)(2,1)S(1)} %get-tuple-element.61), channel_id=1, source_target_pairs={{0,1},{1,0},{2,3},{3,2},{4,5},{5,4},{6,7},{7,6},{8,9},{9,8},{10,11... | collective-permute-start | bytes 393224 | tf_op jit(solution)/shard_map/ppermute | solution.py:28
  78.9 1.8 %collective-permute-start.10 = (bf16[128,512]{1,0:T(8,128)(2,1)S(1)}, bf16[128,512]{1,0:T(8,128)(2,1)S(1)}, u32[]{:S(2)}, u32[]{:S(2)}) collective-permute-start(bf16[128,512]{1,0:T(8,128)(2,1)S(1)} %get-tuple-element.63), channel_id=1, source_target_pairs={{0,1},{1,0},{2,3},{3,2},{4,5},{5,4},{6,7},{7,6},{8,9},{9,8},{10,11... | collective-permute-start | bytes 393224 | tf_op jit(solution)/shard_map/ppermute | solution.py:28

commit v2 on v1

--- a/solution.py
+++ b/solution.py
@@ -53,53 +53,57 @@
     return pl.BlockSpec(memory_space=pltpu.SMEM)
 
 
-def pack_kernel(core, query, key, value, grad, mine, other, done):
+def pack_kernel(core, key, query, grad, value, key_mine, key_other, mine, other, done):
     half = query.shape[1] // 2
     here = pl.multiple_of(core[0] * half, half)
     there = pl.multiple_of((1 - core[0]) * half, half)
-    copies = []
-    for at, source in enumerate((key, query, grad, value)):
-        for side, (target, start) in enumerate(((other, there), (mine, here))):
-            copies.append(
-                pltpu.make_async_copy(
-                    source.at[:, pl.ds(start, half)], target.at[at], done.at[2 * at + side]
-                )
-            )
+    moves = [(key, key_other, there), (key, key_mine, here)]
+    for at, source in enumerate((query, grad, value)):
+        moves += [(source, other.at[at], there), (source, mine.at[at], here)]
+    copies = [
+        pltpu.make_async_copy(source.at[:, pl.ds(start, half)], target, done.at[at])
+        for at, (source, target, start) in enumerate(moves)
+    ]
     for copy in copies:
         copy.start()
     for copy in copies:
         copy.wait()
 
 
-def pack(core, query, key, value, grad):
+def pack(core, key, query, grad, value):
     rows, features = query.shape
-    four = jax.ShapeDtypeStruct((4, rows, features // 2), query.dtype)
+    one = jax.ShapeDtypeStruct((rows, features // 2), query.dtype)
+    three = jax.ShapeDtypeStruct((3, rows, features // 2), query.dtype)
     return pl.pallas_call(
         pack_kernel,
-        out_shape=(four, four),
+        out_shape=(one, one, three, three),
         in_specs=[smem()] + [pl.BlockSpec(memory_space=pltpu.HBM)] * 4,
-        out_specs=tuple(vmem(2)),
+        out_specs=tuple(vmem(4)),
         scratch_shapes=[pltpu.SemaphoreType.DMA((8,))],
         compiler_params=ROOM,
         name="pack",
-    )(core, query, key, value, grad)
-
-
-def join_kernel(mine, part, key, query, grad, value):
-    rows = mine.shape[1]
-    for at, target in enumerate((key, query, grad, value)):
-        target[:rows] = mine[at]
-        target[rows:] = part[at]
-
-
-def join(mine, part):
-    _, rows, half = mine.shape
+    )(core, *(in_hbm(array) for array in (key, query, grad, value)))
+
+
+def in_hbm(array):
+    return pltpu.with_memory_space_constraint(array, pltpu.HBM)
+
+
+def join_kernel(count, mine, part, *targets):
+    rows = mine.shape[-2]
+    for at, target in enumerate(targets):
+        target[:rows] = mine[at] if count > 1 else mine[...]
+        target[rows:] = part[at] if count > 1 else part[...]
+
+
+def join(mine, part, count):
+    rows, half = mine.shape[-2:]
     two = jax.ShapeDtypeStruct((2 * rows, half), mine.dtype)
     return pl.pallas_call(
-        join_kernel,
-        out_shape=(two,) * 4,
+        lambda *refs: join_kernel(count, *refs),
+        out_shape=(two,) * count,
         in_specs=vmem(2),
-        out_specs=tuple(vmem(4)),
+        out_specs=tuple(vmem(count)),
         compiler_params=ROOM,
         name="join",
     )(mine, part)
@@ -307,40 +311,40 @@
         got_two = swap(two, devices, 1)
         return got_one, got_two
 
-    mine, other = pack(place, query_rows, key_rows, value_rows, out_grad)
+    key_mine, key_other, mine, other = pack(place, key_rows, query_rows, out_grad, value_rows)
+    key_part = to_core(key_other, devices)
     part = to_core(other, devices)
-    key, query, grad, value = join(mine, part)
+    (key,) = join(key_mine, key_part, 1)
     first_k, second_k = swaps(key, key)
-    first_v, second_v = swaps(value, value)
-    keys, values = (first_k, key, second_k), (first_v, value, second_v)
+    keys = (first_k, key, second_k)
+    query, grad, value = join(mine, part, 3)
 
     inputs, _ = lax.optimization_barrier((inputs, mine))
     blocks = input_blocks(place, inputs, ny)
     taken = [blocks[0]]
     for step in range(1, ny):
         taken.append(along_y(blocks[step], sizes, step))
+
+    first, own, second, lse = value_pass(place, query, grad, keys, scale)
+    from_first, from_second = swaps(first, second)
+    value_half = (own + from_first.astype(jnp.float32) + from_second.astype(jnp.float32)).astype(
+        jnp.bfloat16
+    )
+    first_v, second_v = swaps(value, value)
+    query, _ = lax.optimization_barrier((query, value_half))
+    dq, dq_other, key_first, key_own, key_second = score_pass(
+        place, query, grad, keys, (first_v, value, second_v), lse, scale
+    )
+    *taken, _ = lax.optimization_barrier((*taken, value_half))
     taken = stack(taken)
     taken_part = to_core(taken, devices)
-
-    first, own, second, lse = value_pass(place, query, grad, keys, scale)
-    from_first, from_second = swaps(first, second)
-    dq, dq_other, key_first, key_own, key_second = score_pass(
-        place, query, grad, keys, values, lse, scale
-    )
-    from_first, from_second, dq, key_first, key_second = lax.optimization_barrier(
-        (from_first, from_second, dq, key_first, key_second)
-    )
-    value_half = (own + from_first.astype(jnp.float32) + from_second.astype(jnp.float32)).astype(
-        jnp.bfloat16
-    )
     gathered = [value_half]
     for step in range(1, ny):
         gathered.append(along_y(value_half, sizes, step))
+    partial = weight_pass(taken, taken_part, gathered)
     key_from_first, key_from_second = swaps(key_first, key_second)
     value_back = to_core(value_half[rows:], devices)
     query_back = to_core(dq_other, devices)
-
-    partial = weight_pass(taken, taken_part, gathered)
     half = features // 2
     own_count = inputs.shape[1] // devices
     pieces = partial.reshape(nx * nz * nc, own_count, half)

time: 96.5 us -> 98.4 us (1.020)
  the two profiles are of different devices: /device:TPU:15 before, /device:TPU:31 now
where the time goes in v2:
time: 98.4 us; the launch traced here: 98.3 us
  starting transfers between devices  47.2 us (48%)
  waiting for transfers between devices  36.3 us (37%)
  Pallas kernels  10.6 us (11%)
  other arithmetic  3.36 us (3%)
    all_to_all x1, starting transfers between devices, steps(): arrived = lax.all_to_all(pieces, ('x', 'z', 'c'), 0, 0, tiled=True)  27.4 us
    ppermute x8, waiting for transfers between devices, swap(): return lax.ppermute(array, AXES, pairs)  16.8 us
    all_to_all x1, waiting for transfers between devices, steps(): arrived = lax.all_to_all(pieces, ('x', 'z', 'c'), 0, 0, tiled=True)  13.9 us
    ppermute x8, starting transfers between devices, swap(): return lax.ppermute(array, AXES, pairs)  10.4 us
    ppermute x6, starting transfers between devices, to_core(): lax.ppermute(array, AXES, [(device, device ^ 1) for device in range(count)])  5.11 us
    ppermute x6, starting transfers between devices, along_y(): return lax.ppermute(array, AXES, pairs)  4.35 us
    ppermute x6, waiting for transfers between devices, along_y(): return lax.ppermute(array, AXES, pairs)  4.15 us
    pallas_call x1, Pallas kernels, score_pass(): pl.pallas_call(lambda *refs: score_kernel(scale, *refs), out_shape=(part,...  3.62 us
  transfers between devices with their start and end apart: 21, of which 10 were waited for; matrix products, arithmetic and copies ran while one was open for 3% of the time, Pallas kernels for 7%

profile of v2, /device:TPU:31, one launch (start us, length us, event | category | flops | bytes accessed | tf_op | source)
XLA Modules:
  0.0 98.3 jit_solution(5639499472200395272)
XLA Ops:
  0.6 0.1 pad_add_fusion.core.refs_0_
  0.7 1.9 %pack.1 = (bf16[128,512]{1,0:T(8,128)(2,1)S(1)}, bf16[128,512]{1,0:T(8,128)(2,1)S(1)}, bf16[3,128,512]{2,1,0:T(8,128)(2,1)S(1)}, bf16[3,128,512]{2,1,0:T(8,128)(2,1)S(1)}) custom-call(s32[3]{0:T(128)S(1)} %pad_add_fusion.core.refs_0_, bf16[128,1024]{1,0:T(8,128)(2,1)} %key.1, bf16[128,1024]{1,0:T(8,128)(2,1)} %query, bf16[128,1024]{1,0:T(8,128)(2,1)} %grad.1, ...), custom_call_target="tpu_custom_call" | custom-call | tf_op jit(solution)/shard_map/pack/pallas_call | solution.py:77
  2.6 0.8 collective-permute-start
  3.4 0.1 collective-permute-start.1
  3.5 1.4 %collective-permute-done.1.refs_1_ = bf16[128,512]{1,0:T(8,128)(2,1)S(1)} collective-permute-done((bf16[128,512]{1,0:T(8,128)(2,1)S(1)}, bf16[128,512]{1,0:T(8,128)(2,1)S(1)}, u32[]{:S(2)}, u32[]{:S(2)}) %collective-permute-start.1) | collective-permute-done | bytes 131104 | tf_op jit(solution)/shard_map/ppermute | solution.py:28
  4.9 1.7 %collective-permute-start.2 = (bf16[256,512]{1,0:T(8,128)(2,1)S(1)}, bf16[256,512]{1,0:T(8,128)(2,1)S(1)}, u32[]{:S(2)}, u32[]{:S(2)}) collective-permute-start(bf16[256,512]{1,0:T(8,128)(2,1)S(1)} %join.3.refs_4_), channel_id=1, source_target_pairs={{0,2},{1,3},{2,0},{3,1},{4,6},{5,7},{6,4},{7,5},{8,10},{9,11},{10,... | collective-permute-start | bytes 786440 | tf_op jit(solution)/shard_map/ppermute | solution.py:38
  6.7 4.9 %collective-permute-start.3 = (bf16[256,512]{1,0:T(8,128)(2,1)S(1)}, bf16[256,512]{1,0:T(8,128)(2,1)S(1)}, u32[]{:S(2)}, u32[]{:S(2)}) collective-permute-start(bf16[256,512]{1,0:T(8,128)(2,1)S(1)} %join.3.refs_4_), channel_id=1, source_target_pairs={{0,254},{1,255},{2,4},{3,5},{4,2},{5,3},{6,8},{7,9},{8,6},{9,7},{1... | collective-permute-start | bytes 786440 | tf_op jit(solution)/shard_map/ppermute | solution.py:38
  11.6 0.0 collective-permute-done.refs_1_
  11.6 0.1 join.2
  11.7 1.2 %collective-permute-done.2.refs_3_ = bf16[256,512]{1,0:T(8,128)(2,1)S(1)} collective-permute-done((bf16[256,512]{1,0:T(8,128)(2,1)S(1)}, bf16[256,512]{1,0:T(8,128)(2,1)S(1)}, u32[]{:S(2)}, u32[]{:S(2)}) %collective-permute-start.2) | collective-permute-done | bytes 262176 | tf_op jit(solution)/shard_map/ppermute | solution.py:38
  12.9 4.8 %collective-permute-done.3.refs_5_ = bf16[256,512]{1,0:T(8,128)(2,1)S(1)} collective-permute-done((bf16[256,512]{1,0:T(8,128)(2,1)S(1)}, bf16[256,512]{1,0:T(8,128)(2,1)S(1)}, u32[]{:S(2)}, u32[]{:S(2)}) %collective-permute-start.3) | collective-permute-done | bytes 262176 | tf_op jit(solution)/shard_map/ppermute | solution.py:38
  17.6 0.0 copy-start
  17.6 2.3 %value_pass.1 = (bf16[256,512]{1,0:T(8,128)(2,1)S(1)}, f32[256,512]{1,0:T(8,128)S(1)}, bf16[256,512]{1,0:T(8,128)(2,1)S(1)}, f32[4,8,256]{2,1,0:T(8,128)S(1)}) custom-call(s32[3]{0:T(128)S(1)} %pad_add_fusion.core.refs_0_, bf16[256,512]{1,0:T(8,128)(2,1)S(1)} %get-tuple-element.45.refs_1_, bf16[256,512]{1,0:T(8,128)(2,1)S(1)} %get-tuple-element.39.refs_2_, ...), custom_call_target="tpu_custom_call" | custom-call | flops 402653184 | bytes 4194304 | tf_op jit(solution)/shard_map/value_pass/pallas_call | solution.py:189
  19.9 3.4 %collective-permute-start.5 = (bf16[256,512]{1,0:T(8,128)(2,1)S(1)}, bf16[256,512]{1,0:T(8,128)(2,1)S(1)}, u32[]{:S(2)}, u32[]{:S(2)}) collective-permute-start(bf16[256,512]{1,0:T(8,128)(2,1)S(1)} %get-tuple-element.44), channel_id=1, source_target_pairs={{0,254},{1,255},{2,4},{3,5},{4,2},{5,3},{6,8},{7,9},{8,6},{9,7},{1... | collective-permute-start | bytes 786440 | tf_op jit(solution)/shard_map/ppermute | solution.py:38
  23.3 0.0 collective-permute-start.4
  23.3 0.0 copy-done
  23.3 0.6 input_blocks.1
  23.9 0.1 collective-permute-start.13
  24.0 2.2 %collective-permute-start.14 = (bf16[128,512]{1,0:T(8,128)(2,1)S(1)}, bf16[128,512]{1,0:T(8,128)(2,1)S(1)}, u32[]{:S(2)}, u32[]{:S(2)}) collective-permute-start(bf16[128,512]{1,0:T(8,128)(2,1)S(1)} %get-tuple-element.56), channel_id=1, source_target_pairs={{0,128},{1,129},{2,130},{3,131},{4,132},{5,133},{6,134},{7,135},{8... | collective-permute-start | bytes 393224 | tf_op jit(solution)/shard_map/ppermute | solution.py:45
  26.2 0.0 collective-permute-start.15
  26.2 2.5 %collective-permute-done.5 = bf16[256,512]{1,0:T(8,128)(2,1)S(1)} collective-permute-done((bf16[256,512]{1,0:T(8,128)(2,1)S(1)}, bf16[256,512]{1,0:T(8,128)(2,1)S(1)}, u32[]{:S(2)}, u32[]{:S(2)}) %collective-permute-start.5) | collective-permute-done | bytes 262176 | tf_op jit(solution)/shard_map/ppermute | solution.py:38
  28.8 0.0 collective-permute-start.6
  28.8 0.6 collective-permute-done.4
  29.4 0.1 add_convert_fusion.1.refs_2_
  29.5 0.0 collective-permute-done.13.refs_1_
  29.5 0.2 collective-permute-done.14.refs_2_
  29.7 2.7 %collective-permute-done.15.refs_3_ = bf16[128,512]{1,0:T(8,128)(2,1)S(1)} collective-permute-done((bf16[128,512]{1,0:T(8,128)(2,1)S(1)}, bf16[128,512]{1,0:T(8,128)(2,1)S(1)}, u32[]{:S(2)}, u32[]{:S(2)}) %collective-permute-start.15) | collective-permute-done | bytes 131104 | tf_op jit(solution)/shard_map/ppermute | solution.py:45
  32.5 2.5 %collective-permute-start.16 = (bf16[4,128,512]{2,1,0:T(8,128)(2,1)S(1)}, bf16[4,128,512]{2,1,0:T(8,128)(2,1)S(1)}, u32[]{:S(2)}, u32[]{:S(2)}) collective-permute-start(bf16[4,128,512]{2,1,0:T(8,128)(2,1)S(1)} %stack.17.refs_0_), channel_id=1, source_target_pairs={{0,1},{1,0},{2,3},{3,2},{4,5},{5,4},{6,7},{7,6},{8,9},{9,8},{10,11... | collective-permute-start | bytes 1572872 | tf_op jit(solution)/shard_map/ppermute | solution.py:28
  35.0 0.2 collective-permute-start.7
  35.2 0.4 collective-permute-start.17
  35.6 1.6 %collective-permute-start.18 = (bf16[256,512]{1,0:T(8,128)(2,1)S(1)}, bf16[256,512]{1,0:T(8,128)(2,1)S(1)}, u32[]{:S(2)}, u32[]{:S(2)}) collective-permute-start(bf16[256,512]{1,0:T(8,128)(2,1)S(1)} %add_convert_fusion.1.refs_2_), channel_id=1, source_target_pairs={{0,128},{1,129},{2,130},{3,131},{4,132},{5,133},{6,134},{7,135},{8... | collective-permute-start | bytes 786440 | tf_op jit(solution)/shard_map/ppermute | solution.py:45
  37.2 0.0 collective-permute-done.6.refs_6_
  37.2 0.0 collective-permute-start.19
  37.2 7.7 %collective-permute-done.7.refs_8_ = bf16[256,512]{1,0:T(8,128)(2,1)S(1)} collective-permute-done((bf16[256,512]{1,0:T(8,128)(2,1)S(1)}, bf16[256,512]{1,0:T(8,128)(2,1)S(1)}, u32[]{:S(2)}, u32[]{:S(2)}) %collective-permute-start.7) | collective-permute-done | bytes 262176 | tf_op jit(solution)/shard_map/ppermute | solution.py:38
  44.9 3.6 %score_pass.1 = (bf16[128,512]{1,0:T(8,128)(2,1)S(1)}, bf16[128,512]{1,0:T(8,128)(2,1)S(1)}, bf16[256,512]{1,0:T(8,128)(2,1)S(1)}, f32[256,512]{1,0:T(8,128)S(1)}, bf16[256,512]{1,0:T(8,128)(2,1)S(1)}) custom-call(s32[3]{0:T(128)S(1)} %pad_add_fusion.core.refs_0_, bf16[256,512]{1,0:T(8,128)(2,1)S(1)} %get-tuple-element.45.refs_1_, ...), custom_call_target="tpu_custom_call" | custom-call | flops 805306368 | bytes 6291456 | tf_op jit(solution)/shard_map/score_pass/pallas_call | solution.py:209
  48.5 1.0 %collective-permute-start.8 = (bf16[128,512]{1,0:T(8,128)(2,1)S(1)}, bf16[128,512]{1,0:T(8,128)(2,1)S(1)}, u32[]{:S(2)}, u32[]{:S(2)}) collective-permute-start(bf16[128,512]{1,0:T(8,128)(2,1)S(1)} %get-tuple-element.49), channel_id=1, source_target_pairs={{0,1},{1,0},{2,3},{3,2},{4,5},{5,4},{6,7},{7,6},{8,9},{9,8},{10,11... | collective-permute-start | bytes 393224 | tf_op jit(solution)/shard_map/ppermute | solution.py:28
  49.5 0.0 collective-permute-done.17.refs_3_
  49.5 0.2 collective-permute-start.10
  49.7 0.0 collective-permute-done.18.refs_4_
  49.7 0.0 collective-permute-start.9
  49.7 1.2 %collective-permute-done.19.refs_5_ = bf16[256,512]{1,0:T(8,128)(2,1)S(1)} collective-permute-done((bf16[256,512]{1,0:T(8,128)(2,1)S(1)}, bf16[256,512]{1,0:T(8,128)(2,1)S(1)}, u32[]{:S(2)}, u32[]{:S(2)}) %collective-permute-start.19) | collective-permute-done | bytes 262176 | tf_op jit(solution)/shard_map/ppermute | solution.py:45
  50.9 0.0 collective-permute-done.16.refs_1_
  50.9 2.1 %weight_pass.1 = bf16[512,512]{1,0:T(8,128)(2,1)} custom-call(bf16[4,128,512]{2,1,0:T(8,128)(2,1)S(1)} %stack.17.refs_0_, bf16[4,128,512]{2,1,0:T(8,128)(2,1)S(1)} %collective-permute-done.16.refs_1_, bf16[256,512]{1,0:T(8,128)(2,1)S(1)} %add_convert_fusion.1.refs_2_, bf16[256,512]{1,0:T(8,128)(2,1)S(1)} %collective-permute-done.17.refs_3_, ...), custom_call_target="tpu_custom_call" | custom-call | flops 536870912 | bytes 4194304 | tf_op jit(solution)/shard_map/weight_pass/pallas_call | solution.py:279
  53.0 27.4 %all-to-all-start = ((bf16[64,8,512]{2,1,0:T(8,128)(2,1)}), bf16[64,8,512]{2,1,0:T(8,128)(2,1)S(1)}, u32[]{:S(2)}, u32[]{:S(2)}) async-start(bf16[64,8,512]{2,1,0:T(8,128)(2,1)} %bitcast.3), calls=%async_computation | async-start | bytes 1048576 | tf_op jit(solution)/shard_map/all_to_all | solution.py:351
  80.4 0.5 collective-permute-start.12
  80.9 0.0 collective-permute-done.10
  80.9 0.0 collective-permute-done.9
  80.9 0.1 add_convert_fusion
  81.0 0.2 collective-permute-start.11
  81.2 0.0 collective-permute-done.8
  81.2 0.8 maximum_select_fusion
  82.0 0.0 collective-permute-done.12
  82.0 0.8 maximum_select_fusion.2
  82.8 0.0 collective-permute-done.11
  82.8 0.8 maximum_select_fusion.1
  83.6 13.9 %all-to-all-done = bf16[64,8,512]{2,1,0:T(8,128)(2,1)S(1)} async-done(((bf16[64,8,512]{2,1,0:T(8,128)(2,1)}), bf16[64,8,512]{2,1,0:T(8,128)(2,1)S(1)}, u32[]{:S(2)}, u32[]{:S(2)}) %all-to-all-start) | async-done | bytes 524320 | tf_op jit(solution)/shard_map/all_to_all | solution.py:351
  97.5 0.1 convert_reduce_fusion
  97.6 0.6 broadcast_multiply_fusion
  (4 shorter events, 0.1 us)
Async XLA Ops:
  2.6 9.0 %collective-permute-start = (bf16[3,128,512]{2,1,0:T(8,128)(2,1)S(1)}, bf16[3,128,512]{2,1,0:T(8,128)(2,1)S(1)}, u32[]{:S(2)}, u32[]{:S(2)}) collective-permute-start(bf16[3,128,512]{2,1,0:T(8,128)(2,1)S(1)} %get-tuple-element.37), channel_id=1, source_target_pairs={{0,1},{1,0},{2,3},{3,2},{4,5},{5,4},{6,7},{7,6},{8,9},{9,8},{10,11... | collective-permute-start | bytes 1179656 | tf_op jit(solution)/shard_map/ppermute | solution.py:28
  3.4 1.5 %collective-permute-start.1 = (bf16[128,512]{1,0:T(8,128)(2,1)S(1)}, bf16[128,512]{1,0:T(8,128)(2,1)S(1)}, u32[]{:S(2)}, u32[]{:S(2)}) collective-permute-start(bf16[128,512]{1,0:T(8,128)(2,1)S(1)} %get-tuple-element.41), channel_id=1, source_target_pairs={{0,1},{1,0},{2,3},{3,2},{4,5},{5,4},{6,7},{7,6},{8,9},{9,8},{10,11... | collective-permute-start | bytes 393224 | tf_op jit(solution)/shard_map/ppermute | solution.py:28
  4.9 7.9 %collective-permute-start.2 = (bf16[256,512]{1,0:T(8,128)(2,1)S(1)}, bf16[256,512]{1,0:T(8,128)(2,1)S(1)}, u32[]{:S(2)}, u32[]{:S(2)}) collective-permute-start(bf16[256,512]{1,0:T(8,128)(2,1)S(1)} %join.3.refs_4_), channel_id=1, source_target_pairs={{0,2},{1,3},{2,0},{3,1},{4,6},{5,7},{6,4},{7,5},{8,10},{9,11},{10,... | collective-permute-start | bytes 786440 | tf_op jit(solution)/shard_map/ppermute | solution.py:38
  6.7 11.0 %collective-permute-start.3 = (bf16[256,512]{1,0:T(8,128)(2,1)S(1)}, bf16[256,512]{1,0:T(8,128)(2,1)S(1)}, u32[]{:S(2)}, u32[]{:S(2)}) collective-permute-start(bf16[256,512]{1,0:T(8,128)(2,1)S(1)} %join.3.refs_4_), channel_id=1, source_target_pairs={{0,254},{1,255},{2,4},{3,5},{4,2},{5,3},{6,8},{7,9},{8,6},{9,7},{1... | collective-permute-start | bytes 786440 | tf_op jit(solution)/shard_map/ppermute | solution.py:38
  17.6 5.7 %copy-start = (bf16[128,2048]{1,0:T(8,128)(2,1)S(1)}, bf16[128,2048]{1,0:T(8,128)(2,1)}, u32[]{:S(2)}) copy-start(bf16[128,2048]{1,0:T(8,128)(2,1)} %refs_1_) | copy-start | bytes 1572868
  19.9 8.8 %collective-permute-start.5 = (bf16[256,512]{1,0:T(8,128)(2,1)S(1)}, bf16[256,512]{1,0:T(8,128)(2,1)S(1)}, u32[]{:S(2)}, u32[]{:S(2)}) collective-permute-start(bf16[256,512]{1,0:T(8,128)(2,1)S(1)} %get-tuple-element.44), channel_id=1, source_target_pairs={{0,254},{1,255},{2,4},{3,5},{4,2},{5,3},{6,8},{7,9},{8,6},{9,7},{1... | collective-permute-start | bytes 786440 | tf_op jit(solution)/shard_map/ppermute | solution.py:38
  23.3 6.1 %collective-permute-start.4 = (bf16[256,512]{1,0:T(8,128)(2,1)S(1)}, bf16[256,512]{1,0:T(8,128)(2,1)S(1)}, u32[]{:S(2)}, u32[]{:S(2)}) collective-permute-start(bf16[256,512]{1,0:T(8,128)(2,1)S(1)} %get-tuple-element.43), channel_id=1, source_target_pairs={{0,2},{1,3},{2,0},{3,1},{4,6},{5,7},{6,4},{7,5},{8,10},{9,11},{10,... | collective-permute-start | bytes 786440 | tf_op jit(solution)/shard_map/ppermute | solution.py:38
  23.9 5.6 %collective-permute-start.13 = (bf16[128,512]{1,0:T(8,128)(2,1)S(1)}, bf16[128,512]{1,0:T(8,128)(2,1)S(1)}, u32[]{:S(2)}, u32[]{:S(2)}) collective-permute-start(bf16[128,512]{1,0:T(8,128)(2,1)S(1)} %get-tuple-element.55), channel_id=1, source_target_pairs={{0,64},{1,65},{2,66},{3,67},{4,68},{5,69},{6,70},{7,71},{8,72},{9,... | collective-permute-start | bytes 393224 | tf_op jit(solution)/shard_map/ppermute | solution.py:45
  24.0 5.7 %collective-permute-start.14 = (bf16[128,512]{1,0:T(8,128)(2,1)S(1)}, bf16[128,512]{1,0:T(8,128)(2,1)S(1)}, u32[]{:S(2)}, u32[]{:S(2)}) collective-permute-start(bf16[128,512]{1,0:T(8,128)(2,1)S(1)} %get-tuple-element.56), channel_id=1, source_target_pairs={{0,128},{1,129},{2,130},{3,131},{4,132},{5,133},{6,134},{7,135},{8... | collective-permute-start | bytes 393224 | tf_op jit(solution)/shard_map/ppermute | solution.py:45
  26.2 6.2 %collective-permute-start.15 = (bf16[128,512]{1,0:T(8,128)(2,1)S(1)}, bf16[128,512]{1,0:T(8,128)(2,1)S(1)}, u32[]{:S(2)}, u32[]{:S(2)}) collective-permute-start(bf16[128,512]{1,0:T(8,128)(2,1)S(1)} %get-tuple-element.57), channel_id=1, source_target_pairs={{0,192},{1,193},{2,194},{3,195},{4,196},{5,197},{6,198},{7,199},{8... | collective-permute-start | bytes 393224 | tf_op jit(solution)/shard_map/ppermute | solution.py:45
  28.8 8.4 %collective-permute-start.6 = (bf16[256,512]{1,0:T(8,128)(2,1)S(1)}, bf16[256,512]{1,0:T(8,128)(2,1)S(1)}, u32[]{:S(2)}, u32[]{:S(2)}) collective-permute-start(bf16[256,512]{1,0:T(8,128)(2,1)S(1)} %get-tuple-element.46.refs_7_), channel_id=1, source_target_pairs={{0,2},{1,3},{2,0},{3,1},{4,6},{5,7},{6,4},{7,5},{8,10},{9,11},{10,... | collective-permute-start | bytes 786440 | tf_op jit(solution)/shard_map/ppermute | solution.py:38
  32.5 18.4 %collective-permute-start.16 = (bf16[4,128,512]{2,1,0:T(8,128)(2,1)S(1)}, bf16[4,128,512]{2,1,0:T(8,128)(2,1)S(1)}, u32[]{:S(2)}, u32[]{:S(2)}) collective-permute-start(bf16[4,128,512]{2,1,0:T(8,128)(2,1)S(1)} %stack.17.refs_0_), channel_id=1, source_target_pairs={{0,1},{1,0},{2,3},{3,2},{4,5},{5,4},{6,7},{7,6},{8,9},{9,8},{10,11... | collective-permute-start | bytes 1572872 | tf_op jit(solution)/shard_map/ppermute | solution.py:28
  35.0 9.9 %collective-permute-start.7 = (bf16[256,512]{1,0:T(8,128)(2,1)S(1)}, bf16[256,512]{1,0:T(8,128)(2,1)S(1)}, u32[]{:S(2)}, u32[]{:S(2)}) collective-permute-start(bf16[256,512]{1,0:T(8,128)(2,1)S(1)} %get-tuple-element.46.refs_7_), channel_id=1, source_target_pairs={{0,254},{1,255},{2,4},{3,5},{4,2},{5,3},{6,8},{7,9},{8,6},{9,7},{1... | collective-permute-start | bytes 786440 | tf_op jit(solution)/shard_map/ppermute | solution.py:38
  35.2 14.4 %collective-permute-start.17 = (bf16[256,512]{1,0:T(8,128)(2,1)S(1)}, bf16[256,512]{1,0:T(8,128)(2,1)S(1)}, u32[]{:S(2)}, u32[]{:S(2)}) collective-permute-start(bf16[256,512]{1,0:T(8,128)(2,1)S(1)} %add_convert_fusion.1.refs_2_), channel_id=1, source_target_pairs={{0,64},{1,65},{2,66},{3,67},{4,68},{5,69},{6,70},{7,71},{8,72},{9,... | collective-permute-start | bytes 786440 | tf_op jit(solution)/shard_map/ppermute | solution.py:45
  35.6 14.1 %collective-permute-start.18 = (bf16[256,512]{1,0:T(8,128)(2,1)S(1)}, bf16[256,512]{1,0:T(8,128)(2,1)S(1)}, u32[]{:S(2)}, u32[]{:S(2)}) collective-permute-start(bf16[256,512]{1,0:T(8,128)(2,1)S(1)} %add_convert_fusion.1.refs_2_), channel_id=1, source_target_pairs={{0,128},{1,129},{2,130},{3,131},{4,132},{5,133},{6,134},{7,135},{8... | collective-permute-start | bytes 786440 | tf_op jit(solution)/shard_map/ppermute | solution.py:45
  37.2 13.7 %collective-permute-start.19 = (bf16[256,512]{1,0:T(8,128)(2,1)S(1)}, bf16[256,512]{1,0:T(8,128)(2,1)S(1)}, u32[]{:S(2)}, u32[]{:S(2)}) collective-permute-start(bf16[256,512]{1,0:T(8,128)(2,1)S(1)} %add_convert_fusion.1.refs_2_), channel_id=1, source_target_pairs={{0,192},{1,193},{2,194},{3,195},{4,196},{5,197},{6,198},{7,199},{8... | collective-permute-start | bytes 786440 | tf_op jit(solution)/shard_map/ppermute | solution.py:45
  48.5 32.8 %collective-permute-start.8 = (bf16[128,512]{1,0:T(8,128)(2,1)S(1)}, bf16[128,512]{1,0:T(8,128)(2,1)S(1)}, u32[]{:S(2)}, u32[]{:S(2)}) collective-permute-start(bf16[128,512]{1,0:T(8,128)(2,1)S(1)} %get-tuple-element.49), channel_id=1, source_target_pairs={{0,1},{1,0},{2,3},{3,2},{4,5},{5,4},{6,7},{7,6},{8,9},{9,8},{10,11... | collective-permute-start | bytes 393224 | tf_op jit(solution)/shard_map/ppermute | solution.py:28
  49.5 31.4 %collective-permute-start.10 = (bf16[256,512]{1,0:T(8,128)(2,1)S(1)}, bf16[256,512]{1,0:T(8,128)(2,1)S(1)}, u32[]{:S(2)}, u32[]{:S(2)}) collective-permute-start(bf16[256,512]{1,0:T(8,128)(2,1)S(1)} %get-tuple-element.52), channel_id=1, source_target_pairs={{0,254},{1,255},{2,4},{3,5},{4,2},{5,3},{6,8},{7,9},{8,6},{9,7},{1... | collective-permute-start | bytes 786440 | tf_op jit(solution)/shard_map/ppermute | solution.py:38
  49.7 31.2 %collective-permute-start.9 = (bf16[256,512]{1,0:T(8,128)(2,1)S(1)}, bf16[256,512]{1,0:T(8,128)(2,1)S(1)}, u32[]{:S(2)}, u32[]{:S(2)}) collective-permute-start(bf16[256,512]{1,0:T(8,128)(2,1)S(1)} %get-tuple-element.51), channel_id=1, source_target_pairs={{0,2},{1,3},{2,0},{3,1},{4,6},{5,7},{6,4},{7,5},{8,10},{9,11},{10,... | collective-permute-start | bytes 786440 | tf_op jit(solution)/shard_map/ppermute | solution.py:38
  53.0 44.5 %all-to-all-start = ((bf16[64,8,512]{2,1,0:T(8,128)(2,1)}), bf16[64,8,512]{2,1,0:T(8,128)(2,1)S(1)}, u32[]{:S(2)}, u32[]{:S(2)}) async-start(bf16[64,8,512]{2,1,0:T(8,128)(2,1)} %bitcast.3), calls=%async_computation | async-start | bytes 1048576 | tf_op jit(solution)/shard_map/all_to_all | solution.py:351
  80.4 1.6 %collective-permute-start.12 = (bf16[128,512]{1,0:T(8,128)(2,1)S(1)}, bf16[128,512]{1,0:T(8,128)(2,1)S(1)}, u32[]{:S(2)}, u32[]{:S(2)}) collective-permute-start(bf16[128,512]{1,0:T(8,128)(2,1)S(1)} %get-tuple-element.63), channel_id=1, source_target_pairs={{0,1},{1,0},{2,3},{3,2},{4,5},{5,4},{6,7},{7,6},{8,9},{9,8},{10,11... | collective-permute-start | bytes 393224 | tf_op jit(solution)/shard_map/ppermute | solution.py:28
  81.0 1.8 %collective-permute-start.11 = (bf16[128,512]{1,0:T(8,128)(2,1)S(1)}, bf16[128,512]{1,0:T(8,128)(2,1)S(1)}, u32[]{:S(2)}, u32[]{:S(2)}) collective-permute-start(bf16[128,512]{1,0:T(8,128)(2,1)S(1)} %get-tuple-element.65), channel_id=1, source_target_pairs={{0,1},{1,0},{2,3},{3,2},{4,5},{5,4},{6,7},{7,6},{8,9},{9,8},{10,11... | collective-permute-start | bytes 393224 | tf_op jit(solution)/shard_map/ppermute | solution.py:28

commit v3 on v2

--- a/solution.py
+++ b/solution.py
@@ -57,7 +57,7 @@
     half = query.shape[1] // 2
     here = pl.multiple_of(core[0] * half, half)
     there = pl.multiple_of((1 - core[0]) * half, half)
-    moves = [(key, key_other, there), (key, key_mine, here)]
+    moves = [(key, key_other.at[0], there), (key, key_mine.at[0], here)]
     for at, source in enumerate((query, grad, value)):
         moves += [(source, other.at[at], there), (source, mine.at[at], here)]
     copies = [
@@ -72,8 +72,9 @@
 
 def pack(core, key, query, grad, value):
     rows, features = query.shape
-    one = jax.ShapeDtypeStruct((rows, features // 2), query.dtype)
-    three = jax.ShapeDtypeStruct((3, rows, features // 2), query.dtype)
+    one, three = (
+        jax.ShapeDtypeStruct((count, rows, features // 2), query.dtype) for count in (1, 3)
+    )
     return pl.pallas_call(
         pack_kernel,
         out_shape=(one, one, three, three),
@@ -89,18 +90,18 @@
     return pltpu.with_memory_space_constraint(array, pltpu.HBM)
 
 
-def join_kernel(count, mine, part, *targets):
-    rows = mine.shape[-2]
+def join_kernel(mine, part, *targets):
+    rows = mine.shape[1]
     for at, target in enumerate(targets):
-        target[:rows] = mine[at] if count > 1 else mine[...]
-        target[rows:] = part[at] if count > 1 else part[...]
-
-
-def join(mine, part, count):
-    rows, half = mine.shape[-2:]
+        target[:rows] = mine[at]
+        target[rows:] = part[at]
+
+
+def join(mine, part):
+    count, rows, half = mine.shape
     two = jax.ShapeDtypeStruct((2 * rows, half), mine.dtype)
     return pl.pallas_call(
-        lambda *refs: join_kernel(count, *refs),
+        join_kernel,
         out_shape=(two,) * count,
         in_specs=vmem(2),
         out_specs=tuple(vmem(count)),
@@ -110,19 +111,14 @@
 
 
 def window_bias(place, tokens):
-    even_core, even_chip = place[0] == 0, place[1] == 0
     left = lax.broadcasted_iota(jnp.int32, (1, 2 * tokens), 1) < tokens
-    right = jnp.logical_not(left)
-
-    def bias(core_even, chip_even, columns):
-        hit = jnp.logical_and(even_core == core_even, even_chip == chip_even)
-        return jnp.where(jnp.logical_and(hit, columns), NEG, 0.0)
-
+    unlike = jnp.where(place[0] == place[1], 0.0, NEG)
+    alike = jnp.where(place[0] == place[1], NEG, 0.0)
     return {
-        0: bias(True, False, right) + bias(False, True, right),
-        1: bias(True, True, left) + bias(False, False, left),
-        4: bias(True, True, right) + bias(False, False, right),
-        5: bias(True, False, left) + bias(False, True, left),
+        0: jnp.where(left, 0.0, unlike),
+        1: jnp.where(left, alike, 0.0),
+        4: jnp.where(left, 0.0, alike),
+        5: jnp.where(left, unlike, 0.0),
     }
 
 
@@ -256,37 +252,55 @@
     )(*blocks)
 
 
-def weight_kernel(count, own, part, *refs):
-    gathered, out = refs[:count], refs[count]
-    rows = own.shape[1]
+def merge_kernel(own, part, out):
+    count, rows, _ = own.shape
+    for step in range(count):
+        at = 2 * step * rows
+        out[:, at : at + rows] = own[step].T
+        out[:, at + rows : at + 2 * rows] = part[step].T
+
+
+def merge(own, part):
+    count, rows, width = own.shape
+    return pl.pallas_call(
+        merge_kernel,
+        out_shape=jax.ShapeDtypeStruct((width, 2 * count * rows), own.dtype),
+        in_specs=vmem(2),
+        out_specs=pl.BlockSpec(memory_space=pltpu.VMEM),
+        compiler_params=ROOM,
+        name="merge",
+    )(own, part)
+
+
+def weight_kernel(inputs, *refs):
+    gathered, out = refs[:-1], refs[-1]
+    rows = gathered[0].shape[0]
     tile = 256
     for low in range(0, out.shape[0], tile):
         total = jnp.zeros((tile, out.shape[1]), jnp.float32)
-        for step in range(count):
-            for held, start in ((own, 0), (part, rows)):
-                total += lax.dot_general(
-                    held[step, :, low : low + tile],
-                    gathered[step][start : start + rows],
-                    FIRST,
-                    preferred_element_type=jnp.float32,
-                )
+        for step, grads in enumerate(gathered):
+            total += jnp.dot(
+                inputs[low : low + tile, step * rows : (step + 1) * rows],
+                grads[...],
+                preferred_element_type=jnp.float32,
+            )
         out[low : low + tile] = total.astype(jnp.bfloat16)
 
 
-def weight_pass(own, part, gathered):
-    count, rows, width = own.shape
+def weight_pass(inputs, gathered):
+    width, tokens = inputs.shape
     columns = gathered[0].shape[1]
     return pl.pallas_call(
-        lambda *refs: weight_kernel(count, *refs),
+        weight_kernel,
         out_shape=jax.ShapeDtypeStruct((width, columns), jnp.bfloat16),
-        in_specs=vmem(2 + count),
+        in_specs=vmem(1 + len(gathered)),
         out_specs=pl.BlockSpec(memory_space=pltpu.VMEM),
         cost_estimate=pl.CostEstimate(
-            flops=4 * count * rows * width * columns, transcendentals=0, bytes_accessed=4 << 20
+            flops=2 * tokens * width * columns, transcendentals=0, bytes_accessed=4 << 20
         ),
         compiler_params=ROOM,
         name="weight_pass",
-    )(own, part, *gathered)
+    )(inputs, *gathered)
 
 
 def steps(query_rows, key_rows, value_rows, out_grad, inputs):
@@ -314,10 +328,11 @@
     key_mine, key_other, mine, other = pack(place, key_rows, query_rows, out_grad, value_rows)
     key_part = to_core(key_other, devices)
     part = to_core(other, devices)
-    (key,) = join(key_mine, key_part, 1)
+    (key,) = join(key_mine, key_part)
     first_k, second_k = swaps(key, key)
     keys = (first_k, key, second_k)
-    query, grad, value = join(mine, part, 3)
+    query, grad, value = join(mine, part)
+    first_v, second_v = swaps(value, value)
 
     inputs, _ = lax.optimization_barrier((inputs, mine))
     blocks = input_blocks(place, inputs, ny)
@@ -330,19 +345,18 @@
     value_half = (own + from_first.astype(jnp.float32) + from_second.astype(jnp.float32)).astype(
         jnp.bfloat16
     )
-    first_v, second_v = swaps(value, value)
-    query, _ = lax.optimization_barrier((query, value_half))
+    *taken, query, _ = lax.optimization_barrier((*taken, query, value_half))
     dq, dq_other, key_first, key_own, key_second = score_pass(
         place, query, grad, keys, (first_v, value, second_v), lse, scale
     )
-    *taken, _ = lax.optimization_barrier((*taken, value_half))
+    key_from_first, key_from_second = swaps(key_first, key_second)
     taken = stack(taken)
     taken_part = to_core(taken, devices)
+    taken = merge(taken, taken_part)
     gathered = [value_half]
     for step in range(1, ny):
         gathered.append(along_y(value_half, sizes, step))
-    partial = weight_pass(taken, taken_part, gathered)
-    key_from_first, key_from_second = swaps(key_first, key_second)
+    partial = weight_pass(taken, gathered)
     value_back = to_core(value_half[rows:], devices)
     query_back = to_core(dq_other, devices)
     half = features // 2

time: 98.4 us -> 97.5 us (level)
  the two profiles are of different devices: /device:TPU:31 before, /device:TPU:1 now
where the time goes in v3:
time: 97.5 us; the launch traced here: 97.3 us
  starting transfers between devices  42.1 us (43%)
  waiting for transfers between devices  40.6 us (42%)
  Pallas kernels  10.4 us (11%)
  other arithmetic  3.36 us (3%)
    ppermute x8, starting transfers between devices, swap(): return lax.ppermute(array, AXES, pairs)  25.9 us
    ppermute x8, waiting for transfers between devices, swap(): return lax.ppermute(array, AXES, pairs)  18.3 us
    all_to_all x1, waiting for transfers between devices, steps(): arrived = lax.all_to_all(pieces, ('x', 'z', 'c'), 0, 0, tiled=True)  14 us
    ppermute x6, waiting for transfers between devices, along_y(): return lax.ppermute(array, AXES, pairs)  7.37 us
    ppermute x6, starting transfers between devices, to_core(): lax.ppermute(array, AXES, [(device, device ^ 1) for device in range(count)])  6.37 us
    all_to_all x1, starting transfers between devices, steps(): arrived = lax.all_to_all(pieces, ('x', 'z', 'c'), 0, 0, tiled=True)  5.58 us
    ppermute x6, starting transfers between devices, along_y(): return lax.ppermute(array, AXES, pairs)  4.29 us
    pallas_call x1, Pallas kernels, score_pass(): pl.pallas_call(lambda *refs: score_kernel(scale, *refs), out_shape=(part,...  3.63 us
  transfers between devices with their start and end apart: 21, of which 7 were waited for; matrix products, arithmetic and copies ran while one was open for 3% of the time, Pallas kernels for 6%

profile of v3, /device:TPU:1, one launch (start us, length us, event | category | flops | bytes accessed | tf_op | source)
XLA Modules:
  0.0 97.3 jit_solution(4646827374211219434)
XLA Ops:
  0.6 0.1 pad_add_fusion.core.refs_0_
  0.7 1.9 %pack.1 = (bf16[1,128,512]{2,1,0:T(8,128)(2,1)S(1)}, bf16[1,128,512]{2,1,0:T(8,128)(2,1)S(1)}, bf16[3,128,512]{2,1,0:T(8,128)(2,1)S(1)}, bf16[3,128,512]{2,1,0:T(8,128)(2,1)S(1)}) custom-call(s32[3]{0:T(128)S(1)} %pad_add_fusion.core.refs_0_, bf16[128,1024]{1,0:T(8,128)(2,1)} %key.1, bf16[128,1024]{1,0:T(8,128)(2,1)} %query, bf16[128,1024]{1,0:T(8,128)(2,1)} %grad.1, ...), custom_call_target="tpu_custom_call" | custom-call | tf_op jit(solution)/shard_map/pack/pallas_call | solution.py:78
  2.6 3.3 %collective-permute-start.4 = (bf16[1,128,512]{2,1,0:T(8,128)(2,1)S(1)}, bf16[1,128,512]{2,1,0:T(8,128)(2,1)S(1)}, u32[]{:S(2)}, u32[]{:S(2)}) collective-permute-start(bf16[1,128,512]{2,1,0:T(8,128)(2,1)S(1)} %get-tuple-element.46), channel_id=1, source_target_pairs={{0,1},{1,0},{2,3},{3,2},{4,5},{5,4},{6,7},{7,6},{8,9},{9,8},{10,11... | collective-permute-start | bytes 393224 | tf_op jit(solution)/shard_map/ppermute | solution.py:28
  5.9 0.1 collective-permute-start.3
  6.0 0.9 collective-permute-done.4.part
  6.9 8.6 %collective-permute-start.6 = (bf16[256,512]{1,0:T(8,128)(2,1)S(1)}, bf16[256,512]{1,0:T(8,128)(2,1)S(1)}, u32[]{:S(2)}, u32[]{:S(2)}) collective-permute-start(bf16[256,512]{1,0:T(8,128)(2,1)S(1)} %join.3.refs_4_), channel_id=1, source_target_pairs={{0,254},{1,255},{2,4},{3,5},{4,2},{5,3},{6,8},{7,9},{8,6},{9,7},{1... | collective-permute-start | bytes 786440 | tf_op jit(solution)/shard_map/ppermute | solution.py:38
  15.5 0.0 collective-permute-start.5
  15.5 0.0 collective-permute-done.3.part
  15.5 0.1 join.2
  15.6 6.3 %collective-permute-done.6.refs_5_ = bf16[256,512]{1,0:T(8,128)(2,1)S(1)} collective-permute-done((bf16[256,512]{1,0:T(8,128)(2,1)S(1)}, bf16[256,512]{1,0:T(8,128)(2,1)S(1)}, u32[]{:S(2)}, u32[]{:S(2)}) %collective-permute-start.6) | collective-permute-done | bytes 262176 | tf_op jit(solution)/shard_map/ppermute | solution.py:38
  21.8 0.9 collective-permute-done.5.refs_3_
  22.7 0.0 copy-start
  22.7 2.3 %value_pass.1 = (bf16[256,512]{1,0:T(8,128)(2,1)S(1)}, f32[256,512]{1,0:T(8,128)S(1)}, bf16[256,512]{1,0:T(8,128)(2,1)S(1)}, f32[4,8,256]{2,1,0:T(8,128)S(1)}) custom-call(s32[3]{0:T(128)S(1)} %pad_add_fusion.core.refs_0_, bf16[256,512]{1,0:T(8,128)(2,1)S(1)} %get-tuple-element.50.refs_1_, bf16[256,512]{1,0:T(8,128)(2,1)S(1)} %get-tuple-element.44.refs_2_, ...), custom_call_target="tpu_custom_call" | custom-call | flops 402653184 | bytes 4194304 | tf_op jit(solution)/shard_map/value_pass/pallas_call | solution.py:185
  25.0 0.4 collective-permute-start.7
  25.4 5.5 %collective-permute-start.8 = (bf16[256,512]{1,0:T(8,128)(2,1)S(1)}, bf16[256,512]{1,0:T(8,128)(2,1)S(1)}, u32[]{:S(2)}, u32[]{:S(2)}) collective-permute-start(bf16[256,512]{1,0:T(8,128)(2,1)S(1)} %get-tuple-element.49), channel_id=1, source_target_pairs={{0,254},{1,255},{2,4},{3,5},{4,2},{5,3},{6,8},{7,9},{8,6},{9,7},{1... | collective-permute-start | bytes 786440 | tf_op jit(solution)/shard_map/ppermute | solution.py:38
  30.9 0.0 copy-done
  30.9 0.6 input_blocks.1
  31.5 0.1 collective-permute-start
  31.6 0.4 collective-permute-start.1
  32.0 2.2 %collective-permute-start.2 = (bf16[128,512]{1,0:T(8,128)(2,1)S(1)}, bf16[128,512]{1,0:T(8,128)(2,1)S(1)}, u32[]{:S(2)}, u32[]{:S(2)}) collective-permute-start(bf16[128,512]{1,0:T(8,128)(2,1)S(1)} %get-tuple-element.41), channel_id=1, source_target_pairs={{0,192},{1,193},{2,194},{3,195},{4,196},{5,197},{6,198},{7,199},{8... | collective-permute-start | bytes 393224 | tf_op jit(solution)/shard_map/ppermute | solution.py:45
  34.3 0.0 collective-permute-done.7
  34.3 2.9 %collective-permute-done.8 = bf16[256,512]{1,0:T(8,128)(2,1)S(1)} collective-permute-done((bf16[256,512]{1,0:T(8,128)(2,1)S(1)}, bf16[256,512]{1,0:T(8,128)(2,1)S(1)}, u32[]{:S(2)}, u32[]{:S(2)}) %collective-permute-start.8) | collective-permute-done | bytes 262176 | tf_op jit(solution)/shard_map/ppermute | solution.py:38
  37.2 0.1 add_convert_fusion.1.refs_0_
  37.3 7.4 %collective-permute-done.refs_1_ = bf16[128,512]{1,0:T(8,128)(2,1)S(1)} collective-permute-done((bf16[128,512]{1,0:T(8,128)(2,1)S(1)}, bf16[128,512]{1,0:T(8,128)(2,1)S(1)}, u32[]{:S(2)}, u32[]{:S(2)}) %collective-permute-start) | collective-permute-done | bytes 131104 | tf_op jit(solution)/shard_map/ppermute | solution.py:45
  44.7 0.0 collective-permute-done.1.refs_2_
  44.7 0.0 collective-permute-done.2.refs_3_
  44.7 0.6 collective-permute-start.16
  45.3 4.4 %collective-permute-start.10 = (bf16[256,512]{1,0:T(8,128)(2,1)S(1)}, bf16[256,512]{1,0:T(8,128)(2,1)S(1)}, u32[]{:S(2)}, u32[]{:S(2)}) collective-permute-start(bf16[256,512]{1,0:T(8,128)(2,1)S(1)} %get-tuple-element.51.refs_7_), channel_id=1, source_target_pairs={{0,254},{1,255},{2,4},{3,5},{4,2},{5,3},{6,8},{7,9},{8,6},{9,7},{1... | collective-permute-start | bytes 786440 | tf_op jit(solution)/shard_map/ppermute | solution.py:38
  49.7 0.0 collective-permute-start.9
  49.8 0.0 collective-permute-start.19
  49.8 1.5 %collective-permute-start.18 = (bf16[256,512]{1,0:T(8,128)(2,1)S(1)}, bf16[256,512]{1,0:T(8,128)(2,1)S(1)}, u32[]{:S(2)}, u32[]{:S(2)}) collective-permute-start(bf16[256,512]{1,0:T(8,128)(2,1)S(1)} %add_convert_fusion.1.refs_0_), channel_id=1, source_target_pairs={{0,128},{1,129},{2,130},{3,131},{4,132},{5,133},{6,134},{7,135},{8... | collective-permute-start | bytes 786440 | tf_op jit(solution)/shard_map/ppermute | solution.py:45
  51.3 8.2 %collective-permute-done.10.refs_8_ = bf16[256,512]{1,0:T(8,128)(2,1)S(1)} collective-permute-done((bf16[256,512]{1,0:T(8,128)(2,1)S(1)}, bf16[256,512]{1,0:T(8,128)(2,1)S(1)}, u32[]{:S(2)}, u32[]{:S(2)}) %collective-permute-start.10) | collective-permute-done | bytes 262176 | tf_op jit(solution)/shard_map/ppermute | solution.py:38
  59.5 0.0 collective-permute-start.17
  59.5 0.0 collective-permute-done.9.refs_6_
  59.5 3.6 %score_pass.1 = (bf16[128,512]{1,0:T(8,128)(2,1)S(1)}, bf16[128,512]{1,0:T(8,128)(2,1)S(1)}, bf16[256,512]{1,0:T(8,128)(2,1)S(1)}, f32[256,512]{1,0:T(8,128)S(1)}, bf16[256,512]{1,0:T(8,128)(2,1)S(1)}) custom-call(s32[3]{0:T(128)S(1)} %pad_add_fusion.core.refs_0_, bf16[256,512]{1,0:T(8,128)(2,1)S(1)} %get-tuple-element.50.refs_1_, ...), custom_call_target="tpu_custom_call" | custom-call | flops 805306368 | bytes 6291456 | tf_op jit(solution)/shard_map/score_pass/pallas_call | solution.py:205
  63.2 1.6 %collective-permute-start.11 = (bf16[128,512]{1,0:T(8,128)(2,1)S(1)}, bf16[128,512]{1,0:T(8,128)(2,1)S(1)}, u32[]{:S(2)}, u32[]{:S(2)}) collective-permute-start(bf16[128,512]{1,0:T(8,128)(2,1)S(1)} %get-tuple-element.54), channel_id=1, source_target_pairs={{0,1},{1,0},{2,3},{3,2},{4,5},{5,4},{6,7},{7,6},{8,9},{9,8},{10,11... | collective-permute-start | bytes 393224 | tf_op jit(solution)/shard_map/ppermute | solution.py:28
  64.8 0.0 collective-permute-done.16.part
  64.8 0.0 collective-permute-start.12
  64.8 0.4 merge.1.inputs
  65.2 0.0 collective-permute-done.19.refs_3_
  65.2 6.9 %collective-permute-start.13 = (bf16[256,512]{1,0:T(8,128)(2,1)S(1)}, bf16[256,512]{1,0:T(8,128)(2,1)S(1)}, u32[]{:S(2)}, u32[]{:S(2)}) collective-permute-start(bf16[256,512]{1,0:T(8,128)(2,1)S(1)} %get-tuple-element.57), channel_id=1, source_target_pairs={{0,254},{1,255},{2,4},{3,5},{4,2},{5,3},{6,8},{7,9},{8,6},{9,7},{1... | collective-permute-start | bytes 786440 | tf_op jit(solution)/shard_map/ppermute | solution.py:38
  72.1 0.0 collective-permute-done.18.refs_2_
  72.1 0.0 collective-permute-done.17.refs_1_
  72.1 1.5 %weight_pass.1 = bf16[512,512]{1,0:T(8,128)(2,1)} custom-call(bf16[512,1024]{1,0:T(8,128)(2,1)S(1)} %merge.1.inputs, bf16[256,512]{1,0:T(8,128)(2,1)S(1)} %add_convert_fusion.1.refs_0_, bf16[256,512]{1,0:T(8,128)(2,1)S(1)} %collective-permute-done.17.refs_1_, bf16[256,512]{1,0:T(8,128)(2,1)S(1)} %collective-permute-done.18.refs_2_, ...), custom_call_target="tpu_custom_call" | custom-call | flops 536870912 | bytes 4194304 | tf_op jit(solution)/shard_map/weight_pass/pallas_call | solution.py:293
  73.7 5.6 %all-to-all-start = ((bf16[64,8,512]{2,1,0:T(8,128)(2,1)}), bf16[64,8,512]{2,1,0:T(8,128)(2,1)S(1)}, u32[]{:S(2)}, u32[]{:S(2)}) async-start(bf16[64,8,512]{2,1,0:T(8,128)(2,1)} %bitcast.3), calls=%async_computation | async-start | bytes 1048576 | tf_op jit(solution)/shard_map/all_to_all | solution.py:365
  79.3 0.7 collective-permute-start.15
  79.9 0.0 collective-permute-done.12
  79.9 0.0 collective-permute-done.13
  79.9 0.1 add_convert_fusion
  80.1 0.1 collective-permute-start.14
  80.2 0.0 collective-permute-done.11
  80.2 0.8 maximum_select_fusion
  81.0 0.0 collective-permute-done.15
  81.0 0.8 maximum_select_fusion.2
  81.8 0.0 collective-permute-done.14
  81.8 0.8 maximum_select_fusion.1
  82.6 14.0 %all-to-all-done = bf16[64,8,512]{2,1,0:T(8,128)(2,1)S(1)} async-done(((bf16[64,8,512]{2,1,0:T(8,128)(2,1)}), bf16[64,8,512]{2,1,0:T(8,128)(2,1)S(1)}, u32[]{:S(2)}, u32[]{:S(2)}) %all-to-all-start) | async-done | bytes 524320 | tf_op jit(solution)/shard_map/all_to_all | solution.py:365
  96.6 0.1 convert_reduce_fusion
  96.7 0.6 broadcast_multiply_fusion
  (4 shorter events, 0.1 us)
Async XLA Ops:
  2.6 4.3 %collective-permute-start.4 = (bf16[1,128,512]{2,1,0:T(8,128)(2,1)S(1)}, bf16[1,128,512]{2,1,0:T(8,128)(2,1)S(1)}, u32[]{:S(2)}, u32[]{:S(2)}) collective-permute-start(bf16[1,128,512]{2,1,0:T(8,128)(2,1)S(1)} %get-tuple-element.46), channel_id=1, source_target_pairs={{0,1},{1,0},{2,3},{3,2},{4,5},{5,4},{6,7},{7,6},{8,9},{9,8},{10,11... | collective-permute-start | bytes 393224 | tf_op jit(solution)/shard_map/ppermute | solution.py:28
  5.9 9.6 %collective-permute-start.3 = (bf16[3,128,512]{2,1,0:T(8,128)(2,1)S(1)}, bf16[3,128,512]{2,1,0:T(8,128)(2,1)S(1)}, u32[]{:S(2)}, u32[]{:S(2)}) collective-permute-start(bf16[3,128,512]{2,1,0:T(8,128)(2,1)S(1)} %get-tuple-element.42), channel_id=1, source_target_pairs={{0,1},{1,0},{2,3},{3,2},{4,5},{5,4},{6,7},{7,6},{8,9},{9,8},{10,11... | collective-permute-start | bytes 1179656 | tf_op jit(solution)/shard_map/ppermute | solution.py:28
  6.9 14.9 %collective-permute-start.6 = (bf16[256,512]{1,0:T(8,128)(2,1)S(1)}, bf16[256,512]{1,0:T(8,128)(2,1)S(1)}, u32[]{:S(2)}, u32[]{:S(2)}) collective-permute-start(bf16[256,512]{1,0:T(8,128)(2,1)S(1)} %join.3.refs_4_), channel_id=1, source_target_pairs={{0,254},{1,255},{2,4},{3,5},{4,2},{5,3},{6,8},{7,9},{8,6},{9,7},{1... | collective-permute-start | bytes 786440 | tf_op jit(solution)/shard_map/ppermute | solution.py:38
  15.5 7.2 %collective-permute-start.5 = (bf16[256,512]{1,0:T(8,128)(2,1)S(1)}, bf16[256,512]{1,0:T(8,128)(2,1)S(1)}, u32[]{:S(2)}, u32[]{:S(2)}) collective-permute-start(bf16[256,512]{1,0:T(8,128)(2,1)S(1)} %join.3.refs_4_), channel_id=1, source_target_pairs={{0,2},{1,3},{2,0},{3,1},{4,6},{5,7},{6,4},{7,5},{8,10},{9,11},{10,... | collective-permute-start | bytes 786440 | tf_op jit(solution)/shard_map/ppermute | solution.py:38
  22.7 8.2 %copy-start = (bf16[128,2048]{1,0:T(8,128)(2,1)S(1)}, bf16[128,2048]{1,0:T(8,128)(2,1)}, u32[]{:S(2)}) copy-start(bf16[128,2048]{1,0:T(8,128)(2,1)} %refs_1_) | copy-start | bytes 1572868
  25.0 9.3 %collective-permute-start.7 = (bf16[256,512]{1,0:T(8,128)(2,1)S(1)}, bf16[256,512]{1,0:T(8,128)(2,1)S(1)}, u32[]{:S(2)}, u32[]{:S(2)}) collective-permute-start(bf16[256,512]{1,0:T(8,128)(2,1)S(1)} %get-tuple-element.48), channel_id=1, source_target_pairs={{0,2},{1,3},{2,0},{3,1},{4,6},{5,7},{6,4},{7,5},{8,10},{9,11},{10,... | collective-permute-start | bytes 786440 | tf_op jit(solution)/shard_map/ppermute | solution.py:38
  25.4 11.8 %collective-permute-start.8 = (bf16[256,512]{1,0:T(8,128)(2,1)S(1)}, bf16[256,512]{1,0:T(8,128)(2,1)S(1)}, u32[]{:S(2)}, u32[]{:S(2)}) collective-permute-start(bf16[256,512]{1,0:T(8,128)(2,1)S(1)} %get-tuple-element.49), channel_id=1, source_target_pairs={{0,254},{1,255},{2,4},{3,5},{4,2},{5,3},{6,8},{7,9},{8,6},{9,7},{1... | collective-permute-start | bytes 786440 | tf_op jit(solution)/shard_map/ppermute | solution.py:38
  31.5 13.2 %collective-permute-start = (bf16[128,512]{1,0:T(8,128)(2,1)S(1)}, bf16[128,512]{1,0:T(8,128)(2,1)S(1)}, u32[]{:S(2)}, u32[]{:S(2)}) collective-permute-start(bf16[128,512]{1,0:T(8,128)(2,1)S(1)} %get-tuple-element.39), channel_id=1, source_target_pairs={{0,64},{1,65},{2,66},{3,67},{4,68},{5,69},{6,70},{7,71},{8,72},{9,... | collective-permute-start | bytes 393224 | tf_op jit(solution)/shard_map/ppermute | solution.py:45
  31.6 13.1 %collective-permute-start.1 = (bf16[128,512]{1,0:T(8,128)(2,1)S(1)}, bf16[128,512]{1,0:T(8,128)(2,1)S(1)}, u32[]{:S(2)}, u32[]{:S(2)}) collective-permute-start(bf16[128,512]{1,0:T(8,128)(2,1)S(1)} %get-tuple-element.40), channel_id=1, source_target_pairs={{0,128},{1,129},{2,130},{3,131},{4,132},{5,133},{6,134},{7,135},{8... | collective-permute-start | bytes 393224 | tf_op jit(solution)/shard_map/ppermute | solution.py:45
  32.0 12.6 %collective-permute-start.2 = (bf16[128,512]{1,0:T(8,128)(2,1)S(1)}, bf16[128,512]{1,0:T(8,128)(2,1)S(1)}, u32[]{:S(2)}, u32[]{:S(2)}) collective-permute-start(bf16[128,512]{1,0:T(8,128)(2,1)S(1)} %get-tuple-element.41), channel_id=1, source_target_pairs={{0,192},{1,193},{2,194},{3,195},{4,196},{5,197},{6,198},{7,199},{8... | collective-permute-start | bytes 393224 | tf_op jit(solution)/shard_map/ppermute | solution.py:45
  44.7 20.1 %collective-permute-start.16 = (bf16[4,128,512]{2,1,0:T(8,128)(2,1)S(1)}, bf16[4,128,512]{2,1,0:T(8,128)(2,1)S(1)}, u32[]{:S(2)}, u32[]{:S(2)}) collective-permute-start(bf16[4,128,512]{2,1,0:T(8,128)(2,1)S(1)} %stack.17.own), channel_id=1, source_target_pairs={{0,1},{1,0},{2,3},{3,2},{4,5},{5,4},{6,7},{7,6},{8,9},{9,8},{10,11... | collective-permute-start | bytes 1572872 | tf_op jit(solution)/shard_map/ppermute | solution.py:28
  45.3 14.2 %collective-permute-start.10 = (bf16[256,512]{1,0:T(8,128)(2,1)S(1)}, bf16[256,512]{1,0:T(8,128)(2,1)S(1)}, u32[]{:S(2)}, u32[]{:S(2)}) collective-permute-start(bf16[256,512]{1,0:T(8,128)(2,1)S(1)} %get-tuple-element.51.refs_7_), channel_id=1, source_target_pairs={{0,254},{1,255},{2,4},{3,5},{4,2},{5,3},{6,8},{7,9},{8,6},{9,7},{1... | collective-permute-start | bytes 786440 | tf_op jit(solution)/shard_map/ppermute | solution.py:38
  49.7 9.8 %collective-permute-start.9 = (bf16[256,512]{1,0:T(8,128)(2,1)S(1)}, bf16[256,512]{1,0:T(8,128)(2,1)S(1)}, u32[]{:S(2)}, u32[]{:S(2)}) collective-permute-start(bf16[256,512]{1,0:T(8,128)(2,1)S(1)} %get-tuple-element.51.refs_7_), channel_id=1, source_target_pairs={{0,2},{1,3},{2,0},{3,1},{4,6},{5,7},{6,4},{7,5},{8,10},{9,11},{10,... | collective-permute-start | bytes 786440 | tf_op jit(solution)/shard_map/ppermute | solution.py:38
  49.8 15.4 %collective-permute-start.19 = (bf16[256,512]{1,0:T(8,128)(2,1)S(1)}, bf16[256,512]{1,0:T(8,128)(2,1)S(1)}, u32[]{:S(2)}, u32[]{:S(2)}) collective-permute-start(bf16[256,512]{1,0:T(8,128)(2,1)S(1)} %add_convert_fusion.1.refs_0_), channel_id=1, source_target_pairs={{0,192},{1,193},{2,194},{3,195},{4,196},{5,197},{6,198},{7,199},{8... | collective-permute-start | bytes 786440 | tf_op jit(solution)/shard_map/ppermute | solution.py:45
  49.8 22.4 %collective-permute-start.18 = (bf16[256,512]{1,0:T(8,128)(2,1)S(1)}, bf16[256,512]{1,0:T(8,128)(2,1)S(1)}, u32[]{:S(2)}, u32[]{:S(2)}) collective-permute-start(bf16[256,512]{1,0:T(8,128)(2,1)S(1)} %add_convert_fusion.1.refs_0_), channel_id=1, source_target_pairs={{0,128},{1,129},{2,130},{3,131},{4,132},{5,133},{6,134},{7,135},{8... | collective-permute-start | bytes 786440 | tf_op jit(solution)/shard_map/ppermute | solution.py:45
  59.5 12.6 %collective-permute-start.17 = (bf16[256,512]{1,0:T(8,128)(2,1)S(1)}, bf16[256,512]{1,0:T(8,128)(2,1)S(1)}, u32[]{:S(2)}, u32[]{:S(2)}) collective-permute-start(bf16[256,512]{1,0:T(8,128)(2,1)S(1)} %add_convert_fusion.1.refs_0_), channel_id=1, source_target_pairs={{0,64},{1,65},{2,66},{3,67},{4,68},{5,69},{6,70},{7,71},{8,72},{9,... | collective-permute-start | bytes 786440 | tf_op jit(solution)/shard_map/ppermute | solution.py:45
  63.2 17.0 %collective-permute-start.11 = (bf16[128,512]{1,0:T(8,128)(2,1)S(1)}, bf16[128,512]{1,0:T(8,128)(2,1)S(1)}, u32[]{:S(2)}, u32[]{:S(2)}) collective-permute-start(bf16[128,512]{1,0:T(8,128)(2,1)S(1)} %get-tuple-element.54), channel_id=1, source_target_pairs={{0,1},{1,0},{2,3},{3,2},{4,5},{5,4},{6,7},{7,6},{8,9},{9,8},{10,11... | collective-permute-start | bytes 393224 | tf_op jit(solution)/shard_map/ppermute | solution.py:28
  64.8 15.1 %collective-permute-start.12 = (bf16[256,512]{1,0:T(8,128)(2,1)S(1)}, bf16[256,512]{1,0:T(8,128)(2,1)S(1)}, u32[]{:S(2)}, u32[]{:S(2)}) collective-permute-start(bf16[256,512]{1,0:T(8,128)(2,1)S(1)} %get-tuple-element.56), channel_id=1, source_target_pairs={{0,2},{1,3},{2,0},{3,1},{4,6},{5,7},{6,4},{7,5},{8,10},{9,11},{10,... | collective-permute-start | bytes 786440 | tf_op jit(solution)/shard_map/ppermute | solution.py:38
  65.2 14.8 %collective-permute-start.13 = (bf16[256,512]{1,0:T(8,128)(2,1)S(1)}, bf16[256,512]{1,0:T(8,128)(2,1)S(1)}, u32[]{:S(2)}, u32[]{:S(2)}) collective-permute-start(bf16[256,512]{1,0:T(8,128)(2,1)S(1)} %get-tuple-element.57), channel_id=1, source_target_pairs={{0,254},{1,255},{2,4},{3,5},{4,2},{5,3},{6,8},{7,9},{8,6},{9,7},{1... | collective-permute-start | bytes 786440 | tf_op jit(solution)/shard_map/ppermute | solution.py:38
  73.7 22.9 %all-to-all-start = ((bf16[64,8,512]{2,1,0:T(8,128)(2,1)}), bf16[64,8,512]{2,1,0:T(8,128)(2,1)S(1)}, u32[]{:S(2)}, u32[]{:S(2)}) async-start(bf16[64,8,512]{2,1,0:T(8,128)(2,1)} %bitcast.3), calls=%async_computation | async-start | bytes 1048576 | tf_op jit(solution)/shard_map/all_to_all | solution.py:365
  79.3 1.7 %collective-permute-start.15 = (bf16[128,512]{1,0:T(8,128)(2,1)S(1)}, bf16[128,512]{1,0:T(8,128)(2,1)S(1)}, u32[]{:S(2)}, u32[]{:S(2)}) collective-permute-start(bf16[128,512]{1,0:T(8,128)(2,1)S(1)} %get-tuple-element.63), channel_id=1, source_target_pairs={{0,1},{1,0},{2,3},{3,2},{4,5},{5,4},{6,7},{7,6},{8,9},{9,8},{10,11... | collective-permute-start | bytes 393224 | tf_op jit(solution)/shard_map/ppermute | solution.py:28
  80.1 1.7 %collective-permute-start.14 = (bf16[128,512]{1,0:T(8,128)(2,1)S(1)}, bf16[128,512]{1,0:T(8,128)(2,1)S(1)}, u32[]{:S(2)}, u32[]{:S(2)}) collective-permute-start(bf16[128,512]{1,0:T(8,128)(2,1)S(1)} %get-tuple-element.65), channel_id=1, source_target_pairs={{0,1},{1,0},{2,3},{3,2},{4,5},{5,4},{6,7},{7,6},{8,9},{9,8},{10,11... | collective-permute-start | bytes 393224 | tf_op jit(solution)/shard_map/ppermute | solution.py:28

commit v4 on v3

--- a/solution.py
+++ b/solution.py
@@ -49,14 +49,11 @@
     return [pl.BlockSpec(memory_space=pltpu.VMEM)] * count
 
 
-def smem():
-    return pl.BlockSpec(memory_space=pltpu.SMEM)
-
-
-def pack_kernel(core, key, query, grad, value, key_mine, key_other, mine, other, done):
+def pack_kernel(key, query, grad, value, key_mine, key_other, mine, other, bias, done):
     half = query.shape[1] // 2
-    here = pl.multiple_of(core[0] * half, half)
-    there = pl.multiple_of((1 - core[0]) * half, half)
+    core = lax.axis_index("c")
+    here = pl.multiple_of(core * half, half)
+    there = pl.multiple_of((1 - core) * half, half)
     moves = [(key, key_other.at[0], there), (key, key_mine.at[0], here)]
     for at, source in enumerate((query, grad, value)):
         moves += [(source, other.at[at], there), (source, mine.at[at], here)]
@@ -66,24 +63,25 @@
     ]
     for copy in copies:
         copy.start()
+    window_bias(core == lax.rem(lax.axis_index("z"), 2), bias)
     for copy in copies:
         copy.wait()
 
 
-def pack(core, key, query, grad, value):
+def pack(key, query, grad, value):
     rows, features = query.shape
     one, three = (
         jax.ShapeDtypeStruct((count, rows, features // 2), query.dtype) for count in (1, 3)
     )
     return pl.pallas_call(
         pack_kernel,
-        out_shape=(one, one, three, three),
-        in_specs=[smem()] + [pl.BlockSpec(memory_space=pltpu.HBM)] * 4,
-        out_specs=tuple(vmem(4)),
+        out_shape=(one, one, three, three, jax.ShapeDtypeStruct((8, 2 * rows), jnp.float32)),
+        in_specs=[pl.BlockSpec(memory_space=pltpu.HBM)] * 4,
+        out_specs=tuple(vmem(5)),
         scratch_shapes=[pltpu.SemaphoreType.DMA((8,))],
         compiler_params=ROOM,
         name="pack",
-    )(core, *(in_hbm(array) for array in (key, query, grad, value)))
+    )(*(in_hbm(array) for array in (key, query, grad, value)))
 
 
 def in_hbm(array):
@@ -110,16 +108,18 @@
     )(mine, part)
 
 
-def window_bias(place, tokens):
-    left = lax.broadcasted_iota(jnp.int32, (1, 2 * tokens), 1) < tokens
-    unlike = jnp.where(place[0] == place[1], 0.0, NEG)
-    alike = jnp.where(place[0] == place[1], NEG, 0.0)
-    return {
-        0: jnp.where(left, 0.0, unlike),
-        1: jnp.where(left, alike, 0.0),
-        4: jnp.where(left, 0.0, alike),
-        5: jnp.where(left, unlike, 0.0),
-    }
+def window_bias(alike, out):
+    shape = out.shape[:0] + (1, out.shape[1])
+    left = lax.broadcasted_iota(jnp.int32, shape, 1) < out.shape[1] // 2
+    unlike = jnp.where(alike, 0.0, NEG)
+    like = jnp.where(alike, NEG, 0.0)
+    out[0:1] = jnp.where(left, 0.0, unlike)
+    out[1:2] = jnp.where(left, like, 0.0)
+    out[2:3] = jnp.zeros(shape, jnp.float32)
+    out[3:4] = jnp.zeros(shape, jnp.float32)
+    out[4:5] = jnp.where(left, 0.0, like)
+    out[5:6] = jnp.where(left, unlike, 0.0)
+    out[6:8] = jnp.zeros((2, out.shape[1]), jnp.float32)
 
 
 def scores_of(bias, keys, queries, scale):
@@ -128,13 +128,12 @@
     parts = []
     for block in range(6):
         part = flat[block * size : (block + 1) * size]
-        parts.append(part + bias[block] if block in bias else part)
+        parts.append(part + bias[block : block + 1] if block in (0, 1, 4, 5) else part)
     return jnp.concatenate(parts, 0)
 
 
-def value_kernel(scale, place, query, grad, first_k, key, second_k, first, own, second, lse):
+def value_kernel(scale, bias, query, grad, first_k, key, second_k, first, own, second, lse):
     two, width = query.shape
-    bias = window_bias(place, two // 2)
     for head in range(width // HEAD):
         at = slice(head * HEAD, (head + 1) * HEAD)
         keys = jnp.concatenate([first_k[:, at], key[:, at], second_k[:, at]], 0)
@@ -151,11 +150,10 @@
 
 
 def score_kernel(
-    scale, place, query, grad, first_k, key, second_k, first_v, value, second_v, lse,
+    scale, bias, query, grad, first_k, key, second_k, first_v, value, second_v, lse,
     query_grad, query_back, first, own, second,
 ):
     two, width = query.shape
-    bias = window_bias(place, two // 2)
     for head in range(width // HEAD):
         at = slice(head * HEAD, (head + 1) * HEAD)
         keys = jnp.concatenate([first_k[:, at], key[:, at], second_k[:, at]], 0)
@@ -176,7 +174,7 @@
         second[:, at] = terms[2 * two :].astype(jnp.bfloat16)
 
 
-def value_pass(core, query, grad, keys, scale):
+def value_pass(bias, query, grad, keys, scale):
     two, width = query.shape
     heads = width // HEAD
     low = jax.ShapeDtypeStruct((two, width), jnp.bfloat16)
@@ -185,17 +183,17 @@
     return pl.pallas_call(
         lambda *refs: value_kernel(scale, *refs),
         out_shape=(low, high, low, jax.ShapeDtypeStruct((heads, 8, two), jnp.float32)),
-        in_specs=[smem()] + vmem(5),
+        in_specs=vmem(6),
         out_specs=tuple(vmem(4)),
         cost_estimate=pl.CostEstimate(
             flops=4 * work * HEAD, transcendentals=work, bytes_accessed=4 << 20
         ),
         compiler_params=ROOM,
         name="value_pass",
-    )(core, query, grad, *keys)
-
-
-def score_pass(core, query, grad, keys, values, lse, scale):
+    )(bias, query, grad, *keys)
+
+
+def score_pass(bias, query, grad, keys, values, lse, scale):
     two, width = query.shape
     heads = width // HEAD
     low = jax.ShapeDtypeStruct((two, width), jnp.bfloat16)
@@ -205,34 +203,34 @@
     return pl.pallas_call(
         lambda *refs: score_kernel(scale, *refs),
         out_shape=(part, part, low, high, low),
-        in_specs=[smem()] + vmem(9),
+        in_specs=vmem(10),
         out_specs=tuple(vmem(5)),
         cost_estimate=pl.CostEstimate(
             flops=8 * work * HEAD, transcendentals=work, bytes_accessed=6 << 20
         ),
         compiler_params=ROOM,
         name="score_pass",
-    )(core, query, grad, *keys, *values, lse)
-
-
-def block_kernel(count, place, own, *blocks):
+    )(bias, query, grad, *keys, *values, lse)
+
+
+def block_kernel(count, own, *blocks):
     size = own.shape[1] // count
     for step, block in enumerate(blocks):
-        target = lax.rem(place[2] + step, count)
+        target = lax.rem(lax.axis_index("y") + step, count)
         block[...] = own[:, pl.ds(pl.multiple_of(target * size, size), size)]
 
 
-def input_blocks(place, own, count):
+def input_blocks(own, count):
     rows, width = own.shape
     block = jax.ShapeDtypeStruct((rows, width // count), own.dtype)
     return pl.pallas_call(
         lambda *refs: block_kernel(count, *refs),
         out_shape=(block,) * count,
-        in_specs=[smem()] + vmem(1),
+        in_specs=vmem(1),
         out_specs=tuple(vmem(count)),
         compiler_params=ROOM,
         name="input_blocks",
-    )(place, own)
+    )(own)
 
 
 def stack_kernel(count, *refs):
@@ -309,11 +307,8 @@
     ny, nx, nz, nc = sizes
     devices = ny * nx * nz * nc
     scale = 1.0 / math.sqrt(HEAD)
-    core = lax.axis_index("c").astype(jnp.int32)
-    parity = lax.rem(lax.axis_index("z").astype(jnp.int32), 2)
-    place = jnp.stack([core, parity, lax.axis_index("y").astype(jnp.int32)])
-    even = core == 0
-    place, even, query_rows = lax.optimization_barrier((place, even, query_rows))
+    even = lax.axis_index("c") == 0
+    even, query_rows = lax.optimization_barrier((even, query_rows))
 
     def both_halves(mine, other):
         return jnp.where(
@@ -325,7 +320,7 @@
         got_two = swap(two, devices, 1)
         return got_one, got_two
 
-    key_mine, key_other, mine, other = pack(place, key_rows, query_rows, out_grad, value_rows)
+    key_mine, key_other, mine, other, bias = pack(key_rows, query_rows, out_grad, value_rows)
     key_part = to_core(key_other, devices)
     part = to_core(other, devices)
     (key,) = join(key_mine, key_part)
@@ -335,21 +330,22 @@
     first_v, second_v = swaps(value, value)
 
     inputs, _ = lax.optimization_barrier((inputs, mine))
-    blocks = input_blocks(place, inputs, ny)
+    blocks = input_blocks(inputs, ny)
     taken = [blocks[0]]
     for step in range(1, ny):
         taken.append(along_y(blocks[step], sizes, step))
 
-    first, own, second, lse = value_pass(place, query, grad, keys, scale)
+    first, own, second, lse = value_pass(bias, query, grad, keys, scale)
     from_first, from_second = swaps(first, second)
     value_half = (own + from_first.astype(jnp.float32) + from_second.astype(jnp.float32)).astype(
         jnp.bfloat16
     )
-    *taken, query, _ = lax.optimization_barrier((*taken, query, value_half))
+    query, _ = lax.optimization_barrier((query, value_half))
     dq, dq_other, key_first, key_own, key_second = score_pass(
-        place, query, grad, keys, (first_v, value, second_v), lse, scale
+        bias, query, grad, keys, (first_v, value, second_v), lse, scale
     )
     key_from_first, key_from_second = swaps(key_first, key_second)
+    *taken, _ = lax.optimization_barrier((*taken, key_own))
     taken = stack(taken)
     taken_part = to_core(taken, devices)
     taken = merge(taken, taken_part)

time: 97.5 us -> 97 us (level)
  waiting for transfers between devices: 40.6 us -> 44.3 us
  Pallas kernels: 10.4 us -> 8.19 us
  starting transfers between devices: 42.1 us -> 40.1 us
    ppermute x6, waiting for transfers between devices: 7.37 us -> 14.4 us  [along_y(): return lax.ppermute(array, AXES, pairs)]
    ppermute x8, starting transfers between devices: 25.9 us -> 22.9 us  [swap(): return lax.ppermute(array, AXES, pairs)]
    ppermute x8, waiting for transfers between devices: 18.3 us -> 15.5 us  [swap(): return lax.ppermute(array, AXES, pairs)]
    all_to_all x1, starting transfers between devices: 5.58 us -> 8.08 us  [steps(): arrived = lax.all_to_all(pieces, ('x', 'z', 'c'), 0, 0, tiled=True)]
    ppermute x6, starting transfers between devices: 4.29 us -> 3.18 us  [along_y(): return lax.ppermute(array, AXES, pairs)]
  transfers between devices with their start and end apart: 21 -> 21, of which waited for: 7 -> 9; matrix products, arithmetic and copies ran while one was open for 3% -> 3% of each run, Pallas kernels for 6% -> 5%
where the time goes in v4:
time: 97 us; the launch traced here: 96.8 us
  waiting for transfers between devices  44.3 us (46%)
  starting transfers between devices  40.1 us (41%)
  Pallas kernels  8.19 us (8%)
  other arithmetic  3.28 us (3%)
    ppermute x8, starting transfers between devices, swap(): return lax.ppermute(array, AXES, pairs)  22.9 us
    ppermute x8, waiting for transfers between devices, swap(): return lax.ppermute(array, AXES, pairs)  15.5 us
    ppermute x6, waiting for transfers between devices, along_y(): return lax.ppermute(array, AXES, pairs)  14.4 us
    all_to_all x1, waiting for transfers between devices, steps(): arrived = lax.all_to_all(pieces, ('x', 'z', 'c'), 0, 0, tiled=True)  13.4 us
    all_to_all x1, starting transfers between devices, steps(): arrived = lax.all_to_all(pieces, ('x', 'z', 'c'), 0, 0, tiled=True)  8.08 us
    ppermute x6, starting transfers between devices, to_core(): lax.ppermute(array, AXES, [(device, device ^ 1) for device in range(count)])  6.01 us
    ppermute x6, starting transfers between devices, along_y(): return lax.ppermute(array, AXES, pairs)  3.18 us
    pallas_call x1, Pallas kernels, score_pass(): pl.pallas_call(lambda *refs: score_kernel(scale, *refs), out_shape=(part,...  3.07 us
  transfers between devices with their start and end apart: 21, of which 9 were waited for; matrix products, arithmetic and copies ran while one was open for 3% of the time, Pallas kernels for 5%

profile of v4, /device:TPU:1, one launch (start us, length us, event | category | flops | bytes accessed | tf_op | source)
XLA Modules:
  0.0 96.8 jit_solution(6692065224917121724)
XLA Ops:
  0.6 1.4 %pack.1 = (bf16[1,128,512]{2,1,0:T(8,128)(2,1)S(1)}, bf16[1,128,512]{2,1,0:T(8,128)(2,1)S(1)}, bf16[3,128,512]{2,1,0:T(8,128)(2,1)S(1)}, bf16[3,128,512]{2,1,0:T(8,128)(2,1)S(1)}, f32[8,256]{1,0:T(8,128)S(1)}) custom-call(bf16[128,1024]{1,0:T(8,128)(2,1)} %key.1, bf16[128,1024]{1,0:T(8,128)(2,1)} %query, bf16[128,1024]{1,0:T(8,128)(2,1)} %grad.1, ...), custom_call_target="tpu_custom_call" | custom-call | tf_op jit(solution)/shard_map/pack/pallas_call | solution.py:76
  2.0 3.3 %collective-permute-start.1 = (bf16[1,128,512]{2,1,0:T(8,128)(2,1)S(1)}, bf16[1,128,512]{2,1,0:T(8,128)(2,1)S(1)}, u32[]{:S(2)}, u32[]{:S(2)}) collective-permute-start(bf16[1,128,512]{2,1,0:T(8,128)(2,1)S(1)} %get-tuple-element.41), channel_id=1, source_target_pairs={{0,1},{1,0},{2,3},{3,2},{4,5},{5,4},{6,7},{7,6},{8,9},{9,8},{10,11... | collective-permute-start | bytes 393224 | tf_op jit(solution)/shard_map/ppermute | solution.py:28
  5.3 0.1 collective-permute-start
  5.4 0.9 collective-permute-done.1.part
  6.3 0.1 collective-permute-start.2
  6.4 9.2 %collective-permute-start.3 = (bf16[256,512]{1,0:T(8,128)(2,1)S(1)}, bf16[256,512]{1,0:T(8,128)(2,1)S(1)}, u32[]{:S(2)}, u32[]{:S(2)}) collective-permute-start(bf16[256,512]{1,0:T(8,128)(2,1)S(1)} %join.3.refs_4_), channel_id=1, source_target_pairs={{0,254},{1,255},{2,4},{3,5},{4,2},{5,3},{6,8},{7,9},{8,6},{9,7},{1... | collective-permute-start | bytes 786440 | tf_op jit(solution)/shard_map/ppermute | solution.py:38
  15.6 0.0 collective-permute-done.part
  15.6 0.1 join.2
  15.7 0.0 collective-permute-done.2.refs_3_
  15.7 6.0 %collective-permute-done.3.refs_5_ = bf16[256,512]{1,0:T(8,128)(2,1)S(1)} collective-permute-done((bf16[256,512]{1,0:T(8,128)(2,1)S(1)}, bf16[256,512]{1,0:T(8,128)(2,1)S(1)}, u32[]{:S(2)}, u32[]{:S(2)}) %collective-permute-start.3) | collective-permute-done | bytes 262176 | tf_op jit(solution)/shard_map/ppermute | solution.py:38
  21.7 0.0 copy-start
  21.7 1.7 %value_pass.1 = (bf16[256,512]{1,0:T(8,128)(2,1)S(1)}, f32[256,512]{1,0:T(8,128)S(1)}, bf16[256,512]{1,0:T(8,128)(2,1)S(1)}, f32[4,8,256]{2,1,0:T(8,128)S(1)}) custom-call(f32[8,256]{1,0:T(8,128)S(1)} %get-tuple-element.35.refs_0_, bf16[256,512]{1,0:T(8,128)(2,1)S(1)} %get-tuple-element.45.refs_1_, bf16[256,512]{1,0:T(8,128)(2,1)S(1)} %get-tuple-element.39.refs_2_, ...), custom_call_target="tpu_custom_call" | custom-call | flops 402653184 | bytes 4194304 | tf_op jit(solution)/shard_map/value_pass/pallas_call | solution.py:183
  23.4 0.1 collective-permute-start.4
  23.5 6.7 %collective-permute-start.5 = (bf16[256,512]{1,0:T(8,128)(2,1)S(1)}, bf16[256,512]{1,0:T(8,128)(2,1)S(1)}, u32[]{:S(2)}, u32[]{:S(2)}) collective-permute-start(bf16[256,512]{1,0:T(8,128)(2,1)S(1)} %get-tuple-element.44), channel_id=1, source_target_pairs={{0,254},{1,255},{2,4},{3,5},{4,2},{5,3},{6,8},{7,9},{8,6},{9,7},{1... | collective-permute-start | bytes 786440 | tf_op jit(solution)/shard_map/ppermute | solution.py:38
  30.2 0.0 collective-permute-start.6
  30.2 1.4 %collective-permute-start.7 = (bf16[256,512]{1,0:T(8,128)(2,1)S(1)}, bf16[256,512]{1,0:T(8,128)(2,1)S(1)}, u32[]{:S(2)}, u32[]{:S(2)}) collective-permute-start(bf16[256,512]{1,0:T(8,128)(2,1)S(1)} %get-tuple-element.46.refs_7_), channel_id=1, source_target_pairs={{0,254},{1,255},{2,4},{3,5},{4,2},{5,3},{6,8},{7,9},{8,6},{9,7},{1... | collective-permute-start | bytes 786440 | tf_op jit(solution)/shard_map/ppermute | solution.py:38
  31.6 0.0 copy-done
  31.6 0.1 collective-permute-start.13
  31.7 0.0 collective-permute-done.4
  31.7 0.4 collective-permute-start.14
  32.2 3.5 %collective-permute-done.5 = bf16[256,512]{1,0:T(8,128)(2,1)S(1)} collective-permute-done((bf16[256,512]{1,0:T(8,128)(2,1)S(1)}, bf16[256,512]{1,0:T(8,128)(2,1)S(1)}, u32[]{:S(2)}, u32[]{:S(2)}) %collective-permute-start.5) | collective-permute-done | bytes 262176 | tf_op jit(solution)/shard_map/ppermute | solution.py:38
  35.7 0.0 collective-permute-start.15
  35.7 0.1 add_convert_fusion.1.refs_0_
  35.8 0.5 collective-permute-done.6.refs_6_
  36.3 5.4 %collective-permute-done.7.refs_8_ = bf16[256,512]{1,0:T(8,128)(2,1)S(1)} collective-permute-done((bf16[256,512]{1,0:T(8,128)(2,1)S(1)}, bf16[256,512]{1,0:T(8,128)(2,1)S(1)}, u32[]{:S(2)}, u32[]{:S(2)}) %collective-permute-start.7) | collective-permute-done | bytes 262176 | tf_op jit(solution)/shard_map/ppermute | solution.py:38
  41.7 3.1 %score_pass.1 = (bf16[128,512]{1,0:T(8,128)(2,1)S(1)}, bf16[128,512]{1,0:T(8,128)(2,1)S(1)}, bf16[256,512]{1,0:T(8,128)(2,1)S(1)}, f32[256,512]{1,0:T(8,128)S(1)}, bf16[256,512]{1,0:T(8,128)(2,1)S(1)}) custom-call(f32[8,256]{1,0:T(8,128)S(1)} %get-tuple-element.35.refs_0_, bf16[256,512]{1,0:T(8,128)(2,1)S(1)} %get-tuple-element.45.refs_1_, ...), custom_call_target="tpu_custom_call" | custom-call | flops 805306368 | bytes 6291456 | tf_op jit(solution)/shard_map/score_pass/pallas_call | solution.py:203
  44.8 2.8 %collective-permute-done.13.refs_1_ = bf16[128,512]{1,0:T(8,128)(2,1)S(1)} collective-permute-done((bf16[128,512]{1,0:T(8,128)(2,1)S(1)}, bf16[128,512]{1,0:T(8,128)(2,1)S(1)}, u32[]{:S(2)}, u32[]{:S(2)}) %collective-permute-start.13) | collective-permute-done | bytes 131104 | tf_op jit(solution)/shard_map/ppermute | solution.py:45
  47.6 0.0 collective-permute-done.14.refs_2_
  47.6 0.0 collective-permute-done.15.refs_3_
  47.7 1.5 %collective-permute-start.16 = (bf16[4,128,512]{2,1,0:T(8,128)(2,1)S(1)}, bf16[4,128,512]{2,1,0:T(8,128)(2,1)S(1)}, u32[]{:S(2)}, u32[]{:S(2)}) collective-permute-start(bf16[4,128,512]{2,1,0:T(8,128)(2,1)S(1)} %stack.1.own), channel_id=1, source_target_pairs={{0,1},{1,0},{2,3},{3,2},{4,5},{5,4},{6,7},{7,6},{8,9},{9,8},{10,11... | collective-permute-start | bytes 1572872 | tf_op jit(solution)/shard_map/ppermute | solution.py:28
  49.1 0.0 collective-permute-start.17
  49.1 0.5 collective-permute-start.18
  49.6 2.2 %collective-permute-start.19 = (bf16[256,512]{1,0:T(8,128)(2,1)S(1)}, bf16[256,512]{1,0:T(8,128)(2,1)S(1)}, u32[]{:S(2)}, u32[]{:S(2)}) collective-permute-start(bf16[256,512]{1,0:T(8,128)(2,1)S(1)} %add_convert_fusion.1.refs_0_), channel_id=1, source_target_pairs={{0,192},{1,193},{2,194},{3,195},{4,196},{5,197},{6,198},{7,199},{8... | collective-permute-start | bytes 786440 | tf_op jit(solution)/shard_map/ppermute | solution.py:45
  51.8 5.4 %collective-permute-start.10 = (bf16[256,512]{1,0:T(8,128)(2,1)S(1)}, bf16[256,512]{1,0:T(8,128)(2,1)S(1)}, u32[]{:S(2)}, u32[]{:S(2)}) collective-permute-start(bf16[256,512]{1,0:T(8,128)(2,1)S(1)} %get-tuple-element.52), channel_id=1, source_target_pairs={{0,254},{1,255},{2,4},{3,5},{4,2},{5,3},{6,8},{7,9},{8,6},{9,7},{1... | collective-permute-start | bytes 786440 | tf_op jit(solution)/shard_map/ppermute | solution.py:38
  57.2 0.0 collective-permute-done.16.part
  57.2 0.0 collective-permute-start.9
  57.2 0.4 merge.1.inputs
  57.6 11.6 %collective-permute-done.17.refs_1_ = bf16[256,512]{1,0:T(8,128)(2,1)S(1)} collective-permute-done((bf16[256,512]{1,0:T(8,128)(2,1)S(1)}, bf16[256,512]{1,0:T(8,128)(2,1)S(1)}, u32[]{:S(2)}, u32[]{:S(2)}) %collective-permute-start.17) | collective-permute-done | bytes 262176 | tf_op jit(solution)/shard_map/ppermute | solution.py:45
  69.2 0.0 collective-permute-done.18.refs_2_
  69.2 0.0 collective-permute-done.19.refs_3_
  69.2 1.5 %weight_pass.1 = bf16[512,512]{1,0:T(8,128)(2,1)} custom-call(bf16[512,1024]{1,0:T(8,128)(2,1)S(1)} %merge.1.inputs, bf16[256,512]{1,0:T(8,128)(2,1)S(1)} %add_convert_fusion.1.refs_0_, bf16[256,512]{1,0:T(8,128)(2,1)S(1)} %collective-permute-done.17.refs_1_, bf16[256,512]{1,0:T(8,128)(2,1)S(1)} %collective-permute-done.18.refs_2_, ...), custom_call_target="tpu_custom_call" | custom-call | flops 536870912 | bytes 4194304 | tf_op jit(solution)/shard_map/weight_pass/pallas_call | solution.py:291
  70.7 8.1 %all-to-all-start = ((bf16[64,8,512]{2,1,0:T(8,128)(2,1)}), bf16[64,8,512]{2,1,0:T(8,128)(2,1)S(1)}, u32[]{:S(2)}, u32[]{:S(2)}) async-start(bf16[64,8,512]{2,1,0:T(8,128)(2,1)} %bitcast), calls=%async_computation | async-start | bytes 1048576 | tf_op jit(solution)/shard_map/all_to_all | solution.py:361
  78.8 0.5 collective-permute-start.12
  79.4 0.1 collective-permute-start.8
  79.5 0.0 collective-permute-done.10
  79.5 0.0 collective-permute-done.9
  79.5 0.1 add_convert_fusion
  79.6 0.5 collective-permute-start.11
  80.1 0.2 collective-permute-done.12
  80.3 0.8 maximum_select_fusion.2
  81.1 0.0 collective-permute-done.8
  81.1 0.8 maximum_select_fusion
  81.9 0.0 collective-permute-done.11
  81.9 0.8 maximum_select_fusion.1
  82.7 13.4 %all-to-all-done = bf16[64,8,512]{2,1,0:T(8,128)(2,1)S(1)} async-done(((bf16[64,8,512]{2,1,0:T(8,128)(2,1)}), bf16[64,8,512]{2,1,0:T(8,128)(2,1)S(1)}, u32[]{:S(2)}, u32[]{:S(2)}) %all-to-all-start) | async-done | bytes 524320 | tf_op jit(solution)/shard_map/all_to_all | solution.py:361
  96.1 0.1 convert_reduce_fusion
  96.2 0.6 broadcast_multiply_fusion
  (5 shorter events, 0.1 us)
Async XLA Ops:
  2.0 4.3 %collective-permute-start.1 = (bf16[1,128,512]{2,1,0:T(8,128)(2,1)S(1)}, bf16[1,128,512]{2,1,0:T(8,128)(2,1)S(1)}, u32[]{:S(2)}, u32[]{:S(2)}) collective-permute-start(bf16[1,128,512]{2,1,0:T(8,128)(2,1)S(1)} %get-tuple-element.41), channel_id=1, source_target_pairs={{0,1},{1,0},{2,3},{3,2},{4,5},{5,4},{6,7},{7,6},{8,9},{9,8},{10,11... | collective-permute-start | bytes 393224 | tf_op jit(solution)/shard_map/ppermute | solution.py:28
  5.3 10.3 %collective-permute-start = (bf16[3,128,512]{2,1,0:T(8,128)(2,1)S(1)}, bf16[3,128,512]{2,1,0:T(8,128)(2,1)S(1)}, u32[]{:S(2)}, u32[]{:S(2)}) collective-permute-start(bf16[3,128,512]{2,1,0:T(8,128)(2,1)S(1)} %get-tuple-element.37), channel_id=1, source_target_pairs={{0,1},{1,0},{2,3},{3,2},{4,5},{5,4},{6,7},{7,6},{8,9},{9,8},{10,11... | collective-permute-start | bytes 1179656 | tf_op jit(solution)/shard_map/ppermute | solution.py:28
  6.3 9.4 %collective-permute-start.2 = (bf16[256,512]{1,0:T(8,128)(2,1)S(1)}, bf16[256,512]{1,0:T(8,128)(2,1)S(1)}, u32[]{:S(2)}, u32[]{:S(2)}) collective-permute-start(bf16[256,512]{1,0:T(8,128)(2,1)S(1)} %join.3.refs_4_), channel_id=1, source_target_pairs={{0,2},{1,3},{2,0},{3,1},{4,6},{5,7},{6,4},{7,5},{8,10},{9,11},{10,... | collective-permute-start | bytes 786440 | tf_op jit(solution)/shard_map/ppermute | solution.py:38
  6.4 15.3 %collective-permute-start.3 = (bf16[256,512]{1,0:T(8,128)(2,1)S(1)}, bf16[256,512]{1,0:T(8,128)(2,1)S(1)}, u32[]{:S(2)}, u32[]{:S(2)}) collective-permute-start(bf16[256,512]{1,0:T(8,128)(2,1)S(1)} %join.3.refs_4_), channel_id=1, source_target_pairs={{0,254},{1,255},{2,4},{3,5},{4,2},{5,3},{6,8},{7,9},{8,6},{9,7},{1... | collective-permute-start | bytes 786440 | tf_op jit(solution)/shard_map/ppermute | solution.py:38
  21.7 9.9 %copy-start = (bf16[128,2048]{1,0:T(8,128)(2,1)S(1)}, bf16[128,2048]{1,0:T(8,128)(2,1)}, u32[]{:S(2)}) copy-start(bf16[128,2048]{1,0:T(8,128)(2,1)} %refs_0_) | copy-start | bytes 1572868
  23.4 8.3 %collective-permute-start.4 = (bf16[256,512]{1,0:T(8,128)(2,1)S(1)}, bf16[256,512]{1,0:T(8,128)(2,1)S(1)}, u32[]{:S(2)}, u32[]{:S(2)}) collective-permute-start(bf16[256,512]{1,0:T(8,128)(2,1)S(1)} %get-tuple-element.43), channel_id=1, source_target_pairs={{0,2},{1,3},{2,0},{3,1},{4,6},{5,7},{6,4},{7,5},{8,10},{9,11},{10,... | collective-permute-start | bytes 786440 | tf_op jit(solution)/shard_map/ppermute | solution.py:38
  23.5 12.2 %collective-permute-start.5 = (bf16[256,512]{1,0:T(8,128)(2,1)S(1)}, bf16[256,512]{1,0:T(8,128)(2,1)S(1)}, u32[]{:S(2)}, u32[]{:S(2)}) collective-permute-start(bf16[256,512]{1,0:T(8,128)(2,1)S(1)} %get-tuple-element.44), channel_id=1, source_target_pairs={{0,254},{1,255},{2,4},{3,5},{4,2},{5,3},{6,8},{7,9},{8,6},{9,7},{1... | collective-permute-start | bytes 786440 | tf_op jit(solution)/shard_map/ppermute | solution.py:38
  30.2 6.1 %collective-permute-start.6 = (bf16[256,512]{1,0:T(8,128)(2,1)S(1)}, bf16[256,512]{1,0:T(8,128)(2,1)S(1)}, u32[]{:S(2)}, u32[]{:S(2)}) collective-permute-start(bf16[256,512]{1,0:T(8,128)(2,1)S(1)} %get-tuple-element.46.refs_7_), channel_id=1, source_target_pairs={{0,2},{1,3},{2,0},{3,1},{4,6},{5,7},{6,4},{7,5},{8,10},{9,11},{10,... | collective-permute-start | bytes 786440 | tf_op jit(solution)/shard_map/ppermute | solution.py:38
  30.2 11.5 %collective-permute-start.7 = (bf16[256,512]{1,0:T(8,128)(2,1)S(1)}, bf16[256,512]{1,0:T(8,128)(2,1)S(1)}, u32[]{:S(2)}, u32[]{:S(2)}) collective-permute-start(bf16[256,512]{1,0:T(8,128)(2,1)S(1)} %get-tuple-element.46.refs_7_), channel_id=1, source_target_pairs={{0,254},{1,255},{2,4},{3,5},{4,2},{5,3},{6,8},{7,9},{8,6},{9,7},{1... | collective-permute-start | bytes 786440 | tf_op jit(solution)/shard_map/ppermute | solution.py:38
  31.6 16.0 %collective-permute-start.13 = (bf16[128,512]{1,0:T(8,128)(2,1)S(1)}, bf16[128,512]{1,0:T(8,128)(2,1)S(1)}, u32[]{:S(2)}, u32[]{:S(2)}) collective-permute-start(bf16[128,512]{1,0:T(8,128)(2,1)S(1)} %get-tuple-element.55), channel_id=1, source_target_pairs={{0,64},{1,65},{2,66},{3,67},{4,68},{5,69},{6,70},{7,71},{8,72},{9,... | collective-permute-start | bytes 393224 | tf_op jit(solution)/shard_map/ppermute | solution.py:45
  31.7 15.9 %collective-permute-start.14 = (bf16[128,512]{1,0:T(8,128)(2,1)S(1)}, bf16[128,512]{1,0:T(8,128)(2,1)S(1)}, u32[]{:S(2)}, u32[]{:S(2)}) collective-permute-start(bf16[128,512]{1,0:T(8,128)(2,1)S(1)} %get-tuple-element.56), channel_id=1, source_target_pairs={{0,128},{1,129},{2,130},{3,131},{4,132},{5,133},{6,134},{7,135},{8... | collective-permute-start | bytes 393224 | tf_op jit(solution)/shard_map/ppermute | solution.py:45
  35.7 11.9 %collective-permute-start.15 = (bf16[128,512]{1,0:T(8,128)(2,1)S(1)}, bf16[128,512]{1,0:T(8,128)(2,1)S(1)}, u32[]{:S(2)}, u32[]{:S(2)}) collective-permute-start(bf16[128,512]{1,0:T(8,128)(2,1)S(1)} %get-tuple-element.57), channel_id=1, source_target_pairs={{0,192},{1,193},{2,194},{3,195},{4,196},{5,197},{6,198},{7,199},{8... | collective-permute-start | bytes 393224 | tf_op jit(solution)/shard_map/ppermute | solution.py:45
  47.7 9.6 %collective-permute-start.16 = (bf16[4,128,512]{2,1,0:T(8,128)(2,1)S(1)}, bf16[4,128,512]{2,1,0:T(8,128)(2,1)S(1)}, u32[]{:S(2)}, u32[]{:S(2)}) collective-permute-start(bf16[4,128,512]{2,1,0:T(8,128)(2,1)S(1)} %stack.1.own), channel_id=1, source_target_pairs={{0,1},{1,0},{2,3},{3,2},{4,5},{5,4},{6,7},{7,6},{8,9},{9,8},{10,11... | collective-permute-start | bytes 1572872 | tf_op jit(solution)/shard_map/ppermute | solution.py:28
  49.1 20.0 %collective-permute-start.17 = (bf16[256,512]{1,0:T(8,128)(2,1)S(1)}, bf16[256,512]{1,0:T(8,128)(2,1)S(1)}, u32[]{:S(2)}, u32[]{:S(2)}) collective-permute-start(bf16[256,512]{1,0:T(8,128)(2,1)S(1)} %add_convert_fusion.1.refs_0_), channel_id=1, source_target_pairs={{0,64},{1,65},{2,66},{3,67},{4,68},{5,69},{6,70},{7,71},{8,72},{9,... | collective-permute-start | bytes 786440 | tf_op jit(solution)/shard_map/ppermute | solution.py:45
  49.1 20.0 %collective-permute-start.18 = (bf16[256,512]{1,0:T(8,128)(2,1)S(1)}, bf16[256,512]{1,0:T(8,128)(2,1)S(1)}, u32[]{:S(2)}, u32[]{:S(2)}) collective-permute-start(bf16[256,512]{1,0:T(8,128)(2,1)S(1)} %add_convert_fusion.1.refs_0_), channel_id=1, source_target_pairs={{0,128},{1,129},{2,130},{3,131},{4,132},{5,133},{6,134},{7,135},{8... | collective-permute-start | bytes 786440 | tf_op jit(solution)/shard_map/ppermute | solution.py:45
  49.6 19.6 %collective-permute-start.19 = (bf16[256,512]{1,0:T(8,128)(2,1)S(1)}, bf16[256,512]{1,0:T(8,128)(2,1)S(1)}, u32[]{:S(2)}, u32[]{:S(2)}) collective-permute-start(bf16[256,512]{1,0:T(8,128)(2,1)S(1)} %add_convert_fusion.1.refs_0_), channel_id=1, source_target_pairs={{0,192},{1,193},{2,194},{3,195},{4,196},{5,197},{6,198},{7,199},{8... | collective-permute-start | bytes 786440 | tf_op jit(solution)/shard_map/ppermute | solution.py:45
  51.8 27.6 %collective-permute-start.10 = (bf16[256,512]{1,0:T(8,128)(2,1)S(1)}, bf16[256,512]{1,0:T(8,128)(2,1)S(1)}, u32[]{:S(2)}, u32[]{:S(2)}) collective-permute-start(bf16[256,512]{1,0:T(8,128)(2,1)S(1)} %get-tuple-element.52), channel_id=1, source_target_pairs={{0,254},{1,255},{2,4},{3,5},{4,2},{5,3},{6,8},{7,9},{8,6},{9,7},{1... | collective-permute-start | bytes 786440 | tf_op jit(solution)/shard_map/ppermute | solution.py:38
  57.2 22.3 %collective-permute-start.9 = (bf16[256,512]{1,0:T(8,128)(2,1)S(1)}, bf16[256,512]{1,0:T(8,128)(2,1)S(1)}, u32[]{:S(2)}, u32[]{:S(2)}) collective-permute-start(bf16[256,512]{1,0:T(8,128)(2,1)S(1)} %get-tuple-element.51), channel_id=1, source_target_pairs={{0,2},{1,3},{2,0},{3,1},{4,6},{5,7},{6,4},{7,5},{8,10},{9,11},{10,... | collective-permute-start | bytes 786440 | tf_op jit(solution)/shard_map/ppermute | solution.py:38
  70.7 25.4 %all-to-all-start = ((bf16[64,8,512]{2,1,0:T(8,128)(2,1)}), bf16[64,8,512]{2,1,0:T(8,128)(2,1)S(1)}, u32[]{:S(2)}, u32[]{:S(2)}) async-start(bf16[64,8,512]{2,1,0:T(8,128)(2,1)} %bitcast), calls=%async_computation | async-start | bytes 1048576 | tf_op jit(solution)/shard_map/all_to_all | solution.py:361
  78.8 1.5 %collective-permute-start.12 = (bf16[128,512]{1,0:T(8,128)(2,1)S(1)}, bf16[128,512]{1,0:T(8,128)(2,1)S(1)}, u32[]{:S(2)}, u32[]{:S(2)}) collective-permute-start(bf16[128,512]{1,0:T(8,128)(2,1)S(1)} %get-tuple-element.63), channel_id=1, source_target_pairs={{0,1},{1,0},{2,3},{3,2},{4,5},{5,4},{6,7},{7,6},{8,9},{9,8},{10,11... | collective-permute-start | bytes 393224 | tf_op jit(solution)/shard_map/ppermute | solution.py:28
  79.4 1.8 %collective-permute-start.8 = (bf16[128,512]{1,0:T(8,128)(2,1)S(1)}, bf16[128,512]{1,0:T(8,128)(2,1)S(1)}, u32[]{:S(2)}, u32[]{:S(2)}) collective-permute-start(bf16[128,512]{1,0:T(8,128)(2,1)S(1)} %get-tuple-element.49), channel_id=1, source_target_pairs={{0,1},{1,0},{2,3},{3,2},{4,5},{5,4},{6,7},{7,6},{8,9},{9,8},{10,11... | collective-permute-start | bytes 393224 | tf_op jit(solution)/shard_map/ppermute | solution.py:28
  79.6 2.3 %collective-permute-start.11 = (bf16[128,512]{1,0:T(8,128)(2,1)S(1)}, bf16[128,512]{1,0:T(8,128)(2,1)S(1)}, u32[]{:S(2)}, u32[]{:S(2)}) collective-permute-start(bf16[128,512]{1,0:T(8,128)(2,1)S(1)} %get-tuple-element.65), channel_id=1, source_target_pairs={{0,1},{1,0},{2,3},{3,2},{4,5},{5,4},{6,7},{7,6},{8,9},{9,8},{10,11... | collective-permute-start | bytes 393224 | tf_op jit(solution)/shard_map/ppermute | solution.py:28

commit v5 on v4

--- a/solution.py
+++ b/solution.py
@@ -10,6 +10,7 @@
 
 HEAD = 128
 NEG = -1e30
+LOG2E = 1.0 / math.log(2.0)
 ROOM = pltpu.CompilerParams(vmem_limit_bytes=20 << 20)
 
 
@@ -137,16 +138,16 @@
     for head in range(width // HEAD):
         at = slice(head * HEAD, (head + 1) * HEAD)
         keys = jnp.concatenate([first_k[:, at], key[:, at], second_k[:, at]], 0)
-        scores = scores_of(bias, keys, query[:, at], scale)
+        scores = scores_of(bias, keys, query[:, at], scale * LOG2E)
         top = jnp.max(scores, axis=0, keepdims=True)
-        raised = jnp.exp(scores - top)
+        raised = jnp.exp2(scores - top)
         total = jnp.sum(raised, axis=0, keepdims=True)
         probs = (raised * (1.0 / total)).astype(jnp.bfloat16)
         terms = jnp.dot(probs, grad[:, at], preferred_element_type=jnp.float32)
         first[:, at] = terms[:two].astype(jnp.bfloat16)
         own[:, at] = terms[two : 2 * two]
         second[:, at] = terms[2 * two :].astype(jnp.bfloat16)
-        lse[head] = jnp.broadcast_to(top + jnp.log(total), lse.shape[1:])
+        lse[head] = jnp.broadcast_to(top + jnp.log(total) * LOG2E, lse.shape[1:])
 
 
 def score_kernel(
@@ -158,8 +159,8 @@
         at = slice(head * HEAD, (head + 1) * HEAD)
         keys = jnp.concatenate([first_k[:, at], key[:, at], second_k[:, at]], 0)
         values = jnp.concatenate([first_v[:, at], value[:, at], second_v[:, at]], 0)
-        scores = scores_of(bias, keys, query[:, at], scale)
-        probs = jnp.exp(scores - lse[head, 0:1])
+        scores = scores_of(bias, keys, query[:, at], scale * LOG2E)
+        probs = jnp.exp2(scores - lse[head, 0:1])
         grad_probs = lax.dot_general(values, grad[:, at], LAST, preferred_element_type=jnp.float32)
         rounded = probs.astype(jnp.bfloat16).astype(jnp.float32)
         delta = jnp.sum(rounded * grad_probs, axis=0, keepdims=True)
@@ -272,16 +273,10 @@
 
 def weight_kernel(inputs, *refs):
     gathered, out = refs[:-1], refs[-1]
-    rows = gathered[0].shape[0]
+    grads = jnp.concatenate([part[...] for part in gathered], 0)
     tile = 256
     for low in range(0, out.shape[0], tile):
-        total = jnp.zeros((tile, out.shape[1]), jnp.float32)
-        for step, grads in enumerate(gathered):
-            total += jnp.dot(
-                inputs[low : low + tile, step * rows : (step + 1) * rows],
-                grads[...],
-                preferred_element_type=jnp.float32,
-            )
+        total = jnp.dot(inputs[low : low + tile], grads, preferred_element_type=jnp.float32)
         out[low : low + tile] = total.astype(jnp.bfloat16)
 
 

time: 97 us -> 96.9 us (level)
  no operation moved by 1% of the time
where the time goes in v5:
time: 96.9 us; the launch traced here: 96.7 us
  waiting for transfers between devices  44.4 us (46%)
  starting transfers between devices  40.1 us (41%)
  Pallas kernels  8.1 us (8%)
  other arithmetic  3.28 us (3%)
    ppermute x8, starting transfers between devices, swap(): return lax.ppermute(array, AXES, pairs)  22.9 us
    ppermute x8, waiting for transfers between devices, swap(): return lax.ppermute(array, AXES, pairs)  15.5 us
    ppermute x6, waiting for transfers between devices, along_y(): return lax.ppermute(array, AXES, pairs)  14.4 us
    all_to_all x1, waiting for transfers between devices, steps(): arrived = lax.all_to_all(pieces, ('x', 'z', 'c'), 0, 0, tiled=True)  13.4 us
    all_to_all x1, starting transfers between devices, steps(): arrived = lax.all_to_all(pieces, ('x', 'z', 'c'), 0, 0, tiled=True)  8.08 us
    ppermute x6, starting transfers between devices, to_core(): lax.ppermute(array, AXES, [(device, device ^ 1) for device in range(count)])  6.01 us
    ppermute x6, starting transfers between devices, along_y(): return lax.ppermute(array, AXES, pairs)  3.18 us
    pallas_call x1, Pallas kernels, score_pass(): pl.pallas_call(lambda *refs: score_kernel(scale, *refs), out_shape=(part,...  3.06 us
  transfers between devices with their start and end apart: 21, of which 9 were waited for; matrix products, arithmetic and copies ran while one was open for 3% of the time, Pallas kernels for 5%

profile of v5, /device:TPU:1, one launch (start us, length us, event | category | flops | bytes accessed | tf_op | source)
XLA Modules:
  0.0 96.7 jit_solution(4880082644957149173)
XLA Ops:
  0.6 1.4 %pack.1 = (bf16[1,128,512]{2,1,0:T(8,128)(2,1)S(1)}, bf16[1,128,512]{2,1,0:T(8,128)(2,1)S(1)}, bf16[3,128,512]{2,1,0:T(8,128)(2,1)S(1)}, bf16[3,128,512]{2,1,0:T(8,128)(2,1)S(1)}, f32[8,256]{1,0:T(8,128)S(1)}) custom-call(bf16[128,1024]{1,0:T(8,128)(2,1)} %key.1, bf16[128,1024]{1,0:T(8,128)(2,1)} %query, bf16[128,1024]{1,0:T(8,128)(2,1)} %grad.1, ...), custom_call_target="tpu_custom_call" | custom-call | tf_op jit(solution)/shard_map/pack/pallas_call | solution.py:77
  2.0 3.3 %collective-permute-start.1 = (bf16[1,128,512]{2,1,0:T(8,128)(2,1)S(1)}, bf16[1,128,512]{2,1,0:T(8,128)(2,1)S(1)}, u32[]{:S(2)}, u32[]{:S(2)}) collective-permute-start(bf16[1,128,512]{2,1,0:T(8,128)(2,1)S(1)} %get-tuple-element.41), channel_id=1, source_target_pairs={{0,1},{1,0},{2,3},{3,2},{4,5},{5,4},{6,7},{7,6},{8,9},{9,8},{10,11... | collective-permute-start | bytes 393224 | tf_op jit(solution)/shard_map/ppermute | solution.py:29
  5.3 0.1 collective-permute-start
  5.4 0.9 collective-permute-done.1.part
  6.3 0.1 collective-permute-start.2
  6.4 9.2 %collective-permute-start.3 = (bf16[256,512]{1,0:T(8,128)(2,1)S(1)}, bf16[256,512]{1,0:T(8,128)(2,1)S(1)}, u32[]{:S(2)}, u32[]{:S(2)}) collective-permute-start(bf16[256,512]{1,0:T(8,128)(2,1)S(1)} %join.3.refs_4_), channel_id=1, source_target_pairs={{0,254},{1,255},{2,4},{3,5},{4,2},{5,3},{6,8},{7,9},{8,6},{9,7},{1... | collective-permute-start | bytes 786440 | tf_op jit(solution)/shard_map/ppermute | solution.py:39
  15.6 0.0 collective-permute-done.part
  15.6 0.1 join.2
  15.7 0.0 collective-permute-done.2.refs_3_
  15.7 6.0 %collective-permute-done.3.refs_5_ = bf16[256,512]{1,0:T(8,128)(2,1)S(1)} collective-permute-done((bf16[256,512]{1,0:T(8,128)(2,1)S(1)}, bf16[256,512]{1,0:T(8,128)(2,1)S(1)}, u32[]{:S(2)}, u32[]{:S(2)}) %collective-permute-start.3) | collective-permute-done | bytes 262176 | tf_op jit(solution)/shard_map/ppermute | solution.py:39
  21.7 0.0 copy-start
  21.7 1.6 %value_pass.1 = (bf16[256,512]{1,0:T(8,128)(2,1)S(1)}, f32[256,512]{1,0:T(8,128)S(1)}, bf16[256,512]{1,0:T(8,128)(2,1)S(1)}, f32[4,8,256]{2,1,0:T(8,128)S(1)}) custom-call(f32[8,256]{1,0:T(8,128)S(1)} %get-tuple-element.35.refs_0_, bf16[256,512]{1,0:T(8,128)(2,1)S(1)} %get-tuple-element.45.refs_1_, bf16[256,512]{1,0:T(8,128)(2,1)S(1)} %get-tuple-element.39.refs_2_, ...), custom_call_target="tpu_custom_call" | custom-call | flops 402653184 | bytes 4194304 | tf_op jit(solution)/shard_map/value_pass/pallas_call | solution.py:184
  23.3 0.1 collective-permute-start.4
  23.4 6.7 %collective-permute-start.5 = (bf16[256,512]{1,0:T(8,128)(2,1)S(1)}, bf16[256,512]{1,0:T(8,128)(2,1)S(1)}, u32[]{:S(2)}, u32[]{:S(2)}) collective-permute-start(bf16[256,512]{1,0:T(8,128)(2,1)S(1)} %get-tuple-element.44), channel_id=1, source_target_pairs={{0,254},{1,255},{2,4},{3,5},{4,2},{5,3},{6,8},{7,9},{8,6},{9,7},{1... | collective-permute-start | bytes 786440 | tf_op jit(solution)/shard_map/ppermute | solution.py:39
  30.1 0.0 collective-permute-start.6
  30.1 1.4 %collective-permute-start.7 = (bf16[256,512]{1,0:T(8,128)(2,1)S(1)}, bf16[256,512]{1,0:T(8,128)(2,1)S(1)}, u32[]{:S(2)}, u32[]{:S(2)}) collective-permute-start(bf16[256,512]{1,0:T(8,128)(2,1)S(1)} %get-tuple-element.46.refs_7_), channel_id=1, source_target_pairs={{0,254},{1,255},{2,4},{3,5},{4,2},{5,3},{6,8},{7,9},{8,6},{9,7},{1... | collective-permute-start | bytes 786440 | tf_op jit(solution)/shard_map/ppermute | solution.py:39
  31.5 0.0 copy-done
  31.5 0.1 collective-permute-start.13
  31.6 0.0 collective-permute-done.4
  31.6 0.4 collective-permute-start.14
  32.1 3.5 %collective-permute-done.5 = bf16[256,512]{1,0:T(8,128)(2,1)S(1)} collective-permute-done((bf16[256,512]{1,0:T(8,128)(2,1)S(1)}, bf16[256,512]{1,0:T(8,128)(2,1)S(1)}, u32[]{:S(2)}, u32[]{:S(2)}) %collective-permute-start.5) | collective-permute-done | bytes 262176 | tf_op jit(solution)/shard_map/ppermute | solution.py:39
  35.6 0.0 collective-permute-start.15
  35.6 0.1 add_convert_fusion.1.refs_0_
  35.7 0.5 collective-permute-done.6.refs_6_
  36.2 5.4 %collective-permute-done.7.refs_8_ = bf16[256,512]{1,0:T(8,128)(2,1)S(1)} collective-permute-done((bf16[256,512]{1,0:T(8,128)(2,1)S(1)}, bf16[256,512]{1,0:T(8,128)(2,1)S(1)}, u32[]{:S(2)}, u32[]{:S(2)}) %collective-permute-start.7) | collective-permute-done | bytes 262176 | tf_op jit(solution)/shard_map/ppermute | solution.py:39
  41.7 3.1 %score_pass.1 = (bf16[128,512]{1,0:T(8,128)(2,1)S(1)}, bf16[128,512]{1,0:T(8,128)(2,1)S(1)}, bf16[256,512]{1,0:T(8,128)(2,1)S(1)}, f32[256,512]{1,0:T(8,128)S(1)}, bf16[256,512]{1,0:T(8,128)(2,1)S(1)}) custom-call(f32[8,256]{1,0:T(8,128)S(1)} %get-tuple-element.35.refs_0_, bf16[256,512]{1,0:T(8,128)(2,1)S(1)} %get-tuple-element.45.refs_1_, ...), custom_call_target="tpu_custom_call" | custom-call | flops 805306368 | bytes 6291456 | tf_op jit(solution)/shard_map/score_pass/pallas_call | solution.py:204
  44.7 2.8 %collective-permute-done.13.refs_1_ = bf16[128,512]{1,0:T(8,128)(2,1)S(1)} collective-permute-done((bf16[128,512]{1,0:T(8,128)(2,1)S(1)}, bf16[128,512]{1,0:T(8,128)(2,1)S(1)}, u32[]{:S(2)}, u32[]{:S(2)}) %collective-permute-start.13) | collective-permute-done | bytes 131104 | tf_op jit(solution)/shard_map/ppermute | solution.py:46
  47.5 0.0 collective-permute-done.14.refs_2_
  47.5 0.0 collective-permute-done.15.refs_3_
  47.6 1.5 %collective-permute-start.16 = (bf16[4,128,512]{2,1,0:T(8,128)(2,1)S(1)}, bf16[4,128,512]{2,1,0:T(8,128)(2,1)S(1)}, u32[]{:S(2)}, u32[]{:S(2)}) collective-permute-start(bf16[4,128,512]{2,1,0:T(8,128)(2,1)S(1)} %stack.1.own), channel_id=1, source_target_pairs={{0,1},{1,0},{2,3},{3,2},{4,5},{5,4},{6,7},{7,6},{8,9},{9,8},{10,11... | collective-permute-start | bytes 1572872 | tf_op jit(solution)/shard_map/ppermute | solution.py:29
  49.0 0.0 collective-permute-start.17
  49.0 0.5 collective-permute-start.18
  49.5 2.2 %collective-permute-start.19 = (bf16[256,512]{1,0:T(8,128)(2,1)S(1)}, bf16[256,512]{1,0:T(8,128)(2,1)S(1)}, u32[]{:S(2)}, u32[]{:S(2)}) collective-permute-start(bf16[256,512]{1,0:T(8,128)(2,1)S(1)} %add_convert_fusion.1.refs_0_), channel_id=1, source_target_pairs={{0,192},{1,193},{2,194},{3,195},{4,196},{5,197},{6,198},{7,199},{8... | collective-permute-start | bytes 786440 | tf_op jit(solution)/shard_map/ppermute | solution.py:46
  51.7 5.4 %collective-permute-start.10 = (bf16[256,512]{1,0:T(8,128)(2,1)S(1)}, bf16[256,512]{1,0:T(8,128)(2,1)S(1)}, u32[]{:S(2)}, u32[]{:S(2)}) collective-permute-start(bf16[256,512]{1,0:T(8,128)(2,1)S(1)} %get-tuple-element.52), channel_id=1, source_target_pairs={{0,254},{1,255},{2,4},{3,5},{4,2},{5,3},{6,8},{7,9},{8,6},{9,7},{1... | collective-permute-start | bytes 786440 | tf_op jit(solution)/shard_map/ppermute | solution.py:39
  57.1 0.0 collective-permute-done.16.part
  57.1 0.0 collective-permute-start.9
  57.1 0.4 merge.1.inputs
  57.5 11.6 %collective-permute-done.17.refs_1_ = bf16[256,512]{1,0:T(8,128)(2,1)S(1)} collective-permute-done((bf16[256,512]{1,0:T(8,128)(2,1)S(1)}, bf16[256,512]{1,0:T(8,128)(2,1)S(1)}, u32[]{:S(2)}, u32[]{:S(2)}) %collective-permute-start.17) | collective-permute-done | bytes 262176 | tf_op jit(solution)/shard_map/ppermute | solution.py:46
  69.1 0.0 collective-permute-done.18.refs_2_
  69.1 0.0 collective-permute-done.19.refs_3_
  69.1 1.5 %weight_pass.1 = bf16[512,512]{1,0:T(8,128)(2,1)} custom-call(bf16[512,1024]{1,0:T(8,128)(2,1)S(1)} %merge.1.inputs, bf16[256,512]{1,0:T(8,128)(2,1)S(1)} %add_convert_fusion.1.refs_0_, bf16[256,512]{1,0:T(8,128)(2,1)S(1)} %collective-permute-done.17.refs_1_, bf16[256,512]{1,0:T(8,128)(2,1)S(1)} %collective-permute-done.18.refs_2_, ...), custom_call_target="tpu_custom_call" | custom-call | flops 536870912 | bytes 4194304 | tf_op jit(solution)/shard_map/weight_pass/pallas_call | solution.py:286
  70.6 8.1 %all-to-all-start = ((bf16[64,8,512]{2,1,0:T(8,128)(2,1)}), bf16[64,8,512]{2,1,0:T(8,128)(2,1)S(1)}, u32[]{:S(2)}, u32[]{:S(2)}) async-start(bf16[64,8,512]{2,1,0:T(8,128)(2,1)} %bitcast), calls=%async_computation | async-start | bytes 1048576 | tf_op jit(solution)/shard_map/all_to_all | solution.py:356
  78.7 0.5 collective-permute-start.12
  79.3 0.1 collective-permute-start.8
  79.4 0.0 collective-permute-done.10
  79.4 0.0 collective-permute-done.9
  79.4 0.1 add_convert_fusion
  79.5 0.5 collective-permute-start.11
  80.0 0.2 collective-permute-done.12
  80.3 0.8 maximum_select_fusion.2
  81.0 0.0 collective-permute-done.8
  81.1 0.8 maximum_select_fusion
  81.8 0.0 collective-permute-done.11
  81.8 0.8 maximum_select_fusion.1
  82.6 13.4 %all-to-all-done = bf16[64,8,512]{2,1,0:T(8,128)(2,1)S(1)} async-done(((bf16[64,8,512]{2,1,0:T(8,128)(2,1)}), bf16[64,8,512]{2,1,0:T(8,128)(2,1)S(1)}, u32[]{:S(2)}, u32[]{:S(2)}) %all-to-all-start) | async-done | bytes 524320 | tf_op jit(solution)/shard_map/all_to_all | solution.py:356
  96.0 0.1 convert_reduce_fusion
  96.1 0.6 broadcast_multiply_fusion
  (5 shorter events, 0.1 us)
Async XLA Ops:
  2.0 4.3 %collective-permute-start.1 = (bf16[1,128,512]{2,1,0:T(8,128)(2,1)S(1)}, bf16[1,128,512]{2,1,0:T(8,128)(2,1)S(1)}, u32[]{:S(2)}, u32[]{:S(2)}) collective-permute-start(bf16[1,128,512]{2,1,0:T(8,128)(2,1)S(1)} %get-tuple-element.41), channel_id=1, source_target_pairs={{0,1},{1,0},{2,3},{3,2},{4,5},{5,4},{6,7},{7,6},{8,9},{9,8},{10,11... | collective-permute-start | bytes 393224 | tf_op jit(solution)/shard_map/ppermute | solution.py:29
  5.3 10.3 %collective-permute-start = (bf16[3,128,512]{2,1,0:T(8,128)(2,1)S(1)}, bf16[3,128,512]{2,1,0:T(8,128)(2,1)S(1)}, u32[]{:S(2)}, u32[]{:S(2)}) collective-permute-start(bf16[3,128,512]{2,1,0:T(8,128)(2,1)S(1)} %get-tuple-element.37), channel_id=1, source_target_pairs={{0,1},{1,0},{2,3},{3,2},{4,5},{5,4},{6,7},{7,6},{8,9},{9,8},{10,11... | collective-permute-start | bytes 1179656 | tf_op jit(solution)/shard_map/ppermute | solution.py:29
  6.3 9.4 %collective-permute-start.2 = (bf16[256,512]{1,0:T(8,128)(2,1)S(1)}, bf16[256,512]{1,0:T(8,128)(2,1)S(1)}, u32[]{:S(2)}, u32[]{:S(2)}) collective-permute-start(bf16[256,512]{1,0:T(8,128)(2,1)S(1)} %join.3.refs_4_), channel_id=1, source_target_pairs={{0,2},{1,3},{2,0},{3,1},{4,6},{5,7},{6,4},{7,5},{8,10},{9,11},{10,... | collective-permute-start | bytes 786440 | tf_op jit(solution)/shard_map/ppermute | solution.py:39
  6.4 15.3 %collective-permute-start.3 = (bf16[256,512]{1,0:T(8,128)(2,1)S(1)}, bf16[256,512]{1,0:T(8,128)(2,1)S(1)}, u32[]{:S(2)}, u32[]{:S(2)}) collective-permute-start(bf16[256,512]{1,0:T(8,128)(2,1)S(1)} %join.3.refs_4_), channel_id=1, source_target_pairs={{0,254},{1,255},{2,4},{3,5},{4,2},{5,3},{6,8},{7,9},{8,6},{9,7},{1... | collective-permute-start | bytes 786440 | tf_op jit(solution)/shard_map/ppermute | solution.py:39
  21.7 9.8 %copy-start = (bf16[128,2048]{1,0:T(8,128)(2,1)S(1)}, bf16[128,2048]{1,0:T(8,128)(2,1)}, u32[]{:S(2)}) copy-start(bf16[128,2048]{1,0:T(8,128)(2,1)} %refs_0_) | copy-start | bytes 1572868
  23.3 8.3 %collective-permute-start.4 = (bf16[256,512]{1,0:T(8,128)(2,1)S(1)}, bf16[256,512]{1,0:T(8,128)(2,1)S(1)}, u32[]{:S(2)}, u32[]{:S(2)}) collective-permute-start(bf16[256,512]{1,0:T(8,128)(2,1)S(1)} %get-tuple-element.43), channel_id=1, source_target_pairs={{0,2},{1,3},{2,0},{3,1},{4,6},{5,7},{6,4},{7,5},{8,10},{9,11},{10,... | collective-permute-start | bytes 786440 | tf_op jit(solution)/shard_map/ppermute | solution.py:39
  23.4 12.2 %collective-permute-start.5 = (bf16[256,512]{1,0:T(8,128)(2,1)S(1)}, bf16[256,512]{1,0:T(8,128)(2,1)S(1)}, u32[]{:S(2)}, u32[]{:S(2)}) collective-permute-start(bf16[256,512]{1,0:T(8,128)(2,1)S(1)} %get-tuple-element.44), channel_id=1, source_target_pairs={{0,254},{1,255},{2,4},{3,5},{4,2},{5,3},{6,8},{7,9},{8,6},{9,7},{1... | collective-permute-start | bytes 786440 | tf_op jit(solution)/shard_map/ppermute | solution.py:39
  30.1 6.1 %collective-permute-start.6 = (bf16[256,512]{1,0:T(8,128)(2,1)S(1)}, bf16[256,512]{1,0:T(8,128)(2,1)S(1)}, u32[]{:S(2)}, u32[]{:S(2)}) collective-permute-start(bf16[256,512]{1,0:T(8,128)(2,1)S(1)} %get-tuple-element.46.refs_7_), channel_id=1, source_target_pairs={{0,2},{1,3},{2,0},{3,1},{4,6},{5,7},{6,4},{7,5},{8,10},{9,11},{10,... | collective-permute-start | bytes 786440 | tf_op jit(solution)/shard_map/ppermute | solution.py:39
  30.1 11.5 %collective-permute-start.7 = (bf16[256,512]{1,0:T(8,128)(2,1)S(1)}, bf16[256,512]{1,0:T(8,128)(2,1)S(1)}, u32[]{:S(2)}, u32[]{:S(2)}) collective-permute-start(bf16[256,512]{1,0:T(8,128)(2,1)S(1)} %get-tuple-element.46.refs_7_), channel_id=1, source_target_pairs={{0,254},{1,255},{2,4},{3,5},{4,2},{5,3},{6,8},{7,9},{8,6},{9,7},{1... | collective-permute-start | bytes 786440 | tf_op jit(solution)/shard_map/ppermute | solution.py:39
  31.5 16.0 %collective-permute-start.13 = (bf16[128,512]{1,0:T(8,128)(2,1)S(1)}, bf16[128,512]{1,0:T(8,128)(2,1)S(1)}, u32[]{:S(2)}, u32[]{:S(2)}) collective-permute-start(bf16[128,512]{1,0:T(8,128)(2,1)S(1)} %get-tuple-element.55), channel_id=1, source_target_pairs={{0,64},{1,65},{2,66},{3,67},{4,68},{5,69},{6,70},{7,71},{8,72},{9,... | collective-permute-start | bytes 393224 | tf_op jit(solution)/shard_map/ppermute | solution.py:46
  31.6 15.9 %collective-permute-start.14 = (bf16[128,512]{1,0:T(8,128)(2,1)S(1)}, bf16[128,512]{1,0:T(8,128)(2,1)S(1)}, u32[]{:S(2)}, u32[]{:S(2)}) collective-permute-start(bf16[128,512]{1,0:T(8,128)(2,1)S(1)} %get-tuple-element.56), channel_id=1, source_target_pairs={{0,128},{1,129},{2,130},{3,131},{4,132},{5,133},{6,134},{7,135},{8... | collective-permute-start | bytes 393224 | tf_op jit(solution)/shard_map/ppermute | solution.py:46
  35.6 11.9 %collective-permute-start.15 = (bf16[128,512]{1,0:T(8,128)(2,1)S(1)}, bf16[128,512]{1,0:T(8,128)(2,1)S(1)}, u32[]{:S(2)}, u32[]{:S(2)}) collective-permute-start(bf16[128,512]{1,0:T(8,128)(2,1)S(1)} %get-tuple-element.57), channel_id=1, source_target_pairs={{0,192},{1,193},{2,194},{3,195},{4,196},{5,197},{6,198},{7,199},{8... | collective-permute-start | bytes 393224 | tf_op jit(solution)/shard_map/ppermute | solution.py:46
  47.6 9.6 %collective-permute-start.16 = (bf16[4,128,512]{2,1,0:T(8,128)(2,1)S(1)}, bf16[4,128,512]{2,1,0:T(8,128)(2,1)S(1)}, u32[]{:S(2)}, u32[]{:S(2)}) collective-permute-start(bf16[4,128,512]{2,1,0:T(8,128)(2,1)S(1)} %stack.1.own), channel_id=1, source_target_pairs={{0,1},{1,0},{2,3},{3,2},{4,5},{5,4},{6,7},{7,6},{8,9},{9,8},{10,11... | collective-permute-start | bytes 1572872 | tf_op jit(solution)/shard_map/ppermute | solution.py:29
  49.0 20.0 %collective-permute-start.17 = (bf16[256,512]{1,0:T(8,128)(2,1)S(1)}, bf16[256,512]{1,0:T(8,128)(2,1)S(1)}, u32[]{:S(2)}, u32[]{:S(2)}) collective-permute-start(bf16[256,512]{1,0:T(8,128)(2,1)S(1)} %add_convert_fusion.1.refs_0_), channel_id=1, source_target_pairs={{0,64},{1,65},{2,66},{3,67},{4,68},{5,69},{6,70},{7,71},{8,72},{9,... | collective-permute-start | bytes 786440 | tf_op jit(solution)/shard_map/ppermute | solution.py:46
  49.0 20.0 %collective-permute-start.18 = (bf16[256,512]{1,0:T(8,128)(2,1)S(1)}, bf16[256,512]{1,0:T(8,128)(2,1)S(1)}, u32[]{:S(2)}, u32[]{:S(2)}) collective-permute-start(bf16[256,512]{1,0:T(8,128)(2,1)S(1)} %add_convert_fusion.1.refs_0_), channel_id=1, source_target_pairs={{0,128},{1,129},{2,130},{3,131},{4,132},{5,133},{6,134},{7,135},{8... | collective-permute-start | bytes 786440 | tf_op jit(solution)/shard_map/ppermute | solution.py:46
  49.5 19.6 %collective-permute-start.19 = (bf16[256,512]{1,0:T(8,128)(2,1)S(1)}, bf16[256,512]{1,0:T(8,128)(2,1)S(1)}, u32[]{:S(2)}, u32[]{:S(2)}) collective-permute-start(bf16[256,512]{1,0:T(8,128)(2,1)S(1)} %add_convert_fusion.1.refs_0_), channel_id=1, source_target_pairs={{0,192},{1,193},{2,194},{3,195},{4,196},{5,197},{6,198},{7,199},{8... | collective-permute-start | bytes 786440 | tf_op jit(solution)/shard_map/ppermute | solution.py:46
  51.7 27.7 %collective-permute-start.10 = (bf16[256,512]{1,0:T(8,128)(2,1)S(1)}, bf16[256,512]{1,0:T(8,128)(2,1)S(1)}, u32[]{:S(2)}, u32[]{:S(2)}) collective-permute-start(bf16[256,512]{1,0:T(8,128)(2,1)S(1)} %get-tuple-element.52), channel_id=1, source_target_pairs={{0,254},{1,255},{2,4},{3,5},{4,2},{5,3},{6,8},{7,9},{8,6},{9,7},{1... | collective-permute-start | bytes 786440 | tf_op jit(solution)/shard_map/ppermute | solution.py:39
  57.1 22.3 %collective-permute-start.9 = (bf16[256,512]{1,0:T(8,128)(2,1)S(1)}, bf16[256,512]{1,0:T(8,128)(2,1)S(1)}, u32[]{:S(2)}, u32[]{:S(2)}) collective-permute-start(bf16[256,512]{1,0:T(8,128)(2,1)S(1)} %get-tuple-element.51), channel_id=1, source_target_pairs={{0,2},{1,3},{2,0},{3,1},{4,6},{5,7},{6,4},{7,5},{8,10},{9,11},{10,... | collective-permute-start | bytes 786440 | tf_op jit(solution)/shard_map/ppermute | solution.py:39
  70.6 25.4 %all-to-all-start = ((bf16[64,8,512]{2,1,0:T(8,128)(2,1)}), bf16[64,8,512]{2,1,0:T(8,128)(2,1)S(1)}, u32[]{:S(2)}, u32[]{:S(2)}) async-start(bf16[64,8,512]{2,1,0:T(8,128)(2,1)} %bitcast), calls=%async_computation | async-start | bytes 1048576 | tf_op jit(solution)/shard_map/all_to_all | solution.py:356
  78.7 1.5 %collective-permute-start.12 = (bf16[128,512]{1,0:T(8,128)(2,1)S(1)}, bf16[128,512]{1,0:T(8,128)(2,1)S(1)}, u32[]{:S(2)}, u32[]{:S(2)}) collective-permute-start(bf16[128,512]{1,0:T(8,128)(2,1)S(1)} %get-tuple-element.63), channel_id=1, source_target_pairs={{0,1},{1,0},{2,3},{3,2},{4,5},{5,4},{6,7},{7,6},{8,9},{9,8},{10,11... | collective-permute-start | bytes 393224 | tf_op jit(solution)/shard_map/ppermute | solution.py:29
  79.3 1.8 %collective-permute-start.8 = (bf16[128,512]{1,0:T(8,128)(2,1)S(1)}, bf16[128,512]{1,0:T(8,128)(2,1)S(1)}, u32[]{:S(2)}, u32[]{:S(2)}) collective-permute-start(bf16[128,512]{1,0:T(8,128)(2,1)S(1)} %get-tuple-element.49), channel_id=1, source_target_pairs={{0,1},{1,0},{2,3},{3,2},{4,5},{5,4},{6,7},{7,6},{8,9},{9,8},{10,11... | collective-permute-start | bytes 393224 | tf_op jit(solution)/shard_map/ppermute | solution.py:29
  79.5 2.3 %collective-permute-start.11 = (bf16[128,512]{1,0:T(8,128)(2,1)S(1)}, bf16[128,512]{1,0:T(8,128)(2,1)S(1)}, u32[]{:S(2)}, u32[]{:S(2)}) collective-permute-start(bf16[128,512]{1,0:T(8,128)(2,1)S(1)} %get-tuple-element.65), channel_id=1, source_target_pairs={{0,1},{1,0},{2,3},{3,2},{4,5},{5,4},{6,7},{7,6},{8,9},{9,8},{10,11... | collective-permute-start | bytes 393224 | tf_op jit(solution)/shard_map/ppermute | solution.py:29
